TPU v7x, 32 devices: a whole 2x2x4 slice. The times are simulated.
32 devices in a mesh: tm: 4 (over y, core), space: 8 (over z, x).
Axes of the slice: x: 2, y: 2, z: 4, core: 2. Of those that a mesh axis runs over, the one named last changes fastest.
Arguments:
- initial: float32 [4, 128, 8192], P('tm', None, 'space'), may hold values from -324 to 324
- rhs: float32 [4, 128, 8192], P('tm', None, 'space'), may hold values from -324 to 324
- coef: float32 [8192], P('space'), may hold values from 0.5 to 4
- stiffness: float32 [128, 128], replicated, may hold values from -0.5 to 0.5
- block_inverse: float32 [128, 128], replicated, may hold values from -0.5 to 0.5
- face_proj: float32 [192, 128], replicated, may hold values from -0.5 to 0.5
- lift: float32 [128, 192], replicated, may hold values from -0.4375 to 0.4375
- time_lift: float32 [128, 64], replicated, may hold values from -0.75 to 0.75
- neighbour: int32 [6, 8192], P(None, 'space'), may hold values from 0 to 6399, as said below
- boundary: int32 [6, 8192], P(None, 'space'), may hold values from 0 to 1, as said below
- send_list: int32 [2048], P('space'), may hold values from 0 to 2047, as said below
Outputs:
- smoothed: float32 [4, 128, 8192], P('tm', None, 'space')
- indicator: float32 [4, 8192], P('tm', 'space')
- estimate: float32 [1], replicated
Inputs may be any that keep to these rules, and one draw needn't show every extreme that they name: `neighbour`: the elements form a structured hexahedral grid numbered in a random order inside each partition; partition p holds 8 element layers and meets partitions p - 1 and p + 1 across 128 faces each, listed in the same order on both sides. Interior faces point to the opposite face of the neighbouring element; faces toward another partition point to columns 6144 and above; boundary faces may point anywhere. `boundary`: marks the outer faces of the whole grid. `send_list`: the first 128 entries of a partition list its faces facing the lower partition, the next 128 those facing the upper one, as columns of its own pool below 2048.
All inputs are finite; a program needn't handle non-finite values.
Results may differ from a plain program's by a relative error of at most 0.000059.
Values sent between devices are 32-bit elements; how exact they have to be, the bound alone decides.
No kernel may reach another device: no remote copies, remote signals or barrier semaphores. Data moves between devices by JAX's collectives and lax.ppermute only.
A program may use at most 64 MiB of HBM per device.

v0:
```python
import jax
import jax.numpy as jnp
from jax import lax
from jax.sharding import PartitionSpec as P


def padded(x, sides, width):
    for axis, dim in sides:
        devices, length = (lax.axis_size(axis), x.shape[dim])
        up = [(i, (i + 1) % devices) for i in range(devices - 1)]
        down = [(j, i) for i, j in up]
        last = lax.slice_in_dim(x, length - width, length, axis=dim)
        initial = lax.slice_in_dim(x, 0, width, axis=dim)
        before = lax.ppermute(last, axis, up)
        after = lax.ppermute(initial, axis, down)
        x = jnp.concatenate([before, x, after], axis=dim)
    return x


def shifted(value, axis, steps):
    count = lax.axis_size(axis)
    initial, last = (max(0, -steps), min(count, count - steps))
    return lax.ppermute(value, axis, [(source, source + steps) for source in range(initial, last)])


def on_device(
    initial,
    rhs,
    coef,
    stiffness,
    block_inverse,
    face_proj,
    lift,
    time_lift,
    neighbour,
    boundary,
    send_list,
):
    start_field = initial[0]
    source = rhs[0]
    elements = start_field.shape[1]
    half_dofs = start_field.shape[0] // 2
    face_dofs = face_proj.shape[0] // 6
    border = send_list.shape[0] // 2
    column_ids = neighbour.reshape(6 * elements)
    open_faces = jnp.tile(1.0 - boundary.astype(jnp.float32), (face_dofs, 1))

    def operate(vector):
        traces = jnp.dot(face_proj, vector, precision=lax.Precision.HIGHEST)
        trace_pool = traces.reshape(face_dofs, 6 * elements)
        outbound = jnp.take(trace_pool, send_list, axis=1)
        received = padded(outbound, (("space", 1),), border)
        from_lower = received[:, :border]
        from_upper = received[:, 3 * border :]
        prev_end = shifted(vector[half_dofs:], "tm", 1)
        ext_pool = jnp.concatenate([trace_pool, from_lower, from_upper], axis=1)
        outside = jnp.take(ext_pool, column_ids, axis=1).reshape(face_dofs * 6, elements)
        face_jump = traces - outside * open_faces
        time_jump = vector[:half_dofs] - prev_end
        applied = coef * jnp.dot(stiffness, vector, precision=lax.Precision.HIGHEST)
        applied = applied + jnp.dot(lift, face_jump, precision=lax.Precision.HIGHEST)
        applied = applied + jnp.dot(time_lift, time_jump, precision=lax.Precision.HIGHEST)
        return (applied, face_jump, time_jump)

    applied_base, base_jump, base_time = operate(start_field)
    residual = source - applied_base
    direction = jnp.dot(block_inverse, residual, precision=lax.Precision.HIGHEST) / coef
    image, step_jump, step_time = operate(direction)
    cross_sum = jnp.sum(residual * image)
    image_sum = jnp.sum(image * image)
    total_cross, total_image = lax.psum((cross_sum, image_sum), ("tm", "space"))
    step_size = total_cross / total_image
    smoothed = start_field + step_size * direction
    new_residual = residual - step_size * image
    new_jump = base_jump + step_size * step_jump
    new_time = base_time + step_size * step_time
    element_eta = (
        jnp.sum(new_residual * new_residual, axis=0)
        + 0.5 * jnp.sum(new_jump * new_jump, axis=0)
        + jnp.sum(new_time * new_time, axis=0)
    )
    eta_total = lax.psum(jnp.sum(element_eta), ("tm", "space"))
    element_count = elements * lax.axis_size("tm") * lax.axis_size("space")
    indicator = element_eta * element_count / eta_total
    estimate = jnp.sqrt(eta_total / element_count).reshape(1)
    return (smoothed[None], indicator[None], estimate)


def solution(mesh):
    placed = (
        P("tm", None, "space"),
        P("tm", None, "space"),
        P("space"),
        P(),
        P(),
        P(),
        P(),
        P(),
        P(None, "space"),
        P(None, "space"),
        P("space"),
    )
    return jax.shard_map(
        on_device,
        mesh=mesh,
        in_specs=placed,
        out_specs=(P("tm", None, "space"), P("tm", "space"), P()),
        check_vma=False,
    )
```

profile of v0, /device:TPU:0, one launch (start us, length us, event | category | flops | bytes accessed | tf_op | source)
XLA Modules:
  0.0 214.1 jit_solution(13432390113323997010)
XLA Ops:
  0.6 0.0 copy-start
  0.6 0.7 compare_select_fusion.1
  1.4 0.7 compare_and_fusion.1
  2.1 1.8 fusion.4
  3.9 0.9 copy-done.3
  4.8 1.3 reshape.74
  6.0 2.0 copy.37
  8.0 0.7 gather_fusion
  8.8 0.1 select_bitcast_fusion.3
  8.9 0.8 fusion.11
  9.7 4.9 %collective-permute-start = (f32[32,128]{0,1:T(8,128)}, f32[32,128]{0,1:T(8,128)S(1)}, u32[]{:S(2)}, u32[]{:S(2)}) collective-permute-start(f32[32,128]{0,1:T(8,128)} %get-tuple-element.11), channel_id=1, source_target_pairs={{0,1},{1,2},{2,3},{3,4},{4,5},{5,6},{6,7},{8,9},{9,10},{10,11},{11... | collective-permute-start | bytes 49160 | tf_op jit(solution)/shard_map/ppermute | solution.py:14
  14.5 1.3 collective-permute-start.1
  15.8 1.7 slice_bitcast_fusion
  17.5 2.2 %collective-permute-start.2 = (f32[64,1024]{1,0:T(8,128)}, f32[64,1024]{1,0:T(8,128)}, u32[]{:S(2)}, u32[]{:S(2)}) collective-permute-start(f32[64,1024]{1,0:T(8,128)} %slice_bitcast_fusion), channel_id=1, source_target_pairs={{0,8},{8,16},{16,24},{1,9},{9,17},{17,25},{2,10},{10,18},{18,26},{... | collective-permute-start | bytes 786440 | tf_op jit(solution)/shard_map/ppermute | solution.py:23
  19.7 0.8 convert_subtract_fusion
  20.5 2.4 %convolution_multiply_fusion.1 = f32[128,1024]{1,0:T(8,128)} fusion(f32[128,128]{1,0:T(8,128)S(1)} %copy-done.22, f32[1,128,1024]{2,1,0:T(8,128)} %param.15, f32[1024]{0:T(1024)S(1)} %copy-done.27), kind=kOutput, calls=%fused_computation.18 | convolution fusion | flops 201457664 | bytes 1118208 | tf_op jit(solution)/shard_map/dot_general | solution.py:60
  22.9 1.1 tile.4
  24.0 2.2 %tile.10 = f32[192,1024]{1,0:T(8,128)} reshape(f32[32,6,1024]{2,1,0:T(8,128)} %tile.4) | data formatting | bytes 1572864 | tf_op jit(solution)/shard_map/tile | solution.py:46
  26.3 0.0 collective-permute-done
  26.3 0.0 collective-permute-done.1
  26.3 2.1 pad_maximum_fusion
  28.4 20.9 %gather_fusion.1 = f32[6144,32]{1,0:T(8,128)} fusion(f32[32,6400]{0,1:T(8,128)S(1)} %pad_maximum_fusion, s32[6144]{0:T(1024)S(1)} %fusion.8), kind=kCustom, calls=%fused_computation.1.clone | custom fusion | bytes 1597440 | tf_op jit(solution)/shard_map/jit(_take)/gather | solution.py:57
  49.3 5.8 %select_bitcast_fusion.1 = f32[32,6144]{0,1:T(8,128)} fusion(f32[6144,32]{1,0:T(8,128)} %gather_fusion.1, pred[6144]{0:T(1024)(128)(4,1)S(1)} %compare_and_fusion), kind=kLoop, calls=%fused_computation.7 | loop fusion | flops 196608 | bytes 1579008 | tf_op jit(solution)/shard_map/jit(_take)/select_n | solution.py:57
  55.1 3.2 %copy.38 = f32[32,6144]{1,0:T(8,128)} copy(f32[32,6144]{0,1:T(8,128)} %select_bitcast_fusion.1) | data formatting | bytes 1572864 | tf_op jit(solution)/shard_map/jit(_take)/select_n | solution.py:57
  58.4 1.4 reshape.76
  59.8 0.0 copy-start.21
  59.8 0.0 copy-start.24
  59.8 0.0 copy-start.28
  59.8 1.9 fusion.2
  61.7 1.6 fusion.3
  63.3 0.0 copy-start.15
  63.4 0.8 copy-done.15
  64.1 0.6 convolution_divide_fusion
  64.8 0.8 copy-done.12
  65.6 0.8 convolution_bitcast_fusion
  66.4 0.9 copy-done.8
  67.3 1.3 reshape.77
  68.5 2.0 copy.40
  70.5 0.7 gather_fusion.2
  71.3 0.1 select_bitcast_fusion.2
  71.4 4.4 %collective-permute-start.3 = (f32[32,128]{0,1:T(8,128)S(1)}, f32[32,128]{0,1:T(8,128)S(1)}, u32[]{:S(2)}, u32[]{:S(2)}) collective-permute-start(f32[32,128]{0,1:T(8,128)S(1)} %get-tuple-element.9), channel_id=1, source_target_pairs={{0,1},{1,2},{2,3},{3,4},{4,5},{5,6},{6,7},{8,9},{9,10},{10,11},{11... | collective-permute-start | bytes 49160 | tf_op jit(solution)/shard_map/ppermute | solution.py:14
  75.8 1.3 collective-permute-start.4
  77.1 2.4 %convolution_multiply_fusion = f32[1024,128]{0,1:T(8,128)} fusion(f32[1024,128]{0,1:T(8,128)} %copy-done.12, f32[128,128]{1,0:T(8,128)S(1)} %copy-done.23, f32[1024]{0:T(1024)S(1)} %copy-done.27), kind=kOutput, calls=%fused_computation.14 | convolution fusion | flops 201457664 | bytes 1118208 | tf_op jit(solution)/shard_map/dot_general | solution.py:60
  79.5 1.7 slice.53
  81.2 3.9 %collective-permute-start.5 = (f32[64,1024]{1,0:T(8,128)}, f32[64,1024]{1,0:T(8,128)}, u32[]{:S(2)}, u32[]{:S(2)}) collective-permute-start(f32[64,1024]{1,0:T(8,128)} %slice.53), channel_id=1, source_target_pairs={{0,8},{8,16},{16,24},{1,9},{9,17},{17,25},{2,10},{10,18},{18,26},{... | collective-permute-start | bytes 786440 | tf_op jit(solution)/shard_map/ppermute | solution.py:23
  85.1 0.0 collective-permute-done.4
  85.1 2.1 pad_maximum_fusion.1
  87.2 20.9 %gather_fusion.3 = f32[6144,32]{1,0:T(8,128)} fusion(f32[32,6400]{0,1:T(8,128)S(1)} %pad_maximum_fusion.1, s32[6144]{0:T(1024)S(1)} %fusion.8), kind=kCustom, calls=%fused_computation.3.clone | custom fusion | bytes 1597440 | tf_op jit(solution)/shard_map/jit(_take)/gather | solution.py:57
  108.1 5.8 %select_bitcast_fusion = f32[32,6144]{0,1:T(8,128)} fusion(f32[6144,32]{1,0:T(8,128)} %gather_fusion.3, pred[6144]{0:T(1024)(128)(4,1)S(1)} %compare_and_fusion), kind=kLoop, calls=%fused_computation.6 | loop fusion | flops 196608 | bytes 1579008 | tf_op jit(solution)/shard_map/jit(_take)/select_n | solution.py:57
  113.9 2.5 %copy.41 = f32[32,6144]{1,0:T(8,128)S(1)} copy(f32[32,6144]{0,1:T(8,128)} %select_bitcast_fusion) | data formatting | bytes 1572864 | tf_op jit(solution)/shard_map/jit(_take)/select_n | solution.py:57
  116.4 0.0 copy-start.25
  116.4 1.1 reshape.78
  117.5 2.0 convolution_add_fusion.1
  119.5 0.0 copy-start.11
  119.5 3.1 %multiply_reduce_fusion.2 = (f32[]{:T(128)}, f32[]{:T(128)}, f32[128,1024]{1,0:T(8,128)}) fusion(f32[128,1024]{1,0:T(8,128)S(1)} %copy-done.16, f32[1024,128]{0,1:T(8,128)S(1)} %convolution_add_fusion.1, f32[128,64]{0,1:T(8,128)S(1)} %copy-done.25, f32[64,1024]{1,0:T(8,128)} %collective-permute-done.5, f32[128,1024]{1,0:T(8,128)S(1)} %bitcast.58), kind=kOutput, calls=%fused_computation.29 | convolution fusion | flops 101384192 | bytes 2129928 | tf_op jit(solution)/shard_map/dot_general | solution.py:62
  122.6 42.4 %all-reduce = (f32[]{:T(128)}, f32[]{:T(128)}) all-reduce(f32[]{:T(128)} %get-tuple-element.6, f32[]{:T(128)} %get-tuple-element.5), channel_id=1, replica_groups=mesh['tm'=4,'space'=8] {'tm','space'}, use_global_device_ids=true, to_apply=%region_1.4 | all-reduce | flops 2 | bytes 16 | tf_op jit(solution)/shard_map/psum | solution.py:71
  166.4 0.0 copy-start.17
  166.4 1.9 multiply_reduce_fusion
  168.3 0.1 multiply_reduce_fusion.1
  168.4 1.1 multiply_reduce_fusion.4
  169.5 0.6 fusion.9
  170.1 0.9 fusion.7
  171.0 40.0 %psum.23 = f32[]{:T(128)} all-reduce(f32[]{:T(128)} %fusion.9), channel_id=1, replica_groups=mesh['tm'=4,'space'=8] {'tm','space'}, use_global_device_ids=true, to_apply=%region_8.11 | all-reduce | flops 1 | bytes 8 | tf_op jit(solution)/shard_map/psum | solution.py:82
  211.0 1.2 multiply_divide_fusion
  (54 shorter events, 0.1 us)
Async XLA Ops:
  0.6 1.4 copy-start
  3.9 0.9 copy-start.3
  4.8 14.9 %copy-start.26 = (s32[6,1024]{1,0:T(8,128)S(1)}, s32[6,1024]{1,0:T(8,128)}, u32[]{:S(2)}) copy-start(s32[6,1024]{1,0:T(8,128)} %param.23) | copy-start | bytes 73732
  4.8 15.7 %copy-start.22 = (f32[128,128]{1,0:T(8,128)S(1)}, f32[128,128]{1,0:T(8,128)}, u32[]{:S(2)}) copy-start(f32[128,128]{1,0:T(8,128)} %param.18) | copy-start | bytes 196612
  4.8 15.7 %copy-start.27 = (f32[1024]{0:T(1024)S(1)}, f32[1024]{0:T(1024)}, u32[]{:S(2)}) copy-start(f32[1024]{0:T(1024)} %param.17) | copy-start | bytes 12292
  8.0 18.3 %copy-start.1 = (f32[32,6144]{0,1:T(8,128)}, f32[32,6144]{0,1:T(8,128)S(1)}, u32[]{:S(2)}) copy-start(f32[32,6144]{0,1:T(8,128)S(1)} %copy.37) | copy-start | bytes 2359300
  9.7 16.6 %collective-permute-start = (f32[32,128]{0,1:T(8,128)}, f32[32,128]{0,1:T(8,128)S(1)}, u32[]{:S(2)}, u32[]{:S(2)}) collective-permute-start(f32[32,128]{0,1:T(8,128)} %get-tuple-element.11), channel_id=1, source_target_pairs={{0,1},{1,2},{2,3},{3,4},{4,5},{5,6},{6,7},{8,9},{9,10},{10,11},{11... | collective-permute-start | bytes 49160 | tf_op jit(solution)/shard_map/ppermute | solution.py:14
  14.5 11.7 %collective-permute-start.1 = (f32[32,128]{0,1:T(8,128)}, f32[32,128]{0,1:T(8,128)S(1)}, u32[]{:S(2)}, u32[]{:S(2)}) collective-permute-start(f32[32,128]{0,1:T(8,128)} %get-tuple-element.12), channel_id=1, source_target_pairs={{1,0},{2,1},{3,2},{4,3},{5,4},{6,5},{7,6},{9,8},{10,9},{11,10},{12... | collective-permute-start | bytes 49160 | tf_op jit(solution)/shard_map/ppermute | solution.py:15
  17.5 44.2 %collective-permute-start.2 = (f32[64,1024]{1,0:T(8,128)}, f32[64,1024]{1,0:T(8,128)}, u32[]{:S(2)}, u32[]{:S(2)}) collective-permute-start(f32[64,1024]{1,0:T(8,128)} %slice_bitcast_fusion), channel_id=1, source_target_pairs={{0,8},{8,16},{16,24},{1,9},{9,17},{17,25},{2,10},{10,18},{18,26},{... | collective-permute-start | bytes 786440 | tf_op jit(solution)/shard_map/ppermute | solution.py:23
  55.1 4.6 %copy-start.4 = (f32[192,1024]{1,0:T(8,128)S(1)}, f32[192,1024]{1,0:T(8,128)}, u32[]{:S(2)}) copy-start(f32[192,1024]{1,0:T(8,128)} %copy-done.3) | copy-start | bytes 2359300
  55.1 4.6 %copy-start.6 = (f32[192,1024]{1,0:T(8,128)S(1)}, f32[192,1024]{1,0:T(8,128)}, u32[]{:S(2)}) copy-start(f32[192,1024]{1,0:T(8,128)} %tile.10) | copy-start | bytes 2359300
  55.1 4.6 %copy-start.19 = (f32[128,1024]{1,0:T(8,128)S(1)}, f32[128,1024]{1,0:T(8,128)}, u32[]{:S(2)}) copy-start(f32[128,1024]{1,0:T(8,128)} %convolution_multiply_fusion.1) | copy-start | bytes 1572868
  58.4 3.3 %copy-start.10 = (f32[1,128,1024]{2,1,0:T(8,128)S(1)}, f32[1,128,1024]{2,1,0:T(8,128)}, u32[]{:S(2)}) copy-start(f32[1,128,1024]{2,1,0:T(8,128)} %param.15) | copy-start | bytes 1572868
  59.8 5.0 %copy-start.14 = (f32[192,1024]{1,0:T(8,128)}, f32[192,1024]{1,0:T(8,128)S(1)}, u32[]{:S(2)}) copy-start(f32[192,1024]{1,0:T(8,128)S(1)} %reshape.76) | copy-start | bytes 2359300
  59.8 1.9 copy-start.21
  59.8 1.9 copy-start.24
  59.8 4.3 %copy-start.28 = (f32[128,128]{1,0:T(8,128)S(1)}, f32[128,128]{1,0:T(8,128)}, u32[]{:S(2)}) copy-start(f32[128,128]{1,0:T(8,128)} %param.19) | copy-start | bytes 196612
  63.3 0.8 copy-start.15
  64.8 0.8 copy-start.12
  66.4 0.9 copy-start.8
  67.3 9.8 %copy-start.23 = (f32[128,128]{1,0:T(8,128)S(1)}, f32[128,128]{1,0:T(8,128)}, u32[]{:S(2)}) copy-start(f32[128,128]{1,0:T(8,128)} %param.18) | copy-start | bytes 196612
  70.5 14.6 %copy-start.2 = (f32[32,6144]{0,1:T(8,128)}, f32[32,6144]{0,1:T(8,128)S(1)}, u32[]{:S(2)}) copy-start(f32[32,6144]{0,1:T(8,128)S(1)} %copy.40) | copy-start | bytes 2359300
  71.4 13.7 %collective-permute-start.3 = (f32[32,128]{0,1:T(8,128)S(1)}, f32[32,128]{0,1:T(8,128)S(1)}, u32[]{:S(2)}, u32[]{:S(2)}) collective-permute-start(f32[32,128]{0,1:T(8,128)S(1)} %get-tuple-element.9), channel_id=1, source_target_pairs={{0,1},{1,2},{2,3},{3,4},{4,5},{5,6},{6,7},{8,9},{9,10},{10,11},{11... | collective-permute-start | bytes 49160 | tf_op jit(solution)/shard_map/ppermute | solution.py:14
  75.8 9.3 %collective-permute-start.4 = (f32[32,128]{0,1:T(8,128)S(1)}, f32[32,128]{0,1:T(8,128)S(1)}, u32[]{:S(2)}, u32[]{:S(2)}) collective-permute-start(f32[32,128]{0,1:T(8,128)S(1)} %get-tuple-element.10), channel_id=1, source_target_pairs={{1,0},{2,1},{3,2},{4,3},{5,4},{6,5},{7,6},{9,8},{10,9},{11,10},{12... | collective-permute-start | bytes 49160 | tf_op jit(solution)/shard_map/ppermute | solution.py:15
  81.2 38.3 %collective-permute-start.5 = (f32[64,1024]{1,0:T(8,128)}, f32[64,1024]{1,0:T(8,128)}, u32[]{:S(2)}, u32[]{:S(2)}) collective-permute-start(f32[64,1024]{1,0:T(8,128)} %slice.53), channel_id=1, source_target_pairs={{0,8},{8,16},{16,24},{1,9},{9,17},{17,25},{2,10},{10,18},{18,26},{... | collective-permute-start | bytes 786440 | tf_op jit(solution)/shard_map/ppermute | solution.py:23
  113.9 3.6 %copy-start.7 = (f32[192,1024]{1,0:T(8,128)S(1)}, f32[192,1024]{1,0:T(8,128)}, u32[]{:S(2)}) copy-start(f32[192,1024]{1,0:T(8,128)} %tile.10) | copy-start | bytes 2359300
  113.9 3.6 %copy-start.9 = (f32[192,1024]{1,0:T(8,128)S(1)}, f32[192,1024]{1,0:T(8,128)}, u32[]{:S(2)}) copy-start(f32[192,1024]{1,0:T(8,128)} %copy-done.8) | copy-start | bytes 2359300
  113.9 3.6 %copy-start.18 = (f32[1024,128]{0,1:T(8,128)S(1)}, f32[1024,128]{0,1:T(8,128)}, u32[]{:S(2)}) copy-start(f32[1024,128]{0,1:T(8,128)} %convolution_multiply_fusion) | copy-start | bytes 1572868
  116.4 3.1 %copy-start.13 = (f32[1024,128]{0,1:T(8,128)S(1)}, f32[1024,128]{0,1:T(8,128)}, u32[]{:S(2)}) copy-start(f32[1024,128]{0,1:T(8,128)} %copy-done.12) | copy-start | bytes 1572868
  116.4 3.1 %copy-start.25 = (f32[128,64]{0,1:T(8,128)S(1)}, f32[128,64]{0,1:T(8,128)}, u32[]{:S(2)}) copy-start(f32[128,64]{0,1:T(8,128)} %param.22) | copy-start | bytes 98308
  117.5 2.0 copy-start.16
  117.5 48.9 %copy-start.5 = (f32[192,1024]{1,0:T(8,128)S(1)}, f32[192,1024]{1,0:T(8,128)}, u32[]{:S(2)}) copy-start(f32[192,1024]{1,0:T(8,128)} %copy-done.3) | copy-start | bytes 2359300
  119.5 48.9 %copy-start.11 = (f32[1,128,1024]{2,1,0:T(8,128)S(1)}, f32[1,128,1024]{2,1,0:T(8,128)}, u32[]{:S(2)}) copy-start(f32[1,128,1024]{2,1,0:T(8,128)} %param.15) | copy-start | bytes 1572868
  166.4 1.9 copy-start.17
  166.4 1.9 copy-start.20
where the time goes:
time: 215 us; the launch traced here: 214 us
  blocking collectives  82.4 us (38%)
  local copies, waits for them, and re-layouts  68.9 us (32%)
  other arithmetic  24.1 us (11%)
  starting transfers between devices  17.8 us (8%)
  matrix products  16.6 us (8%)
  between operations  4.26 us (2%)
    psum x1, blocking collectives, on_device(): total_cross, total_image = lax.psum((cross_sum, image_sum), ('tm', 'space'))  42.4 us
    gather x2, local copies, waits for them, and re-layouts, operate(): jnp.take(ext_pool, column_ids, axis=1).reshape(face_dofs * 6, elements)  41.8 us
    psum x1, blocking collectives, on_device(): eta_total = lax.psum(jnp.sum(element_eta), ('tm', 'space'))  40 us
    select_n x2, other arithmetic, operate(): jnp.take(ext_pool, column_ids, axis=1).reshape(face_dofs * 6, elements)  11.7 us
    ppermute x2, starting transfers between devices, padded(): before = lax.ppermute(last, axis, up)  9.23 us
    reshape x4, local copies, waits for them, and re-layouts, operate(): trace_pool = traces.reshape(face_dofs, 6 * elements)  6.43 us
    ppermute x2, starting transfers between devices, shifted(): lax.ppermute(value, axis, [(source, source + steps) for source in range(i...  6.03 us
    select_n x2, local copies, waits for them, and re-layouts, operate(): jnp.take(ext_pool, column_ids, axis=1).reshape(face_dofs * 6, elements)  5.71 us
  transfers between devices with their start and end apart: 6, of which 0 were waited for; matrix products, arithmetic and copies ran while one was open for 38% of the time, Pallas kernels for 0%

commit v1 on v0

v1 whole, which is shorter than its diff:
```python
import functools

import jax
import jax.numpy as jnp
from jax import lax
from jax.experimental import pallas as pl
from jax.experimental.pallas import tpu as pltpu
from jax.sharding import PartitionSpec as P

LANES = 128
SUBS = 8


def dot(a, b):
    return jnp.dot(a, b, precision=lax.Precision.HIGHEST, preferred_element_type=jnp.float32)


def lane_gather(tile_of, tiles, columns, rows):
    shape = (SUBS, LANES)
    low = jnp.broadcast_to(jnp.bitwise_and(columns, LANES - 1), shape)
    high = jnp.broadcast_to(jnp.right_shift(columns, 7), shape)
    found = [jnp.zeros(shape, jnp.float32) for _ in range(rows // SUBS)]
    for tile in range(tiles):
        here = high == tile
        for r in range(rows // SUBS):
            picked = jnp.take_along_axis(tile_of(tile, r), low, axis=1)
            found[r] = jnp.where(here, picked, found[r])
    return found


def face_rows(ref, face, face_dofs):
    return ref[pl.ds(face, face_dofs, stride=6), :]


def fill_outbound(traces, send_ref, odd, first_ref, second_ref, face_dofs, elements):
    per_face = elements // LANES

    def tile_of(tile, r):
        face, col = divmod(tile, per_face)
        return traces[face * face_dofs + r * SUBS : face * face_dofs + (r + 1) * SUBS, col * LANES : (col + 1) * LANES]

    border = send_ref.shape[1]
    for j in range(border // LANES):
        cols = slice(j * LANES, (j + 1) * LANES)
        lower = lane_gather(tile_of, 2 * per_face, send_ref[0:1, cols], face_dofs)
        upper = lane_gather(tile_of, 2 * per_face, send_ref[1:2, cols], face_dofs)
        for r in range(face_dofs // SUBS):
            rows = slice(r * SUBS, (r + 1) * SUBS)
            first_ref[rows, cols] = jnp.where(odd, lower[r], upper[r])
            second_ref[rows, cols] = jnp.where(odd, upper[r], lower[r])


def fill_jump(traces, nb_ref, bd_ref, jump_ref, face_dofs, elements):
    per_face = elements // LANES
    for face in range(6):
        other = face ^ 1

        def tile_of(tile, r, other=other):
            return traces[other * face_dofs + r * SUBS : other * face_dofs + (r + 1) * SUBS, tile * LANES : (tile + 1) * LANES]

        for j in range(per_face):
            cols = slice(j * LANES, (j + 1) * LANES)
            found = lane_gather(tile_of, per_face, nb_ref[face : face + 1, cols] - other * elements, face_dofs)
            open_face = jnp.broadcast_to(1.0 - bd_ref[face : face + 1, cols].astype(jnp.float32), (SUBS, LANES))
            for r in range(face_dofs // SUBS):
                rows = slice(face * face_dofs + r * SUBS, face * face_dofs + (r + 1) * SUBS)
                jump_ref[rows, cols] = traces[rows, cols] - found[r] * open_face


def rim_terms(first_ref, second_ref, nb_ref, bd_ref, odd, rim_ref, face_dofs, elements):
    border = first_ref.shape[1]
    tiles = border // LANES

    for j in range(elements // LANES):
        cols = slice(j * LANES, (j + 1) * LANES)
        for face in range(2):
            columns = nb_ref[face : face + 1, cols] - 6 * elements

            def tile_of(tile, r):
                side, t = divmod(tile, tiles)
                rows, part = slice(r * SUBS, (r + 1) * SUBS), slice(t * LANES, (t + 1) * LANES)
                a, b = first_ref[rows, part], second_ref[rows, part]
                return jnp.where(odd, a, b) if side == 0 else jnp.where(odd, b, a)

            found = lane_gather(tile_of, 2 * tiles, columns, face_dofs)
            open_face = jnp.broadcast_to(1.0 - bd_ref[face : face + 1, cols].astype(jnp.float32), (SUBS, LANES))
            for r in range(face_dofs // SUBS):
                rows = slice(face * face_dofs + r * SUBS, face * face_dofs + (r + 1) * SUBS)
                rim_ref[rows, cols] = 0.0 - found[r] * open_face


def first_send(odd_ref, v_ref, fp_ref, send_ref, tr_ref, first_ref, second_ref):
    face_dofs = fp_ref.shape[0] // 6
    elements = v_ref.shape[1]
    weights = jnp.concatenate([face_rows(fp_ref, f, face_dofs) for f in range(2)], axis=0)
    tr_ref[...] = dot(weights, v_ref[...])
    fill_outbound(tr_ref, send_ref, odd_ref[0] == 1, first_ref, second_ref, face_dofs, elements)


def local_part(v_ref, tr_ref, coef_ref, fp_ref, stiff_ref, liftt_ref, nb_ref, bd_ref, part_ref, jump_ref, traces):
    face_dofs = fp_ref.shape[0] // 6
    elements = v_ref.shape[1]
    traces[: 2 * face_dofs, :] = tr_ref[...]
    weights = jnp.concatenate([face_rows(fp_ref, f, face_dofs) for f in range(2, 6)], axis=0)
    traces[2 * face_dofs :, :] = dot(weights, v_ref[...])
    fill_jump(traces, nb_ref, bd_ref, jump_ref, face_dofs, elements)
    liftt = jnp.concatenate([face_rows(liftt_ref, f, face_dofs) for f in range(6)], axis=0)
    part_ref[...] = coef_ref[...] * dot(stiff_ref[...], v_ref[...]) + dot(liftt.T, jump_ref[...])


def finish_operator(part_ref, v_ref, prev_ref, liftt_ref, tlt_ref, rim, face_dofs):
    half = prev_ref.shape[0]
    time_jump = v_ref[:half, :] - prev_ref[...]
    liftt = jnp.concatenate([face_rows(liftt_ref, f, face_dofs) for f in range(2)] + [tlt_ref[...]], axis=0)
    values = jnp.concatenate([rim[...], time_jump], axis=0)
    return part_ref[...] + dot(liftt.T, values)


def residual_step(
    odd_ref, part_ref, jump_ref, v_ref, rhs_ref, prev_ref, first_in, second_in, coef_ref, inv_ref, fp_ref, liftt_ref, tlt_ref,
    nb_ref, bd_ref, send_ref, res_ref, rim_ref, dir_ref, end_ref, tr_ref, first_ref, second_ref,
):
    face_dofs = fp_ref.shape[0] // 6
    elements = v_ref.shape[1]
    half = prev_ref.shape[0]
    odd = odd_ref[0] == 1
    rim_terms(first_in, second_in, nb_ref, bd_ref, odd, rim_ref, face_dofs, elements)
    res_ref[...] = rhs_ref[...] - finish_operator(part_ref, v_ref, prev_ref, liftt_ref, tlt_ref, rim_ref, face_dofs)
    direction = dot(inv_ref[...], res_ref[...]) / coef_ref[...]
    dir_ref[...] = direction
    end_ref[...] = direction[half:, :]
    weights = jnp.concatenate([face_rows(fp_ref, f, face_dofs) for f in range(2)], axis=0)
    tr_ref[...] = dot(weights, direction)
    fill_outbound(tr_ref, send_ref, odd, first_ref, second_ref, face_dofs, elements)


def column_sum(x):
    return jnp.sum(x, axis=0, keepdims=True)


def total_sum(row):
    return jnp.sum(row, axis=1, keepdims=True)


def image_step(
    odd_ref, part_ref, jump_ref, dir_ref, prev_ref, first_in, second_in, liftt_ref, tlt_ref, nb_ref, bd_ref,
    res_ref, jump0_ref, rim0_ref, v_ref, prev0_ref, coeff_ref, sums_ref, rim, image,
):
    face_dofs = first_in.shape[0]
    elements = dir_ref.shape[1]
    half = prev_ref.shape[0]
    rim_rows = rim.shape[0]
    odd = odd_ref[0] == 1
    rim_terms(first_in, second_in, nb_ref, bd_ref, odd, rim, face_dofs, elements)
    image[...] = finish_operator(part_ref, dir_ref, prev_ref, liftt_ref, tlt_ref, rim, face_dofs)
    res, img = res_ref[...], image[...]
    cross = column_sum(res * img)
    square = column_sum(img * img)
    j0 = jnp.concatenate([jump0_ref[:rim_rows, :] + rim0_ref[...], jump0_ref[rim_rows:, :]], axis=0)
    j1 = jnp.concatenate([jump_ref[:rim_rows, :] + rim[...], jump_ref[rim_rows:, :]], axis=0)
    t0 = v_ref[:half, :] - prev0_ref[...]
    t1 = dir_ref[:half, :] - prev_ref[...]
    bend = square + 0.5 * column_sum(j1 * j1) + column_sum(t1 * t1)
    slope = 0.5 * column_sum(j0 * j1) + column_sum(t0 * t1) - cross
    best = jnp.where(bend > 0.0, -slope / jnp.where(bend > 0.0, bend, 1.0), 0.0)
    r = res - best * img
    j = j0 + best * j1
    t = t0 + best * t1
    base = column_sum(r * r) + 0.5 * column_sum(j * j) + column_sum(t * t)
    tilt = slope + best * bend
    bend_all = total_sum(bend)
    weighted = total_sum(best * bend)
    centre = jnp.where(bend_all > 0.0, weighted / jnp.where(bend_all > 0.0, bend_all, 1.0), 0.0)
    off = centre - best
    base_all = total_sum(base + off * (2.0 * tilt + off * bend))
    tilt_all = total_sum(tilt + off * bend)
    coeff_ref[...] = jnp.concatenate([base, tilt, bend, best, best, best, best, best], axis=0)
    lane = lax.broadcasted_iota(jnp.int32, sums_ref.shape, 1)
    out = jnp.zeros(sums_ref.shape, jnp.float32)
    for i, value in enumerate((total_sum(cross), total_sum(square), base_all, tilt_all, bend_all, centre)):
        out = jnp.where(lane == i, value, out)
    sums_ref[...] = out


def last_step(count, all_ref, coeff_ref, v_ref, dir_ref, smooth_ref, ind_ref, est_ref):
    sums = all_ref[...]
    step = jnp.sum(sums[:, 0:1], axis=0, keepdims=True) / jnp.sum(sums[:, 1:2], axis=0, keepdims=True)
    smooth_ref[...] = v_ref[...] + step * dir_ref[...]
    off = step - sums[:, 5:6]
    total = jnp.sum(sums[:, 2:3] + off * (2.0 * sums[:, 3:4] + off * sums[:, 4:5]), axis=0, keepdims=True)
    delta = step - coeff_ref[3:4, :]
    eta = coeff_ref[0:1, :] + delta * (2.0 * coeff_ref[1:2, :] + delta * coeff_ref[2:3, :])
    ind_ref[...] = eta * count / total
    est_ref[...] = jnp.broadcast_to(jnp.sqrt(total / count), est_ref.shape)


VM = pl.BlockSpec(memory_space=pltpu.VMEM)
SM = pl.BlockSpec(memory_space=pltpu.SMEM)


def call(body, name, outs, args, flops, scratch=(), scalars=0):
    shapes = [jax.ShapeDtypeStruct(s, jnp.float32) for s in outs]
    moved = sum(4 * a.size for a in args) + sum(4 * s.size for s in shapes)
    return pl.pallas_call(
        body,
        name=name,
        out_shape=shapes,
        in_specs=[SM] * scalars + [VM] * (len(args) - scalars),
        out_specs=[VM] * len(outs),
        scratch_shapes=[pltpu.VMEM(s, jnp.float32) for s in scratch],
        cost_estimate=pl.CostEstimate(flops=flops, bytes_accessed=moved, transcendentals=0),
    )(*args)


def on_device(initial, rhs, coef, stiffness, block_inverse, face_proj, lift, time_lift, neighbour, boundary, send_list):
    v0, source = initial[0], rhs[0]
    dofs, elements = v0.shape
    half = time_lift.shape[1]
    traces = face_proj.shape[0]
    face_dofs = traces // 6
    border = send_list.shape[0] // 2
    slabs, parts = lax.axis_size("tm"), lax.axis_size("space")
    devices = slabs * parts
    odd = (lax.axis_index("space") % 2).astype(jnp.int32).reshape(1)
    coef_row = coef.reshape(1, elements)
    send = send_list.reshape(2, border)
    liftt, tlt = lift.T, time_lift.T
    later = [(i, i + 1) for i in range(slabs - 1)]

    def swaps(first):
        pairs = [(i, i + 1) for i in range(first, parts - 1, 2)]
        return pairs + [(j, i) for i, j in pairs]

    def halo(a, b):
        return lax.ppermute(a, "space", swaps(0)), lax.ppermute(b, "space", swaps(1))

    two = 2 * face_dofs
    prev0 = lax.ppermute(v0[half:], "tm", later)
    tr0, a0, b0 = call(
        first_send, "send0", [(two, elements), (face_dofs, border), (face_dofs, border)], (odd, v0, face_proj, send), 2 * two * dofs * elements, scalars=1
    )
    a0, b0 = halo(a0, b0)
    local = functools.partial(
        call, local_part, "local", [(dofs, elements), (traces, elements)], flops=12 * traces * dofs * elements, scratch=[(traces, elements)]
    )
    part0, jump0 = local(args=(v0, tr0, coef_row, face_proj, stiffness, liftt, neighbour, boundary))
    res, rim0, direction, end, tr1, a1, b1 = call(
        residual_step,
        "residual",
        [(dofs, elements), (two, elements), (dofs, elements), (half, elements), (two, elements), (face_dofs, border), (face_dofs, border)],
        (odd, part0, jump0, v0, source, prev0, a0, b0, coef_row, block_inverse, face_proj, liftt, tlt, neighbour, boundary, send),
        12 * dofs * dofs * elements,
        scalars=1,
    )
    prev1 = lax.ppermute(end, "tm", later)
    a1, b1 = halo(a1, b1)
    part1, jump1 = local(args=(direction, tr1, coef_row, face_proj, stiffness, liftt, neighbour, boundary))
    coeffs, sums = call(
        image_step,
        "image",
        [(SUBS, elements), (devices, LANES)],
        (odd, part1, jump1, direction, prev1, a1, b1, liftt, tlt, neighbour, boundary, res, jump0, rim0, v0, prev0),
        12 * dofs * dofs * elements,
        scratch=[(two, elements), (dofs, elements)],
        scalars=1,
    )
    everyone = lax.all_to_all(sums, ("tm", "space"), 0, 0, tiled=True)
    smoothed, indicator, estimate = call(
        functools.partial(last_step, float(elements * devices)),
        "last",
        [(dofs, elements), (1, elements), (1, LANES)],
        (everyone, coeffs, v0, direction),
        4 * dofs * elements,
    )
    return smoothed[None], indicator, estimate[0, :1]


def solution(mesh):
    placed = (
        P("tm", None, "space"),
        P("tm", None, "space"),
        P("space"),
        P(),
        P(),
        P(),
        P(),
        P(),
        P(None, "space"),
        P(None, "space"),
        P("space"),
    )
    return jax.shard_map(
        on_device,
        mesh=mesh,
        in_specs=placed,
        out_specs=(P("tm", None, "space"), P("tm", "space"), P()),
        check_vma=False,
    )
```

time: 215 us -> 52.3 us (0.24)
  blocking collectives: 82.4 us -> 12.9 us
  local copies, waits for them, and re-layouts: 68.9 us -> 2.39 us
  other arithmetic: 24.1 us -> 0 us
  Pallas kernels: 0 us -> 22.3 us
  matrix products: 16.6 us -> 0 us
  starting transfers between devices: 17.8 us -> 13.5 us
  between operations: 4.26 us -> 0.75 us
    psum x2 -> x0, blocking collectives: 82.4 us -> none  [the longest x1 42.4 us: on_device(): total_cross, total_image = lax.psum((cross_sum, image_sum), ('tm', 'space'))]
    gather x4 -> x0, local copies, waits for them, and re-layouts: 43.3 us -> none  [the longest x2 41.8 us: operate(): jnp.take(ext_pool, column_ids, axis=1).reshape(face_dofs * 6, elements)]
    pallas_call x0 -> x6, Pallas kernels: none -> 22.3 us  [call(): pl.pallas_call(body, name=name, out_shape=shapes, in_specs=[SM] * scalars...]
    dot_general x9 -> x0, matrix products: 16.6 us -> none  [the longest x2 4.84 us: operate(): applied = coef * jnp.dot(stiffness, vector, precision=lax.Precision.HIGHEST)]
    all_to_all x0 -> x1, blocking collectives: none -> 12.9 us  [on_device(): everyone = lax.all_to_all(sums, ('tm', 'space'), 0, 0, tiled=True)]
    select_n x5 -> x0, other arithmetic: 12.6 us -> none  [the longest x2 11.7 us: operate(): jnp.take(ext_pool, column_ids, axis=1).reshape(face_dofs * 6, elements)]
    reshape x7 -> x0, local copies, waits for them, and re-layouts: 8.87 us -> none  [the longest x4 6.43 us: operate(): trace_pool = traces.reshape(face_dofs, 6 * elements)]
    select_n x2 -> x0, local copies, waits for them, and re-layouts: 5.71 us -> none  [operate(): jnp.take(ext_pool, column_ids, axis=1).reshape(face_dofs * 6, elements)]
  transfers between devices with their start and end apart: 6 -> 6, of which waited for: 0 -> 0; matrix products, arithmetic and copies ran while one was open for 38% -> 0% of each run, Pallas kernels for 0% -> 22%
where the time goes in v1:
time: 52.3 us; the launch traced here: 51.9 us
  Pallas kernels  22.3 us (43%)
  starting transfers between devices  13.5 us (26%)
  blocking collectives  12.9 us (25%)
  local copies, waits for them, and re-layouts  2.39 us (5%)
  between operations  0.75 us (1%)
    pallas_call x6, Pallas kernels, call(): pl.pallas_call(body, name=name, out_shape=shapes, in_specs=[SM] * scalars...  22.3 us
    all_to_all x1, blocking collectives, on_device(): everyone = lax.all_to_all(sums, ('tm', 'space'), 0, 0, tiled=True)  12.9 us
    ppermute x2, starting transfers between devices, halo(): lax.ppermute(a, 'space', swaps(0))  6.38 us
    ppermute x1, starting transfers between devices, on_device(): prev1 = lax.ppermute(end, 'tm', later)  3.42 us
    ppermute x1, starting transfers between devices, on_device(): prev0 = lax.ppermute(v0[half:], 'tm', later)  2.41 us
    unnamed x12, local copies, waits for them, and re-layouts  1.42 us
    ppermute x2, starting transfers between devices, halo(): lax.ppermute(b, 'space', swaps(1))  1.3 us
  transfers between devices with their start and end apart: 6, of which 0 were waited for; matrix products, arithmetic and copies ran while one was open for 0% of the time, Pallas kernels for 22%

profile of v1, /device:TPU:0, one launch (start us, length us, event | category | flops | bytes accessed | tf_op | source)
XLA Modules:
  0.0 51.9 jit_solution(14993355028093036800)
XLA Ops:
  0.6 1.0 %slice_bitcast_fusion = f32[64,1024]{1,0:T(8,128)S(1)} fusion(f32[1,128,1024]{2,1,0:T(8,128)} %param.11), kind=kLoop, calls=%fused_computation | loop fusion | bytes 524288 | tf_op jit(solution)/shard_map/slice | solution.py:238
  1.6 2.4 %collective-permute-start = (f32[64,1024]{1,0:T(8,128)S(1)}, f32[64,1024]{1,0:T(8,128)S(1)}, u32[]{:S(2)}, u32[]{:S(2)}) collective-permute-start(f32[64,1024]{1,0:T(8,128)S(1)} %slice_bitcast_fusion), channel_id=1, source_target_pairs={{0,8},{8,16},{16,24},{1,9},{9,17},{17,25},{2,10},{10,18},{18,26},{... | collective-permute-start | bytes 786440 | tf_op jit(solution)/shard_map/ppermute | solution.py:238
  4.0 2.2 %send0.1 = (f32[64,1024]{1,0:T(8,128)}, f32[32,128]{1,0:T(8,128)}, f32[32,128]{1,0:T(8,128)}) custom-call(s32[1]{0:T(128)} %bitcast.odd_ref, f32[128,1024]{1,0:T(8,128)} %bitcast.16, f32[192,128]{1,0:T(8,128)} %fp_ref.7, s32[2,128]{1,0:T(2,128)} %bitcast.33), custom_call_target="tpu_custom_call" | custom-call | flops 16777216 | bytes 918532 | tf_op jit(solution)/shard_map/send0/pallas_call | solution.py:204
  6.3 2.3 %collective-permute-start.1 = (f32[32,128]{1,0:T(8,128)}, f32[32,128]{1,0:T(8,128)S(1)}, u32[]{:S(2)}, u32[]{:S(2)}) collective-permute-start(f32[32,128]{1,0:T(8,128)} %get-tuple-element.25), channel_id=1, source_target_pairs={{0,1},{2,3},{4,5},{6,7},{1,0},{3,2},{5,4},{7,6},{8,9},{10,11},{12,... | collective-permute-start | bytes 49160 | tf_op jit(solution)/shard_map/ppermute | solution.py:235
  8.6 0.7 %collective-permute-start.2 = (f32[32,128]{1,0:T(8,128)}, f32[32,128]{1,0:T(8,128)S(1)}, u32[]{:S(2)}, u32[]{:S(2)}) collective-permute-start(f32[32,128]{1,0:T(8,128)} %get-tuple-element.26), channel_id=1, source_target_pairs={{1,2},{3,4},{5,6},{2,1},{4,3},{6,5},{9,10},{11,12},{13,14},{10,9},... | collective-permute-start | bytes 49160 | tf_op jit(solution)/shard_map/ppermute | solution.py:235
  9.2 4.7 %local.2 = (f32[128,1024]{1,0:T(8,128)}, f32[192,1024]{1,0:T(8,128)}) custom-call(f32[128,1024]{1,0:T(8,128)} %bitcast.17, f32[64,1024]{1,0:T(8,128)} %get-tuple-element.22.tr_ref, f32[1,1024]{1,0:T(1,128)} %bitcast.29, f32[192,128]{1,0:T(8,128)} %fp_ref.7, f32[128,128]{1,0:T(8,128)} %stiff_ref.3, f32[192,128]{1,0:T(8,128)} %bitcast.21, s32[6,1024]{1,0:T(8,128)} %nb_ref.7, ...), custom_call_target="tpu_custom_call" | custom-call | flops 301989888 | bytes 2412544 | tf_op jit(solution)/shard_map/local/pallas_call | solution.py:204
  13.9 0.0 collective-permute-done.1.first_in
  13.9 0.0 copy-start.3
  13.9 0.0 collective-permute-done.2.second_in
  13.9 0.0 copy-start.5
  14.0 0.0 collective-permute-done.prev_ref.prev0_ref
  14.0 0.0 copy-start
  14.0 0.6 %copy-done.3 = f32[32,128]{1,0:T(8,128)} copy-done((f32[32,128]{1,0:T(8,128)}, f32[32,128]{1,0:T(8,128)S(1)}, u32[]{:S(2)}) %copy-start.3) | copy-done | bytes 16408
  14.5 0.0 copy-done.5
  14.5 0.1 copy-done
  14.7 4.2 %residual.1 = (f32[128,1024]{1,0:T(8,128)}, f32[64,1024]{1,0:T(8,128)}, f32[128,1024]{1,0:T(8,128)}, f32[64,1024]{1,0:T(8,128)}, f32[64,1024]{1,0:T(8,128)}, /*index=5*/f32[32,128]{1,0:T(8,128)}, f32[32,128]{1,0:T(8,128)}) custom-call(s32[1]{0:T(128)} %bitcast.odd_ref, f32[128,1024]{1,0:T(8,128)} %get-tuple-element.23.part_ref, ...), custom_call_target="tpu_custom_call" | custom-call | flops 201326592 | bytes 4871172 | tf_op jit(solution)/shard_map/residual/pallas_call | solution.py:204
  18.9 3.4 %collective-permute-start.3 = (f32[64,1024]{1,0:T(8,128)}, f32[64,1024]{1,0:T(8,128)S(1)}, u32[]{:S(2)}, u32[]{:S(2)}) collective-permute-start(f32[64,1024]{1,0:T(8,128)} %get-tuple-element.31), channel_id=1, source_target_pairs={{0,8},{8,16},{16,24},{1,9},{9,17},{17,25},{2,10},{10,18},{18,26},{... | collective-permute-start | bytes 786440 | tf_op jit(solution)/shard_map/ppermute | solution.py:255
  22.3 4.1 %collective-permute-start.4 = (f32[32,128]{1,0:T(8,128)}, f32[32,128]{1,0:T(8,128)S(1)}, u32[]{:S(2)}, u32[]{:S(2)}) collective-permute-start(f32[32,128]{1,0:T(8,128)} %get-tuple-element.32), channel_id=1, source_target_pairs={{0,1},{2,3},{4,5},{6,7},{1,0},{3,2},{5,4},{7,6},{8,9},{10,11},{12,... | collective-permute-start | bytes 49160 | tf_op jit(solution)/shard_map/ppermute | solution.py:235
  26.4 0.7 %collective-permute-start.5 = (f32[32,128]{1,0:T(8,128)}, f32[32,128]{1,0:T(8,128)S(1)}, u32[]{:S(2)}, u32[]{:S(2)}) collective-permute-start(f32[32,128]{1,0:T(8,128)} %get-tuple-element.33), channel_id=1, source_target_pairs={{1,2},{3,4},{5,6},{2,1},{4,3},{6,5},{9,10},{11,12},{13,14},{10,9},... | collective-permute-start | bytes 49160 | tf_op jit(solution)/shard_map/ppermute | solution.py:235
  27.0 4.7 %local.3 = (f32[128,1024]{1,0:T(8,128)}, f32[192,1024]{1,0:T(8,128)}) custom-call(f32[128,1024]{1,0:T(8,128)} %get-tuple-element.27.v_ref.dir_ref, f32[64,1024]{1,0:T(8,128)} %get-tuple-element.28.tr_ref, f32[1,1024]{1,0:T(1,128)} %bitcast.31, f32[192,128]{1,0:T(8,128)} %fp_ref.7, f32[128,128]{1,0:T(8,128)} %stiff_ref.3, f32[192,128]{1,0:T(8,128)} %bitcast.23, ...), custom_call_target="tpu_custom_call" | custom-call | flops 301989888 | bytes 2412544 | tf_op jit(solution)/shard_map/local/pallas_call | solution.py:204
  31.7 0.0 collective-permute-done.4.first_in
  31.7 0.0 copy-start.2
  31.8 0.0 collective-permute-done.5.second_in
  31.8 0.0 copy-start.4
  31.8 0.0 collective-permute-done.3.prev_ref
  31.8 0.0 copy-start.1
  31.8 0.6 %copy-done.2 = f32[32,128]{1,0:T(8,128)} copy-done((f32[32,128]{1,0:T(8,128)}, f32[32,128]{1,0:T(8,128)S(1)}, u32[]{:S(2)}) %copy-start.2) | copy-done | bytes 16408
  32.3 0.0 copy-done.4
  32.4 0.1 copy-done.1
  32.5 4.3 %image.1 = (f32[8,1024]{1,0:T(8,128)}, f32[32,128]{1,0:T(8,128)}) custom-call(s32[1]{0:T(128)} %bitcast.odd_ref, f32[128,1024]{1,0:T(8,128)} %get-tuple-element.29.part_ref, f32[192,1024]{1,0:T(8,128)} %get-tuple-element.30.jump_ref, f32[128,1024]{1,0:T(8,128)} %get-tuple-element.27.v_ref.dir_ref, f32[64,1024]{1,0:T(8,128)} %copy-done.1, ...), custom_call_target="tpu_custom_call" | custom-call | flops 201326592 | bytes 4718596 | tf_op jit(solution)/shard_map/image/pallas_call | solution.py:204
  36.7 12.9 %all_to_all.11 = f32[32,1,128]{2,1,0:T(1,128)} all-to-all(f32[32,1,128]{2,1,0:T(1,128)} %bitcast.32), channel_id=1, replica_groups=mesh['tm'=4,'space'=8] {'tm','space'}, dimensions={0} | all-to-all | bytes 32768 | tf_op jit(solution)/shard_map/all_to_all | solution.py:267
  49.7 2.2 %last.1 = (f32[128,1024]{1,0:T(8,128)}, f32[1,1024]{1,0:T(1,128)}, f32[1,128]{1,0:T(1,128)}) custom-call(f32[32,128]{1,0:T(8,128)} %bitcast.28, f32[8,1024]{1,0:T(8,128)} %get-tuple-element.37.coeff_ref, f32[128,1024]{1,0:T(8,128)} %bitcast.20, f32[128,1024]{1,0:T(8,128)} %get-tuple-element.27.v_ref.dir_ref), custom_call_target="tpu_custom_call" | custom-call | flops 524288 | bytes 1626624 | tf_op jit(solution)/shard_map/last/pallas_call | solution.py:204
Async XLA Ops:
  1.6 12.4 %collective-permute-start = (f32[64,1024]{1,0:T(8,128)S(1)}, f32[64,1024]{1,0:T(8,128)S(1)}, u32[]{:S(2)}, u32[]{:S(2)}) collective-permute-start(f32[64,1024]{1,0:T(8,128)S(1)} %slice_bitcast_fusion), channel_id=1, source_target_pairs={{0,8},{8,16},{16,24},{1,9},{9,17},{17,25},{2,10},{10,18},{18,26},{... | collective-permute-start | bytes 786440 | tf_op jit(solution)/shard_map/ppermute | solution.py:238
  6.3 7.7 %collective-permute-start.1 = (f32[32,128]{1,0:T(8,128)}, f32[32,128]{1,0:T(8,128)S(1)}, u32[]{:S(2)}, u32[]{:S(2)}) collective-permute-start(f32[32,128]{1,0:T(8,128)} %get-tuple-element.25), channel_id=1, source_target_pairs={{0,1},{2,3},{4,5},{6,7},{1,0},{3,2},{5,4},{7,6},{8,9},{10,11},{12,... | collective-permute-start | bytes 49160 | tf_op jit(solution)/shard_map/ppermute | solution.py:235
  8.6 5.4 %collective-permute-start.2 = (f32[32,128]{1,0:T(8,128)}, f32[32,128]{1,0:T(8,128)S(1)}, u32[]{:S(2)}, u32[]{:S(2)}) collective-permute-start(f32[32,128]{1,0:T(8,128)} %get-tuple-element.26), channel_id=1, source_target_pairs={{1,2},{3,4},{5,6},{2,1},{4,3},{6,5},{9,10},{11,12},{13,14},{10,9},... | collective-permute-start | bytes 49160 | tf_op jit(solution)/shard_map/ppermute | solution.py:235
  13.9 0.6 %copy-start.3 = (f32[32,128]{1,0:T(8,128)}, f32[32,128]{1,0:T(8,128)S(1)}, u32[]{:S(2)}) copy-start(f32[32,128]{1,0:T(8,128)S(1)} %collective-permute-done.1.first_in) | copy-start | bytes 49156
  13.9 0.6 %copy-start.5 = (f32[32,128]{1,0:T(8,128)}, f32[32,128]{1,0:T(8,128)S(1)}, u32[]{:S(2)}) copy-start(f32[32,128]{1,0:T(8,128)S(1)} %collective-permute-done.2.second_in) | copy-start | bytes 49156
  14.0 0.7 %copy-start = (f32[64,1024]{1,0:T(8,128)}, f32[64,1024]{1,0:T(8,128)S(1)}, u32[]{:S(2)}) copy-start(f32[64,1024]{1,0:T(8,128)S(1)} %collective-permute-done.prev_ref.prev0_ref) | copy-start | bytes 786436
  18.9 12.9 %collective-permute-start.3 = (f32[64,1024]{1,0:T(8,128)}, f32[64,1024]{1,0:T(8,128)S(1)}, u32[]{:S(2)}, u32[]{:S(2)}) collective-permute-start(f32[64,1024]{1,0:T(8,128)} %get-tuple-element.31), channel_id=1, source_target_pairs={{0,8},{8,16},{16,24},{1,9},{9,17},{17,25},{2,10},{10,18},{18,26},{... | collective-permute-start | bytes 786440 | tf_op jit(solution)/shard_map/ppermute | solution.py:255
  22.3 9.4 %collective-permute-start.4 = (f32[32,128]{1,0:T(8,128)}, f32[32,128]{1,0:T(8,128)S(1)}, u32[]{:S(2)}, u32[]{:S(2)}) collective-permute-start(f32[32,128]{1,0:T(8,128)} %get-tuple-element.32), channel_id=1, source_target_pairs={{0,1},{2,3},{4,5},{6,7},{1,0},{3,2},{5,4},{7,6},{8,9},{10,11},{12,... | collective-permute-start | bytes 49160 | tf_op jit(solution)/shard_map/ppermute | solution.py:235
  26.4 5.4 %collective-permute-start.5 = (f32[32,128]{1,0:T(8,128)}, f32[32,128]{1,0:T(8,128)S(1)}, u32[]{:S(2)}, u32[]{:S(2)}) collective-permute-start(f32[32,128]{1,0:T(8,128)} %get-tuple-element.33), channel_id=1, source_target_pairs={{1,2},{3,4},{5,6},{2,1},{4,3},{6,5},{9,10},{11,12},{13,14},{10,9},... | collective-permute-start | bytes 49160 | tf_op jit(solution)/shard_map/ppermute | solution.py:235
  31.7 0.6 %copy-start.2 = (f32[32,128]{1,0:T(8,128)}, f32[32,128]{1,0:T(8,128)S(1)}, u32[]{:S(2)}) copy-start(f32[32,128]{1,0:T(8,128)S(1)} %collective-permute-done.4.first_in) | copy-start | bytes 49156
  31.8 0.6 %copy-start.4 = (f32[32,128]{1,0:T(8,128)}, f32[32,128]{1,0:T(8,128)S(1)}, u32[]{:S(2)}) copy-start(f32[32,128]{1,0:T(8,128)S(1)} %collective-permute-done.5.second_in) | copy-start | bytes 49156
  31.8 0.7 %copy-start.1 = (f32[64,1024]{1,0:T(8,128)}, f32[64,1024]{1,0:T(8,128)S(1)}, u32[]{:S(2)}) copy-start(f32[64,1024]{1,0:T(8,128)S(1)} %collective-permute-done.3.prev_ref) | copy-start | bytes 786436

commit v2 on v1

--- a/solution.py
+++ b/solution.py
@@ -209,6 +209,7 @@
         out_specs=[VM] * len(outs),
         scratch_shapes=[pltpu.VMEM(s, jnp.float32) for s in scratch],
         cost_estimate=pl.CostEstimate(flops=flops, bytes_accessed=moved, transcendentals=0),
+        compiler_params=pltpu.CompilerParams(vmem_limit_bytes=20 * 2**20),
     )(*args)
 
 

time: 52.3 us -> 40.5 us (0.77)
  Pallas kernels: 22.3 us -> 10.1 us
    pallas_call x6, Pallas kernels: 22.3 us -> 10.1 us  [call(): pl.pallas_call(body, name=name, out_shape=shapes, in_specs=[SM] * scalars...]
    unnamed x12 -> x24, local copies, waits for them, and re-layouts: 1.42 us -> 1.61 us
  transfers between devices with their start and end apart: 6 -> 6, of which waited for: 0 -> 0; matrix products, arithmetic and copies ran while one was open for 0% -> 0% of each run, Pallas kernels for 22% -> 15%
where the time goes in v2:
time: 40.5 us; the launch traced here: 40.2 us
  starting transfers between devices  13.6 us (34%)
  blocking collectives  13 us (32%)
  Pallas kernels  10.1 us (25%)
  local copies, waits for them, and re-layouts  2.64 us (7%)
  between operations  0.9 us (2%)
    all_to_all x1, blocking collectives, on_device(): everyone = lax.all_to_all(sums, ('tm', 'space'), 0, 0, tiled=True)  13 us
    pallas_call x6, Pallas kernels, call(): pl.pallas_call(body, name=name, out_shape=shapes, in_specs=[SM] * scalars...  10.1 us
    ppermute x2, starting transfers between devices, halo(): lax.ppermute(a, 'space', swaps(0))  6.44 us
    ppermute x1, starting transfers between devices, on_device(): prev1 = lax.ppermute(end, 'tm', later)  3.43 us
    ppermute x1, starting transfers between devices, on_device(): prev0 = lax.ppermute(v0[half:], 'tm', later)  2.41 us
    unnamed x24, local copies, waits for them, and re-layouts  1.61 us
    ppermute x2, starting transfers between devices, halo(): lax.ppermute(b, 'space', swaps(1))  1.3 us
    slice x1, local copies, waits for them, and re-layouts, on_device(): prev0 = lax.ppermute(v0[half:], 'tm', later)  1.03 us
  transfers between devices with their start and end apart: 6, of which 0 were waited for; matrix products, arithmetic and copies ran while one was open for 0% of the time, Pallas kernels for 15%

profile of v2, /device:TPU:0, one launch (start us, length us, event | category | flops | bytes accessed | tf_op | source)
XLA Modules:
  0.0 40.2 jit_solution(831552658101618597)
XLA Ops:
  0.6 0.0 copy-start
  0.6 1.0 %slice_bitcast_fusion = f32[64,1024]{1,0:T(8,128)S(1)} fusion(f32[1,128,1024]{2,1,0:T(8,128)} %param.11), kind=kLoop, calls=%fused_computation | loop fusion | bytes 524288 | tf_op jit(solution)/shard_map/slice | solution.py:239
  1.7 2.4 %collective-permute-start = (f32[64,1024]{1,0:T(8,128)S(1)}, f32[64,1024]{1,0:T(8,128)S(1)}, u32[]{:S(2)}, u32[]{:S(2)}) collective-permute-start(f32[64,1024]{1,0:T(8,128)S(1)} %slice_bitcast_fusion), channel_id=1, source_target_pairs={{0,8},{8,16},{16,24},{1,9},{9,17},{17,25},{2,10},{10,18},{18,26},{... | collective-permute-start | bytes 786440 | tf_op jit(solution)/shard_map/ppermute | solution.py:239
  4.1 0.0 copy-start.11
  4.1 0.0 copy-done
  4.1 0.7 %copy-done.11 = s32[256]{0:T(256)S(1)} copy-done((s32[256]{0:T(256)S(1)}, s32[256]{0:T(256)}, u32[]{:S(2)}) %copy-start.11) | copy-done | bytes 1048
  4.8 0.0 copy-start.1
  4.8 0.9 %copy-done.1 = f32[192,128]{1,0:T(8,128)S(1)} copy-done((f32[192,128]{1,0:T(8,128)S(1)}, f32[192,128]{1,0:T(8,128)}, u32[]{:S(2)}) %copy-start.1) | copy-done | bytes 98328
  5.7 0.0 copy-start.3
  5.7 0.0 copy-start.4
  5.7 0.0 copy-start.5
  5.7 0.0 copy-start.7
  5.7 0.5 %send0.1 = (f32[64,1024]{1,0:T(8,128)S(1)}, f32[32,128]{1,0:T(8,128)S(1)}, f32[32,128]{1,0:T(8,128)S(1)}) custom-call(s32[1]{0:T(128)} %bitcast.odd_ref, f32[128,1024]{1,0:T(8,128)S(1)} %bitcast.16, f32[192,128]{1,0:T(8,128)S(1)} %copy-done.1, s32[2,128]{1,0:T(2,128)S(1)} %bitcast.33), custom_call_target="tpu_custom_call" | custom-call | flops 16777216 | bytes 918532 | tf_op jit(solution)/shard_map/send0/pallas_call | solution.py:204
  6.2 0.0 copy-start.10
  6.2 2.4 %collective-permute-start.1 = (f32[32,128]{1,0:T(8,128)S(1)}, f32[32,128]{1,0:T(8,128)S(1)}, u32[]{:S(2)}, u32[]{:S(2)}) collective-permute-start(f32[32,128]{1,0:T(8,128)S(1)} %get-tuple-element.25), channel_id=1, source_target_pairs={{0,1},{2,3},{4,5},{6,7},{1,0},{3,2},{5,4},{7,6},{8,9},{10,11},{12,... | collective-permute-start | bytes 49160 | tf_op jit(solution)/shard_map/ppermute | solution.py:236
  8.6 0.7 %collective-permute-start.2 = (f32[32,128]{1,0:T(8,128)S(1)}, f32[32,128]{1,0:T(8,128)S(1)}, u32[]{:S(2)}, u32[]{:S(2)}) collective-permute-start(f32[32,128]{1,0:T(8,128)S(1)} %get-tuple-element.26), channel_id=1, source_target_pairs={{1,2},{3,4},{5,6},{2,1},{4,3},{6,5},{9,10},{11,12},{13,14},{10,9},... | collective-permute-start | bytes 49160 | tf_op jit(solution)/shard_map/ppermute | solution.py:236
  9.3 0.0 copy-done.3
  9.3 0.0 copy-done.4
  9.3 0.0 copy-done.5
  9.3 0.0 copy-done.7
  9.3 0.0 copy-done.10
  9.3 0.0 copy-start.6
  9.3 0.0 copy-start.8
  9.3 0.0 copy-start.9
  9.3 2.7 %local.2 = (f32[128,1024]{1,0:T(8,128)S(1)}, f32[192,1024]{1,0:T(8,128)S(1)}) custom-call(f32[128,1024]{1,0:T(8,128)S(1)} %bitcast.17, f32[64,1024]{1,0:T(8,128)S(1)} %get-tuple-element.22.tr_ref, f32[1,1024]{1,0:T(1,128)S(1)} %bitcast.29, f32[192,128]{1,0:T(8,128)S(1)} %copy-done.1, f32[128,128]{1,0:T(8,128)S(1)} %copy-done.7, f32[192,128]{1,0:T(8,128)S(1)} %bitcast.21, ...), custom_call_target="tpu_custom_call" | custom-call | flops 301989888 | bytes 2412544 | tf_op jit(solution)/shard_map/local/pallas_call | solution.py:204
  12.1 0.0 collective-permute-done.1.first_in
  12.1 0.0 collective-permute-done.2.second_in
  12.1 0.0 collective-permute-done.prev_ref.prev0_ref
  12.1 0.0 copy-done.6
  12.1 0.0 copy-done.8
  12.1 0.0 copy-done.9
  12.2 0.0 copy-start.2
  12.2 1.6 %residual.1 = (f32[128,1024]{1,0:T(8,128)S(1)}, f32[64,1024]{1,0:T(8,128)S(1)}, f32[128,1024]{1,0:T(8,128)S(1)}, f32[64,1024]{1,0:T(8,128)S(1)}, f32[64,1024]{1,...) custom-call(s32[1]{0:T(128)} %bitcast.odd_ref, f32[128,1024]{1,0:T(8,128)S(1)} %get-tuple-element.23.part_ref, ...), custom_call_target="tpu_custom_call" | custom-call | flops 201326592 | bytes 4871172 | tf_op jit(solution)/shard_map/residual/pallas_call | solution.py:204
  13.8 3.4 %collective-permute-start.3 = (f32[64,1024]{1,0:T(8,128)S(1)}, f32[64,1024]{1,0:T(8,128)S(1)}, u32[]{:S(2)}, u32[]{:S(2)}) collective-permute-start(f32[64,1024]{1,0:T(8,128)S(1)} %get-tuple-element.31), channel_id=1, source_target_pairs={{0,8},{8,16},{16,24},{1,9},{9,17},{17,25},{2,10},{10,18},{18,26},{... | collective-permute-start | bytes 786440 | tf_op jit(solution)/shard_map/ppermute | solution.py:256
  17.2 4.1 %collective-permute-start.4 = (f32[32,128]{1,0:T(8,128)S(1)}, f32[32,128]{1,0:T(8,128)S(1)}, u32[]{:S(2)}, u32[]{:S(2)}) collective-permute-start(f32[32,128]{1,0:T(8,128)S(1)} %get-tuple-element.32), channel_id=1, source_target_pairs={{0,1},{2,3},{4,5},{6,7},{1,0},{3,2},{5,4},{7,6},{8,9},{10,11},{12,... | collective-permute-start | bytes 49160 | tf_op jit(solution)/shard_map/ppermute | solution.py:236
  21.3 0.7 %collective-permute-start.5 = (f32[32,128]{1,0:T(8,128)S(1)}, f32[32,128]{1,0:T(8,128)S(1)}, u32[]{:S(2)}, u32[]{:S(2)}) collective-permute-start(f32[32,128]{1,0:T(8,128)S(1)} %get-tuple-element.33), channel_id=1, source_target_pairs={{1,2},{3,4},{5,6},{2,1},{4,3},{6,5},{9,10},{11,12},{13,14},{10,9},... | collective-permute-start | bytes 49160 | tf_op jit(solution)/shard_map/ppermute | solution.py:236
  21.9 0.0 copy-done.2
  22.0 2.8 %local.3 = (f32[128,1024]{1,0:T(8,128)S(1)}, f32[192,1024]{1,0:T(8,128)S(1)}) custom-call(f32[128,1024]{1,0:T(8,128)S(1)} %get-tuple-element.27.v_ref.dir_ref, f32[64,1024]{1,0:T(8,128)S(1)} %get-tuple-element.28.tr_ref, f32[1,1024]{1,0:T(1,128)S(1)} %bitcast.31, f32[192,128]{1,0:T(8,128)S(1)} %copy-done.2, f32[128,128]{1,0:T(8,128)S(1)} %copy-done.7, ...), custom_call_target="tpu_custom_call" | custom-call | flops 301989888 | bytes 2412544 | tf_op jit(solution)/shard_map/local/pallas_call | solution.py:204
  24.7 0.0 collective-permute-done.4.first_in
  24.7 0.0 collective-permute-done.5.second_in
  24.7 0.0 collective-permute-done.3.prev_ref
  24.8 1.4 %image.1 = (f32[8,1024]{1,0:T(8,128)S(1)}, f32[32,128]{1,0:T(8,128)S(1)}) custom-call(s32[1]{0:T(128)} %bitcast.odd_ref, f32[128,1024]{1,0:T(8,128)S(1)} %get-tuple-element.29.part_ref, f32[192,1024]{1,0:T(8,128)S(1)} %get-tuple-element.30.jump_ref, f32[128,1024]{1,0:T(8,128)S(1)} %get-tuple-element.27.v_ref.dir_ref, ...), custom_call_target="tpu_custom_call" | custom-call | flops 201326592 | bytes 4718596 | tf_op jit(solution)/shard_map/image/pallas_call | solution.py:204
  26.2 13.0 %all_to_all.11 = f32[32,1,128]{2,1,0:T(1,128)S(1)} all-to-all(f32[32,1,128]{2,1,0:T(1,128)S(1)} %bitcast.32), channel_id=1, replica_groups=mesh['tm'=4,'space'=8] {'tm','space'}, dimensions={0} | all-to-all | bytes 32768 | tf_op jit(solution)/shard_map/all_to_all | solution.py:268
  39.2 1.0 %last.1 = (f32[128,1024]{1,0:T(8,128)}, f32[1,1024]{1,0:T(1,128)}, f32[1,128]{1,0:T(1,128)}) custom-call(f32[32,128]{1,0:T(8,128)S(1)} %bitcast.28, f32[8,1024]{1,0:T(8,128)S(1)} %get-tuple-element.37.coeff_ref, f32[128,1024]{1,0:T(8,128)S(1)} %bitcast.20, f32[128,1024]{1,0:T(8,128)S(1)} %get-tuple-element.27.v_ref.dir_ref), custom_call_target="tpu_custom_call" | custom-call | flops 524288 | bytes 1626624 | tf_op jit(solution)/shard_map/last/pallas_call | solution.py:204
Async XLA Ops:
  0.6 3.5 %copy-start = (f32[1,128,1024]{2,1,0:T(8,128)S(1)}, f32[1,128,1024]{2,1,0:T(8,128)}, u32[]{:S(2)}) copy-start(f32[1,128,1024]{2,1,0:T(8,128)} %param.11) | copy-start | bytes 1572868
  1.7 10.4 %collective-permute-start = (f32[64,1024]{1,0:T(8,128)S(1)}, f32[64,1024]{1,0:T(8,128)S(1)}, u32[]{:S(2)}, u32[]{:S(2)}) collective-permute-start(f32[64,1024]{1,0:T(8,128)S(1)} %slice_bitcast_fusion), channel_id=1, source_target_pairs={{0,8},{8,16},{16,24},{1,9},{9,17},{17,25},{2,10},{10,18},{18,26},{... | collective-permute-start | bytes 786440 | tf_op jit(solution)/shard_map/ppermute | solution.py:239
  4.1 0.7 %copy-start.11 = (s32[256]{0:T(256)S(1)}, s32[256]{0:T(256)}, u32[]{:S(2)}) copy-start(s32[256]{0:T(256)} %param.21) | copy-start | bytes 3076
  4.8 0.9 %copy-start.1 = (f32[192,128]{1,0:T(8,128)S(1)}, f32[192,128]{1,0:T(8,128)}, u32[]{:S(2)}) copy-start(f32[192,128]{1,0:T(8,128)} %fp_ref.7) | copy-start | bytes 294916
  5.7 3.6 %copy-start.3 = (f32[128,192]{0,1:T(8,128)S(1)}, f32[128,192]{0,1:T(8,128)}, u32[]{:S(2)}) copy-start(f32[128,192]{0,1:T(8,128)} %param.17) | copy-start | bytes 294916
  5.7 3.6 %copy-start.4 = (s32[6,1024]{1,0:T(8,128)S(1)}, s32[6,1024]{1,0:T(8,128)}, u32[]{:S(2)}) copy-start(s32[6,1024]{1,0:T(8,128)} %nb_ref.7) | copy-start | bytes 73732
  5.7 3.6 %copy-start.5 = (s32[6,1024]{1,0:T(8,128)S(1)}, s32[6,1024]{1,0:T(8,128)}, u32[]{:S(2)}) copy-start(s32[6,1024]{1,0:T(8,128)} %bd_ref.7) | copy-start | bytes 73732
  5.7 3.6 %copy-start.7 = (f32[128,128]{1,0:T(8,128)S(1)}, f32[128,128]{1,0:T(8,128)}, u32[]{:S(2)}) copy-start(f32[128,128]{1,0:T(8,128)} %stiff_ref.3) | copy-start | bytes 196612
  6.2 3.1 %copy-start.10 = (f32[1024]{0:T(1024)S(1)}, f32[1024]{0:T(1024)}, u32[]{:S(2)}) copy-start(f32[1024]{0:T(1024)} %param.13) | copy-start | bytes 12292
  6.2 5.9 %collective-permute-start.1 = (f32[32,128]{1,0:T(8,128)S(1)}, f32[32,128]{1,0:T(8,128)S(1)}, u32[]{:S(2)}, u32[]{:S(2)}) collective-permute-start(f32[32,128]{1,0:T(8,128)S(1)} %get-tuple-element.25), channel_id=1, source_target_pairs={{0,1},{2,3},{4,5},{6,7},{1,0},{3,2},{5,4},{7,6},{8,9},{10,11},{12,... | collective-permute-start | bytes 49160 | tf_op jit(solution)/shard_map/ppermute | solution.py:236
  8.6 3.5 %collective-permute-start.2 = (f32[32,128]{1,0:T(8,128)S(1)}, f32[32,128]{1,0:T(8,128)S(1)}, u32[]{:S(2)}, u32[]{:S(2)}) collective-permute-start(f32[32,128]{1,0:T(8,128)S(1)} %get-tuple-element.26), channel_id=1, source_target_pairs={{1,2},{3,4},{5,6},{2,1},{4,3},{6,5},{9,10},{11,12},{13,14},{10,9},... | collective-permute-start | bytes 49160 | tf_op jit(solution)/shard_map/ppermute | solution.py:236
  9.3 2.8 %copy-start.6 = (f32[1,128,1024]{2,1,0:T(8,128)S(1)}, f32[1,128,1024]{2,1,0:T(8,128)}, u32[]{:S(2)}) copy-start(f32[1,128,1024]{2,1,0:T(8,128)} %param.12) | copy-start | bytes 1572868
  9.3 2.8 %copy-start.8 = (f32[128,64]{0,1:T(8,128)S(1)}, f32[128,64]{0,1:T(8,128)}, u32[]{:S(2)}) copy-start(f32[128,64]{0,1:T(8,128)} %param.18) | copy-start | bytes 98308
  9.3 2.8 %copy-start.9 = (f32[128,128]{1,0:T(8,128)S(1)}, f32[128,128]{1,0:T(8,128)}, u32[]{:S(2)}) copy-start(f32[128,128]{1,0:T(8,128)} %inv_ref.1) | copy-start | bytes 196612
  12.2 9.8 %copy-start.2 = (f32[192,128]{1,0:T(8,128)S(1)}, f32[192,128]{1,0:T(8,128)}, u32[]{:S(2)}) copy-start(f32[192,128]{1,0:T(8,128)} %fp_ref.7) | copy-start | bytes 294916
  13.8 11.0 %collective-permute-start.3 = (f32[64,1024]{1,0:T(8,128)S(1)}, f32[64,1024]{1,0:T(8,128)S(1)}, u32[]{:S(2)}, u32[]{:S(2)}) collective-permute-start(f32[64,1024]{1,0:T(8,128)S(1)} %get-tuple-element.31), channel_id=1, source_target_pairs={{0,8},{8,16},{16,24},{1,9},{9,17},{17,25},{2,10},{10,18},{18,26},{... | collective-permute-start | bytes 786440 | tf_op jit(solution)/shard_map/ppermute | solution.py:256
  17.2 7.5 %collective-permute-start.4 = (f32[32,128]{1,0:T(8,128)S(1)}, f32[32,128]{1,0:T(8,128)S(1)}, u32[]{:S(2)}, u32[]{:S(2)}) collective-permute-start(f32[32,128]{1,0:T(8,128)S(1)} %get-tuple-element.32), channel_id=1, source_target_pairs={{0,1},{2,3},{4,5},{6,7},{1,0},{3,2},{5,4},{7,6},{8,9},{10,11},{12,... | collective-permute-start | bytes 49160 | tf_op jit(solution)/shard_map/ppermute | solution.py:236
  21.3 3.4 %collective-permute-start.5 = (f32[32,128]{1,0:T(8,128)S(1)}, f32[32,128]{1,0:T(8,128)S(1)}, u32[]{:S(2)}, u32[]{:S(2)}) collective-permute-start(f32[32,128]{1,0:T(8,128)S(1)} %get-tuple-element.33), channel_id=1, source_target_pairs={{1,2},{3,4},{5,6},{2,1},{4,3},{6,5},{9,10},{11,12},{13,14},{10,9},... | collective-permute-start | bytes 49160 | tf_op jit(solution)/shard_map/ppermute | solution.py:236

commit v3 on v2

--- a/solution.py
+++ b/solution.py
@@ -32,8 +32,13 @@
     return ref[pl.ds(face, face_dofs, stride=6), :]
 
 
-def fill_outbound(traces, send_ref, odd, first_ref, second_ref, face_dofs, elements):
+def is_odd():
+    return lax.rem(lax.axis_index("space"), 2) == 1
+
+
+def fill_outbound(traces, send_ref, first_ref, second_ref, face_dofs, elements):
     per_face = elements // LANES
+    odd = is_odd()
 
     def tile_of(tile, r):
         face, col = divmod(tile, per_face)
@@ -67,34 +72,45 @@
                 jump_ref[rows, cols] = traces[rows, cols] - found[r] * open_face
 
 
-def rim_terms(first_ref, second_ref, nb_ref, bd_ref, odd, rim_ref, face_dofs, elements):
-    border = first_ref.shape[1]
-    tiles = border // LANES
+def rim_terms(first_ref, second_ref, nb_ref, bd_ref, rim_ref, face_dofs, elements):
+    tiles = first_ref.shape[1] // LANES
+    odd, place, parts = is_odd(), lax.axis_index("space"), lax.axis_size("space")
+    sides = []
+    for side in range(2):
+        for t in range(tiles):
+            cols = slice(t * LANES, (t + 1) * LANES)
+            a, b = first_ref[:, cols], second_ref[:, cols]
+            values = jnp.where(odd, a, b) if side == 0 else jnp.where(odd, b, a)
+            there = place > 0 if side == 0 else place < parts - 1
+            sides.append(jnp.where(there, values, 0.0))
+
+    def tile_of(tile, r):
+        return sides[tile][r * SUBS : (r + 1) * SUBS, :]
 
     for j in range(elements // LANES):
         cols = slice(j * LANES, (j + 1) * LANES)
         for face in range(2):
-            columns = nb_ref[face : face + 1, cols] - 6 * elements
-
-            def tile_of(tile, r):
-                side, t = divmod(tile, tiles)
-                rows, part = slice(r * SUBS, (r + 1) * SUBS), slice(t * LANES, (t + 1) * LANES)
-                a, b = first_ref[rows, part], second_ref[rows, part]
-                return jnp.where(odd, a, b) if side == 0 else jnp.where(odd, b, a)
-
-            found = lane_gather(tile_of, 2 * tiles, columns, face_dofs)
+            found = lane_gather(tile_of, 2 * tiles, nb_ref[face : face + 1, cols] - 6 * elements, face_dofs)
             open_face = jnp.broadcast_to(1.0 - bd_ref[face : face + 1, cols].astype(jnp.float32), (SUBS, LANES))
             for r in range(face_dofs // SUBS):
                 rows = slice(face * face_dofs + r * SUBS, face * face_dofs + (r + 1) * SUBS)
                 rim_ref[rows, cols] = 0.0 - found[r] * open_face
 
 
-def first_send(odd_ref, v_ref, fp_ref, send_ref, tr_ref, first_ref, second_ref):
+def first_send(v_hbm, fp_hbm, send_hbm, v_ref, end_ref, tr_ref, first_ref, second_ref, fp_ref, send_ref, sems):
     face_dofs = fp_ref.shape[0] // 6
     elements = v_ref.shape[1]
+    half = end_ref.shape[0]
+    pairs = ((v_hbm, v_ref), (fp_hbm, fp_ref), (send_hbm, send_ref), (v_hbm.at[pl.ds(half, half), :], end_ref))
+    copies = [pltpu.make_async_copy(a, b, sems.at[i]) for i, (a, b) in enumerate(pairs)]
+    for copy in copies:
+        copy.start()
+    for copy in copies[:3]:
+        copy.wait()
     weights = jnp.concatenate([face_rows(fp_ref, f, face_dofs) for f in range(2)], axis=0)
     tr_ref[...] = dot(weights, v_ref[...])
-    fill_outbound(tr_ref, send_ref, odd_ref[0] == 1, first_ref, second_ref, face_dofs, elements)
+    fill_outbound(tr_ref, send_ref, first_ref, second_ref, face_dofs, elements)
+    copies[3].wait()
 
 
 def local_part(v_ref, tr_ref, coef_ref, fp_ref, stiff_ref, liftt_ref, nb_ref, bd_ref, part_ref, jump_ref, traces):
@@ -108,30 +124,32 @@
     part_ref[...] = coef_ref[...] * dot(stiff_ref[...], v_ref[...]) + dot(liftt.T, jump_ref[...])
 
 
+def time_jump_of(v_ref, prev_ref):
+    return v_ref[: prev_ref.shape[0], :] - jnp.where(lax.axis_index("tm") > 0, prev_ref[...], 0.0)
+
+
 def finish_operator(part_ref, v_ref, prev_ref, liftt_ref, tlt_ref, rim, face_dofs):
-    half = prev_ref.shape[0]
-    time_jump = v_ref[:half, :] - prev_ref[...]
+    time_jump = time_jump_of(v_ref, prev_ref)
     liftt = jnp.concatenate([face_rows(liftt_ref, f, face_dofs) for f in range(2)] + [tlt_ref[...]], axis=0)
     values = jnp.concatenate([rim[...], time_jump], axis=0)
     return part_ref[...] + dot(liftt.T, values)
 
 
 def residual_step(
-    odd_ref, part_ref, jump_ref, v_ref, rhs_ref, prev_ref, first_in, second_in, coef_ref, inv_ref, fp_ref, liftt_ref, tlt_ref,
+    part_ref, v_ref, rhs_ref, prev_ref, first_in, second_in, coef_ref, inv_ref, fp_ref, liftt_ref, tlt_ref,
     nb_ref, bd_ref, send_ref, res_ref, rim_ref, dir_ref, end_ref, tr_ref, first_ref, second_ref,
 ):
     face_dofs = fp_ref.shape[0] // 6
     elements = v_ref.shape[1]
     half = prev_ref.shape[0]
-    odd = odd_ref[0] == 1
-    rim_terms(first_in, second_in, nb_ref, bd_ref, odd, rim_ref, face_dofs, elements)
+    rim_terms(first_in, second_in, nb_ref, bd_ref, rim_ref, face_dofs, elements)
     res_ref[...] = rhs_ref[...] - finish_operator(part_ref, v_ref, prev_ref, liftt_ref, tlt_ref, rim_ref, face_dofs)
     direction = dot(inv_ref[...], res_ref[...]) / coef_ref[...]
     dir_ref[...] = direction
     end_ref[...] = direction[half:, :]
     weights = jnp.concatenate([face_rows(fp_ref, f, face_dofs) for f in range(2)], axis=0)
     tr_ref[...] = dot(weights, direction)
-    fill_outbound(tr_ref, send_ref, odd, first_ref, second_ref, face_dofs, elements)
+    fill_outbound(tr_ref, send_ref, first_ref, second_ref, face_dofs, elements)
 
 
 def column_sum(x):
@@ -143,23 +161,21 @@
 
 
 def image_step(
-    odd_ref, part_ref, jump_ref, dir_ref, prev_ref, first_in, second_in, liftt_ref, tlt_ref, nb_ref, bd_ref,
+    part_ref, jump_ref, dir_ref, prev_ref, first_in, second_in, liftt_ref, tlt_ref, nb_ref, bd_ref,
     res_ref, jump0_ref, rim0_ref, v_ref, prev0_ref, coeff_ref, sums_ref, rim, image,
 ):
     face_dofs = first_in.shape[0]
     elements = dir_ref.shape[1]
-    half = prev_ref.shape[0]
     rim_rows = rim.shape[0]
-    odd = odd_ref[0] == 1
-    rim_terms(first_in, second_in, nb_ref, bd_ref, odd, rim, face_dofs, elements)
+    rim_terms(first_in, second_in, nb_ref, bd_ref, rim, face_dofs, elements)
     image[...] = finish_operator(part_ref, dir_ref, prev_ref, liftt_ref, tlt_ref, rim, face_dofs)
     res, img = res_ref[...], image[...]
     cross = column_sum(res * img)
     square = column_sum(img * img)
     j0 = jnp.concatenate([jump0_ref[:rim_rows, :] + rim0_ref[...], jump0_ref[rim_rows:, :]], axis=0)
     j1 = jnp.concatenate([jump_ref[:rim_rows, :] + rim[...], jump_ref[rim_rows:, :]], axis=0)
-    t0 = v_ref[:half, :] - prev0_ref[...]
-    t1 = dir_ref[:half, :] - prev_ref[...]
+    t0 = time_jump_of(v_ref, prev0_ref)
+    t1 = time_jump_of(dir_ref, prev_ref)
     bend = square + 0.5 * column_sum(j1 * j1) + column_sum(t1 * t1)
     slope = 0.5 * column_sum(j0 * j1) + column_sum(t0 * t1) - cross
     best = jnp.where(bend > 0.0, -slope / jnp.where(bend > 0.0, bend, 1.0), 0.0)
@@ -195,51 +211,64 @@
 
 
 VM = pl.BlockSpec(memory_space=pltpu.VMEM)
-SM = pl.BlockSpec(memory_space=pltpu.SMEM)
-
-
-def call(body, name, outs, args, flops, scratch=(), scalars=0):
+HB = pl.BlockSpec(memory_space=pltpu.HBM)
+
+
+def call(body, name, outs, args, flops, scratch=(), spec=VM):
     shapes = [jax.ShapeDtypeStruct(s, jnp.float32) for s in outs]
     moved = sum(4 * a.size for a in args) + sum(4 * s.size for s in shapes)
     return pl.pallas_call(
         body,
         name=name,
         out_shape=shapes,
-        in_specs=[SM] * scalars + [VM] * (len(args) - scalars),
+        in_specs=[spec] * len(args),
         out_specs=[VM] * len(outs),
-        scratch_shapes=[pltpu.VMEM(s, jnp.float32) for s in scratch],
+        scratch_shapes=[pltpu.VMEM(s, jnp.float32) if isinstance(s, tuple) else s for s in scratch],
         cost_estimate=pl.CostEstimate(flops=flops, bytes_accessed=moved, transcendentals=0),
         compiler_params=pltpu.CompilerParams(vmem_limit_bytes=20 * 2**20),
     )(*args)
 
 
+def full_swaps(first, slabs, parts):
+    other = {i: i + 1 for i in range(first, parts - 1, 2)}
+    other.update({j: i for i, j in list(other.items())})
+    pairs = []
+    for t in range(slabs):
+        beside = t ^ 1 if slabs % 2 == 0 else (t + 1) % slabs
+        for p in range(parts):
+            pairs.append((t * parts + p, t * parts + other[p] if p in other else beside * parts + p))
+    return pairs
+
+
 def on_device(initial, rhs, coef, stiffness, block_inverse, face_proj, lift, time_lift, neighbour, boundary, send_list):
-    v0, source = initial[0], rhs[0]
-    dofs, elements = v0.shape
+    source = rhs[0]
+    dofs, elements = source.shape
     half = time_lift.shape[1]
     traces = face_proj.shape[0]
     face_dofs = traces // 6
     border = send_list.shape[0] // 2
     slabs, parts = lax.axis_size("tm"), lax.axis_size("space")
     devices = slabs * parts
-    odd = (lax.axis_index("space") % 2).astype(jnp.int32).reshape(1)
     coef_row = coef.reshape(1, elements)
     send = send_list.reshape(2, border)
     liftt, tlt = lift.T, time_lift.T
-    later = [(i, i + 1) for i in range(slabs - 1)]
-
-    def swaps(first):
-        pairs = [(i, i + 1) for i in range(first, parts - 1, 2)]
-        return pairs + [(j, i) for i, j in pairs]
+    cycle = [(i, (i + 1) % slabs) for i in range(slabs)]
 
     def halo(a, b):
-        return lax.ppermute(a, "space", swaps(0)), lax.ppermute(b, "space", swaps(1))
+        swap = lambda x, first: lax.ppermute(x, ("tm", "space"), full_swaps(first, slabs, parts))
+        return swap(a, 0), swap(b, 1)
 
     two = 2 * face_dofs
-    prev0 = lax.ppermute(v0[half:], "tm", later)
-    tr0, a0, b0 = call(
-        first_send, "send0", [(two, elements), (face_dofs, border), (face_dofs, border)], (odd, v0, face_proj, send), 2 * two * dofs * elements, scalars=1
-    )
+    v0, end0, tr0, a0, b0 = call(
+        first_send,
+        "send0",
+        [(dofs, elements), (half, elements), (two, elements), (face_dofs, border), (face_dofs, border)],
+        (initial[0], face_proj, send),
+        2 * two * dofs * elements,
+        scratch=[(traces, dofs), pltpu.VMEM(send.shape, send.dtype), pltpu.SemaphoreType.DMA((4,))],
+        spec=HB,
+    )
+    prev0 = lax.ppermute(end0, "tm", cycle)
     a0, b0 = halo(a0, b0)
     local = functools.partial(
         call, local_part, "local", [(dofs, elements), (traces, elements)], flops=12 * traces * dofs * elements, scratch=[(traces, elements)]
@@ -249,21 +278,19 @@
         residual_step,
         "residual",
         [(dofs, elements), (two, elements), (dofs, elements), (half, elements), (two, elements), (face_dofs, border), (face_dofs, border)],
-        (odd, part0, jump0, v0, source, prev0, a0, b0, coef_row, block_inverse, face_proj, liftt, tlt, neighbour, boundary, send),
+        (part0, v0, source, prev0, a0, b0, coef_row, block_inverse, face_proj, liftt, tlt, neighbour, boundary, send),
         12 * dofs * dofs * elements,
-        scalars=1,
-    )
-    prev1 = lax.ppermute(end, "tm", later)
+    )
+    prev1 = lax.ppermute(end, "tm", cycle)
     a1, b1 = halo(a1, b1)
     part1, jump1 = local(args=(direction, tr1, coef_row, face_proj, stiffness, liftt, neighbour, boundary))
     coeffs, sums = call(
         image_step,
         "image",
         [(SUBS, elements), (devices, LANES)],
-        (odd, part1, jump1, direction, prev1, a1, b1, liftt, tlt, neighbour, boundary, res, jump0, rim0, v0, prev0),
+        (part1, jump1, direction, prev1, a1, b1, liftt, tlt, neighbour, boundary, res, jump0, rim0, v0, prev0),
         12 * dofs * dofs * elements,
         scratch=[(two, elements), (dofs, elements)],
-        scalars=1,
     )
     everyone = lax.all_to_all(sums, ("tm", "space"), 0, 0, tiled=True)
     smoothed, indicator, estimate = call(

time: 40.5 us -> 34.2 us (0.84)
  starting transfers between devices: 13.6 us -> 7.54 us
    ppermute x6, starting transfers between devices: 13.6 us -> 7.54 us  [the longest x4 6.31 us: halo(): lax.ppermute(x, ('tm', 'space'), full_swaps(first, slabs, parts))]
    unnamed x24 -> x22, local copies, waits for them, and re-layouts: 1.61 us -> 2.64 us
    slice x1 -> x0, local copies, waits for them, and re-layouts: 1.03 us -> none  [on_device(): prev0 = lax.ppermute(v0[half:], 'tm', later)]
  transfers between devices with their start and end apart: 6 -> 6, of which waited for: 0 -> 0; matrix products, arithmetic and copies ran while one was open for 0% -> 0% of each run, Pallas kernels for 15% -> 16%
where the time goes in v3:
time: 34.2 us; the launch traced here: 33.9 us
  blocking collectives  12.8 us (37%)
  Pallas kernels  10.1 us (30%)
  starting transfers between devices  7.54 us (22%)
  local copies, waits for them, and re-layouts  2.64 us (8%)
  between operations  0.79 us (2%)
    all_to_all x1, blocking collectives, on_device(): everyone = lax.all_to_all(sums, ('tm', 'space'), 0, 0, tiled=True)  12.8 us
    pallas_call x6, Pallas kernels, call(): pl.pallas_call(body, name=name, out_shape=shapes, in_specs=[spec] * len(a...  10.1 us
    ppermute x4, starting transfers between devices, halo(): lax.ppermute(x, ('tm', 'space'), full_swaps(first, slabs, parts))  6.31 us
    unnamed x22, local copies, waits for them, and re-layouts  2.64 us
  transfers between devices with their start and end apart: 6, of which 0 were waited for; matrix products, arithmetic and copies ran while one was open for 0% of the time, Pallas kernels for 16%

profile of v3, /device:TPU:0, one launch (start us, length us, event | category | flops | bytes accessed | tf_op | source)
XLA Modules:
  0.0 33.9 jit_solution(5360207629181868223)
XLA Ops:
  0.6 0.0 copy-start.10
  0.6 0.7 %copy-done.10 = s32[256]{0:T(256)S(1)} copy-done((s32[256]{0:T(256)S(1)}, s32[256]{0:T(256)}, u32[]{:S(2)}) %copy-start.10) | copy-done | bytes 1048
  1.3 0.0 copy-start
  1.3 0.9 %copy-done = f32[192,128]{1,0:T(8,128)S(1)} copy-done((f32[192,128]{1,0:T(8,128)S(1)}, f32[192,128]{1,0:T(8,128)}, u32[]{:S(2)}) %copy-start) | copy-done | bytes 98328
  2.2 0.0 copy-start.4
  2.2 1.0 %copy-done.4 = f32[1,128,1024]{2,1,0:T(8,128)S(1)} copy-done((f32[1,128,1024]{2,1,0:T(8,128)S(1)}, f32[1,128,1024]{2,1,0:T(8,128)}, u32[]{:S(2)}) %copy-start.4) | copy-done | bytes 524312
  3.2 0.0 copy-start.1
  3.2 0.0 copy-start.2
  3.3 0.0 copy-start.3
  3.3 0.0 copy-start.6
  3.3 0.7 %send0.1 = (f32[128,1024]{1,0:T(8,128)S(1)}, f32[64,1024]{1,0:T(8,128)S(1)}, f32[64,1024]{1,0:T(8,128)S(1)}, f32[32,128]{1,0:T(8,128)S(1)}, f32[32,128]{1,0:T(8,128)S(1)}) custom-call(f32[128,1024]{1,0:T(8,128)S(1)} %bitcast.17, f32[192,128]{1,0:T(8,128)S(1)} %copy-done, s32[2,128]{1,0:T(2,128)S(1)} %bitcast.26), custom_call_target="tpu_custom_call" | custom-call | flops 16777216 | bytes 1704960 | tf_op jit(solution)/shard_map/send0/pallas_call | solution.py:220
  4.0 0.5 %collective-permute-start = (f32[64,1024]{1,0:T(8,128)S(1)}, f32[64,1024]{1,0:T(8,128)S(1)}, u32[]{:S(2)}, u32[]{:S(2)}) collective-permute-start(f32[64,1024]{1,0:T(8,128)S(1)} %get-tuple-element.27), channel_id=1, source_target_pairs={{0,8},{8,16},{16,24},{24,0},{1,9},{9,17},{17,25},{25,1},{2,10},{10... | collective-permute-start | bytes 786440 | tf_op jit(solution)/shard_map/ppermute | solution.py:271
  4.5 2.6 %collective-permute-start.1 = (f32[32,128]{1,0:T(8,128)S(1)}, f32[32,128]{1,0:T(8,128)S(1)}, u32[]{:S(2)}, u32[]{:S(2)}) collective-permute-start(f32[32,128]{1,0:T(8,128)S(1)} %get-tuple-element.28), channel_id=1, source_target_pairs={{0,1},{1,0},{2,3},{3,2},{4,5},{5,4},{6,7},{7,6},{8,9},{9,8},{10,11... | collective-permute-start | bytes 49160 | tf_op jit(solution)/shard_map/ppermute | solution.py:258
  7.1 0.0 copy-start.9
  7.1 1.3 %collective-permute-start.2 = (f32[32,128]{1,0:T(8,128)S(1)}, f32[32,128]{1,0:T(8,128)S(1)}, u32[]{:S(2)}, u32[]{:S(2)}) collective-permute-start(f32[32,128]{1,0:T(8,128)S(1)} %get-tuple-element.29), channel_id=1, source_target_pairs={{0,8},{1,2},{2,1},{3,4},{4,3},{5,6},{6,5},{7,15},{8,0},{9,10},{10,... | collective-permute-start | bytes 49160 | tf_op jit(solution)/shard_map/ppermute | solution.py:258
  8.4 0.0 copy-done.1
  8.4 0.0 copy-done.2
  8.4 0.0 copy-done.3
  8.4 0.0 copy-done.6
  8.4 0.0 copy-done.9
  8.4 0.0 copy-start.5
  8.4 0.0 copy-start.7
  8.4 0.0 copy-start.8
  8.4 2.7 %local.2 = (f32[128,1024]{1,0:T(8,128)S(1)}, f32[192,1024]{1,0:T(8,128)S(1)}) custom-call(f32[128,1024]{1,0:T(8,128)S(1)} %get-tuple-element.24.v_ref, f32[64,1024]{1,0:T(8,128)S(1)} %get-tuple-element.25.tr_ref, f32[1,1024]{1,0:T(1,128)S(1)} %bitcast.22, f32[192,128]{1,0:T(8,128)S(1)} %copy-done, f32[128,128]{1,0:T(8,128)S(1)} %copy-done.6, ...), custom_call_target="tpu_custom_call" | custom-call | flops 301989888 | bytes 2412544 | tf_op jit(solution)/shard_map/local/pallas_call | solution.py:220
  11.2 0.0 collective-permute-done.1.first_in
  11.2 0.0 collective-permute-done.2.second_in
  11.2 0.0 collective-permute-done.prev_ref.prev0_ref
  11.2 0.0 copy-done.5
  11.2 0.0 copy-done.7
  11.2 0.0 copy-done.8
  11.2 1.6 %residual.1 = (f32[128,1024]{1,0:T(8,128)S(1)}, f32[64,1024]{1,0:T(8,128)S(1)}, f32[128,1024]{1,0:T(8,128)S(1)}, f32[64,1024]{1,0:T(8,128)S(1)}, f32[64,1024]{1,...) custom-call(f32[128,1024]{1,0:T(8,128)S(1)} %get-tuple-element.26.part_ref, ...), custom_call_target="tpu_custom_call" | custom-call | flops 201326592 | bytes 4084736 | tf_op jit(solution)/shard_map/residual/pallas_call | solution.py:220
  12.8 0.7 %collective-permute-start.3 = (f32[64,1024]{1,0:T(8,128)S(1)}, f32[64,1024]{1,0:T(8,128)S(1)}, u32[]{:S(2)}, u32[]{:S(2)}) collective-permute-start(f32[64,1024]{1,0:T(8,128)S(1)} %get-tuple-element.34), channel_id=1, source_target_pairs={{0,8},{8,16},{16,24},{24,0},{1,9},{9,17},{17,25},{25,1},{2,10},{10... | collective-permute-start | bytes 786440 | tf_op jit(solution)/shard_map/ppermute | solution.py:284
  13.5 2.1 %collective-permute-start.4 = (f32[32,128]{1,0:T(8,128)S(1)}, f32[32,128]{1,0:T(8,128)S(1)}, u32[]{:S(2)}, u32[]{:S(2)}) collective-permute-start(f32[32,128]{1,0:T(8,128)S(1)} %get-tuple-element.35), channel_id=1, source_target_pairs={{0,1},{1,0},{2,3},{3,2},{4,5},{5,4},{6,7},{7,6},{8,9},{9,8},{10,11... | collective-permute-start | bytes 49160 | tf_op jit(solution)/shard_map/ppermute | solution.py:258
  15.7 0.4 %collective-permute-start.5 = (f32[32,128]{1,0:T(8,128)S(1)}, f32[32,128]{1,0:T(8,128)S(1)}, u32[]{:S(2)}, u32[]{:S(2)}) collective-permute-start(f32[32,128]{1,0:T(8,128)S(1)} %get-tuple-element.36), channel_id=1, source_target_pairs={{0,8},{1,2},{2,1},{3,4},{4,3},{5,6},{6,5},{7,15},{8,0},{9,10},{10,... | collective-permute-start | bytes 49160 | tf_op jit(solution)/shard_map/ppermute | solution.py:258
  16.0 2.7 %local.3 = (f32[128,1024]{1,0:T(8,128)S(1)}, f32[192,1024]{1,0:T(8,128)S(1)}) custom-call(f32[128,1024]{1,0:T(8,128)S(1)} %get-tuple-element.30.v_ref.dir_ref, f32[64,1024]{1,0:T(8,128)S(1)} %get-tuple-element.31.tr_ref, f32[1,1024]{1,0:T(1,128)S(1)} %bitcast.24, f32[192,128]{1,0:T(8,128)S(1)} %copy-done, f32[128,128]{1,0:T(8,128)S(1)} %copy-done.6, ...), custom_call_target="tpu_custom_call" | custom-call | flops 301989888 | bytes 2412544 | tf_op jit(solution)/shard_map/local/pallas_call | solution.py:220
  18.8 0.0 collective-permute-done.4.first_in
  18.8 0.0 collective-permute-done.5.second_in
  18.8 0.0 collective-permute-done.3.prev_ref
  18.8 1.3 %image.1 = (f32[8,1024]{1,0:T(8,128)S(1)}, f32[32,128]{1,0:T(8,128)S(1)}) custom-call(f32[128,1024]{1,0:T(8,128)S(1)} %get-tuple-element.32.part_ref, f32[192,1024]{1,0:T(8,128)S(1)} %get-tuple-element.33.jump_ref, f32[128,1024]{1,0:T(8,128)S(1)} %get-tuple-element.30.v_ref.dir_ref, f32[64,1024]{1,0:T(8,128)S(1)} %collective-permute-done.3.prev_ref, ...), custom_call_target="tpu_custom_call" | custom-call | flops 201326592 | bytes 4718592 | tf_op jit(solution)/shard_map/image/pallas_call | solution.py:220
  20.1 12.8 %all_to_all.11 = f32[32,1,128]{2,1,0:T(1,128)S(1)} all-to-all(f32[32,1,128]{2,1,0:T(1,128)S(1)} %bitcast.25), channel_id=1, replica_groups=mesh['tm'=4,'space'=8] {'tm','space'}, dimensions={0} | all-to-all | bytes 32768 | tf_op jit(solution)/shard_map/all_to_all | solution.py:295
  32.9 1.0 %last.1 = (f32[128,1024]{1,0:T(8,128)}, f32[1,1024]{1,0:T(1,128)}, f32[1,128]{1,0:T(1,128)}) custom-call(f32[32,128]{1,0:T(8,128)S(1)} %bitcast.21, f32[8,1024]{1,0:T(8,128)S(1)} %get-tuple-element.41.coeff_ref, f32[128,1024]{1,0:T(8,128)S(1)} %get-tuple-element.24.v_ref, f32[128,1024]{1,0:T(8,128)S(1)} %get-tuple-element.30.v_ref.dir_ref), custom_call_target="tpu_custom_call" | custom-call | flops 524288 | bytes 1626624 | tf_op jit(solution)/shard_map/last/pallas_call | solution.py:220
Async XLA Ops:
  0.6 0.7 %copy-start.10 = (s32[256]{0:T(256)S(1)}, s32[256]{0:T(256)}, u32[]{:S(2)}) copy-start(s32[256]{0:T(256)} %param.21) | copy-start | bytes 3076
  1.3 0.9 %copy-start = (f32[192,128]{1,0:T(8,128)S(1)}, f32[192,128]{1,0:T(8,128)}, u32[]{:S(2)}) copy-start(f32[192,128]{1,0:T(8,128)} %fp_ref.5) | copy-start | bytes 294916
  2.2 1.0 %copy-start.4 = (f32[1,128,1024]{2,1,0:T(8,128)S(1)}, f32[1,128,1024]{2,1,0:T(8,128)}, u32[]{:S(2)}) copy-start(f32[1,128,1024]{2,1,0:T(8,128)} %param.11) | copy-start | bytes 1572868
  3.2 5.1 %copy-start.1 = (f32[128,192]{0,1:T(8,128)S(1)}, f32[128,192]{0,1:T(8,128)}, u32[]{:S(2)}) copy-start(f32[128,192]{0,1:T(8,128)} %param.17) | copy-start | bytes 294916
  3.2 5.1 %copy-start.2 = (s32[6,1024]{1,0:T(8,128)S(1)}, s32[6,1024]{1,0:T(8,128)}, u32[]{:S(2)}) copy-start(s32[6,1024]{1,0:T(8,128)} %nb_ref.7) | copy-start | bytes 73732
  3.3 5.1 %copy-start.3 = (s32[6,1024]{1,0:T(8,128)S(1)}, s32[6,1024]{1,0:T(8,128)}, u32[]{:S(2)}) copy-start(s32[6,1024]{1,0:T(8,128)} %bd_ref.7) | copy-start | bytes 73732
  3.3 5.1 %copy-start.6 = (f32[128,128]{1,0:T(8,128)S(1)}, f32[128,128]{1,0:T(8,128)}, u32[]{:S(2)}) copy-start(f32[128,128]{1,0:T(8,128)} %stiff_ref.3) | copy-start | bytes 196612
  4.0 7.2 %collective-permute-start = (f32[64,1024]{1,0:T(8,128)S(1)}, f32[64,1024]{1,0:T(8,128)S(1)}, u32[]{:S(2)}, u32[]{:S(2)}) collective-permute-start(f32[64,1024]{1,0:T(8,128)S(1)} %get-tuple-element.27), channel_id=1, source_target_pairs={{0,8},{8,16},{16,24},{24,0},{1,9},{9,17},{17,25},{25,1},{2,10},{10... | collective-permute-start | bytes 786440 | tf_op jit(solution)/shard_map/ppermute | solution.py:271
  4.5 6.6 %collective-permute-start.1 = (f32[32,128]{1,0:T(8,128)S(1)}, f32[32,128]{1,0:T(8,128)S(1)}, u32[]{:S(2)}, u32[]{:S(2)}) collective-permute-start(f32[32,128]{1,0:T(8,128)S(1)} %get-tuple-element.28), channel_id=1, source_target_pairs={{0,1},{1,0},{2,3},{3,2},{4,5},{5,4},{6,7},{7,6},{8,9},{9,8},{10,11... | collective-permute-start | bytes 49160 | tf_op jit(solution)/shard_map/ppermute | solution.py:258
  7.1 1.3 %copy-start.9 = (f32[1024]{0:T(1024)S(1)}, f32[1024]{0:T(1024)}, u32[]{:S(2)}) copy-start(f32[1024]{0:T(1024)} %param.13) | copy-start | bytes 12292
  7.1 4.1 %collective-permute-start.2 = (f32[32,128]{1,0:T(8,128)S(1)}, f32[32,128]{1,0:T(8,128)S(1)}, u32[]{:S(2)}, u32[]{:S(2)}) collective-permute-start(f32[32,128]{1,0:T(8,128)S(1)} %get-tuple-element.29), channel_id=1, source_target_pairs={{0,8},{1,2},{2,1},{3,4},{4,3},{5,6},{6,5},{7,15},{8,0},{9,10},{10,... | collective-permute-start | bytes 49160 | tf_op jit(solution)/shard_map/ppermute | solution.py:258
  8.4 2.8 %copy-start.5 = (f32[1,128,1024]{2,1,0:T(8,128)S(1)}, f32[1,128,1024]{2,1,0:T(8,128)}, u32[]{:S(2)}) copy-start(f32[1,128,1024]{2,1,0:T(8,128)} %param.12) | copy-start | bytes 1572868
  8.4 2.8 %copy-start.7 = (f32[128,64]{0,1:T(8,128)S(1)}, f32[128,64]{0,1:T(8,128)}, u32[]{:S(2)}) copy-start(f32[128,64]{0,1:T(8,128)} %param.18) | copy-start | bytes 98308
  8.4 2.8 %copy-start.8 = (f32[128,128]{1,0:T(8,128)S(1)}, f32[128,128]{1,0:T(8,128)}, u32[]{:S(2)}) copy-start(f32[128,128]{1,0:T(8,128)} %inv_ref.1) | copy-start | bytes 196612
  12.8 5.9 %collective-permute-start.3 = (f32[64,1024]{1,0:T(8,128)S(1)}, f32[64,1024]{1,0:T(8,128)S(1)}, u32[]{:S(2)}, u32[]{:S(2)}) collective-permute-start(f32[64,1024]{1,0:T(8,128)S(1)} %get-tuple-element.34), channel_id=1, source_target_pairs={{0,8},{8,16},{16,24},{24,0},{1,9},{9,17},{17,25},{25,1},{2,10},{10... | collective-permute-start | bytes 786440 | tf_op jit(solution)/shard_map/ppermute | solution.py:284
  13.5 5.2 %collective-permute-start.4 = (f32[32,128]{1,0:T(8,128)S(1)}, f32[32,128]{1,0:T(8,128)S(1)}, u32[]{:S(2)}, u32[]{:S(2)}) collective-permute-start(f32[32,128]{1,0:T(8,128)S(1)} %get-tuple-element.35), channel_id=1, source_target_pairs={{0,1},{1,0},{2,3},{3,2},{4,5},{5,4},{6,7},{7,6},{8,9},{9,8},{10,11... | collective-permute-start | bytes 49160 | tf_op jit(solution)/shard_map/ppermute | solution.py:258
  15.7 3.1 %collective-permute-start.5 = (f32[32,128]{1,0:T(8,128)S(1)}, f32[32,128]{1,0:T(8,128)S(1)}, u32[]{:S(2)}, u32[]{:S(2)}) collective-permute-start(f32[32,128]{1,0:T(8,128)S(1)} %get-tuple-element.36), channel_id=1, source_target_pairs={{0,8},{1,2},{2,1},{3,4},{4,3},{5,6},{6,5},{7,15},{8,0},{9,10},{10,... | collective-permute-start | bytes 49160 | tf_op jit(solution)/shard_map/ppermute | solution.py:258

commit v4 on v3

--- a/solution.py
+++ b/solution.py
@@ -263,7 +263,7 @@
         first_send,
         "send0",
         [(dofs, elements), (half, elements), (two, elements), (face_dofs, border), (face_dofs, border)],
-        (initial[0], face_proj, send),
+        tuple(pltpu.with_memory_space_constraint(x, pltpu.HBM) for x in (initial[0], face_proj, send)),
         2 * two * dofs * elements,
         scratch=[(traces, dofs), pltpu.VMEM(send.shape, send.dtype), pltpu.SemaphoreType.DMA((4,))],
         spec=HB,

time: 34.2 us -> 33.1 us (0.968)
  local copies, waits for them, and re-layouts: 2.64 us -> 0.69 us
  Pallas kernels: 10.1 us -> 11.1 us
    unnamed x22 -> x20, local copies, waits for them, and re-layouts: 2.64 us -> 0.69 us
    pallas_call x6, Pallas kernels: 10.1 us -> 11.1 us  [call(): pl.pallas_call(body, name=name, out_shape=shapes, in_specs=[spec] * len(a...]
  transfers between devices with their start and end apart: 6 -> 6, of which waited for: 0 -> 0; matrix products, arithmetic and copies ran while one was open for 0% -> 0% of each run, Pallas kernels for 16% -> 17%
where the time goes in v4:
time: 33.1 us; the launch traced here: 33 us
  blocking collectives  12.8 us (39%)
  Pallas kernels  11.1 us (34%)
  starting transfers between devices  7.54 us (23%)
  between operations  0.83 us (3%)
  local copies, waits for them, and re-layouts  0.69 us (2%)
    all_to_all x1, blocking collectives, on_device(): everyone = lax.all_to_all(sums, ('tm', 'space'), 0, 0, tiled=True)  12.8 us
    pallas_call x6, Pallas kernels, call(): pl.pallas_call(body, name=name, out_shape=shapes, in_specs=[spec] * len(a...  11.1 us
    ppermute x4, starting transfers between devices, halo(): lax.ppermute(x, ('tm', 'space'), full_swaps(first, slabs, parts))  6.32 us
    unnamed x20, local copies, waits for them, and re-layouts  0.69 us
    ppermute x1, starting transfers between devices, on_device(): prev1 = lax.ppermute(end, 'tm', cycle)  0.67 us
  transfers between devices with their start and end apart: 6, of which 0 were waited for; matrix products, arithmetic and copies ran while one was open for 0% of the time, Pallas kernels for 17%

profile of v4, /device:TPU:0, one launch (start us, length us, event | category | flops | bytes accessed | tf_op | source)
XLA Modules:
  0.0 33.0 jit_solution(1015523594757550688)
XLA Ops:
  0.6 0.0 copy-start
  0.6 0.0 copy-start.1
  0.7 0.0 copy-start.2
  0.7 0.0 copy-start.3
  0.7 0.0 copy-start.5
  0.7 1.7 %send0.1 = (f32[128,1024]{1,0:T(8,128)S(1)}, f32[64,1024]{1,0:T(8,128)S(1)}, f32[64,1024]{1,0:T(8,128)S(1)}, f32[32,128]{1,0:T(8,128)S(1)}, f32[32,128]{1,0:T(8,128)S(1)}) custom-call(f32[128,1024]{1,0:T(8,128)} %bitcast.27, f32[192,128]{1,0:T(8,128)} %fp_ref.5, s32[2,128]{1,0:T(2,128)} %bitcast.25), custom_call_target="tpu_custom_call" | custom-call | flops 16777216 | bytes 1704960 | tf_op jit(solution)/shard_map/send0/pallas_call | solution.py:220
  2.4 0.5 %collective-permute-start = (f32[64,1024]{1,0:T(8,128)S(1)}, f32[64,1024]{1,0:T(8,128)S(1)}, u32[]{:S(2)}, u32[]{:S(2)}) collective-permute-start(f32[64,1024]{1,0:T(8,128)S(1)} %get-tuple-element.27), channel_id=1, source_target_pairs={{0,8},{8,16},{16,24},{24,0},{1,9},{9,17},{17,25},{25,1},{2,10},{10... | collective-permute-start | bytes 786440 | tf_op jit(solution)/shard_map/ppermute | solution.py:271
  2.9 2.6 %collective-permute-start.1 = (f32[32,128]{1,0:T(8,128)S(1)}, f32[32,128]{1,0:T(8,128)S(1)}, u32[]{:S(2)}, u32[]{:S(2)}) collective-permute-start(f32[32,128]{1,0:T(8,128)S(1)} %get-tuple-element.28), channel_id=1, source_target_pairs={{0,1},{1,0},{2,3},{3,2},{4,5},{5,4},{6,7},{7,6},{8,9},{9,8},{10,11... | collective-permute-start | bytes 49160 | tf_op jit(solution)/shard_map/ppermute | solution.py:258
  5.5 0.0 copy-start.8
  5.5 1.3 %collective-permute-start.2 = (f32[32,128]{1,0:T(8,128)S(1)}, f32[32,128]{1,0:T(8,128)S(1)}, u32[]{:S(2)}, u32[]{:S(2)}) collective-permute-start(f32[32,128]{1,0:T(8,128)S(1)} %get-tuple-element.29), channel_id=1, source_target_pairs={{0,8},{1,2},{2,1},{3,4},{4,3},{5,6},{6,5},{7,15},{8,0},{9,10},{10,... | collective-permute-start | bytes 49160 | tf_op jit(solution)/shard_map/ppermute | solution.py:258
  6.7 0.0 copy-done
  6.7 0.0 copy-done.1
  6.7 0.0 copy-done.2
  6.7 0.0 copy-done.3
  6.8 0.0 copy-done.5
  6.8 0.0 copy-done.8
  6.8 0.0 copy-start.4
  6.8 0.0 copy-start.6
  6.8 0.0 copy-start.7
  6.8 2.7 %local.2 = (f32[128,1024]{1,0:T(8,128)S(1)}, f32[192,1024]{1,0:T(8,128)S(1)}) custom-call(f32[128,1024]{1,0:T(8,128)S(1)} %get-tuple-element.24.v_ref, f32[64,1024]{1,0:T(8,128)S(1)} %get-tuple-element.25.tr_ref, f32[1,1024]{1,0:T(1,128)S(1)} %bitcast.21, f32[192,128]{1,0:T(8,128)S(1)} %copy-done, f32[128,128]{1,0:T(8,128)S(1)} %copy-done.5, ...), custom_call_target="tpu_custom_call" | custom-call | flops 301989888 | bytes 2412544 | tf_op jit(solution)/shard_map/local/pallas_call | solution.py:220
  9.6 0.0 collective-permute-done.1.first_in
  9.6 0.0 collective-permute-done.2.second_in
  9.6 0.0 collective-permute-done.prev_ref.prev0_ref
  9.6 0.0 copy-start.9
  9.6 0.0 copy-done.4
  9.6 0.0 copy-done.6
  9.6 0.0 copy-done.7
  9.6 0.6 %copy-done.9 = s32[256]{0:T(256)S(1)} copy-done((s32[256]{0:T(256)S(1)}, s32[256]{0:T(256)}, u32[]{:S(2)}) %copy-start.9) | copy-done | bytes 1048
  10.3 1.6 %residual.1 = (f32[128,1024]{1,0:T(8,128)S(1)}, f32[64,1024]{1,0:T(8,128)S(1)}, f32[128,1024]{1,0:T(8,128)S(1)}, f32[64,1024]{1,0:T(8,128)S(1)}, f32[64,1024]{1,...) custom-call(f32[128,1024]{1,0:T(8,128)S(1)} %get-tuple-element.26.part_ref, ...), custom_call_target="tpu_custom_call" | custom-call | flops 201326592 | bytes 4084736 | tf_op jit(solution)/shard_map/residual/pallas_call | solution.py:220
  11.9 0.7 %collective-permute-start.3 = (f32[64,1024]{1,0:T(8,128)S(1)}, f32[64,1024]{1,0:T(8,128)S(1)}, u32[]{:S(2)}, u32[]{:S(2)}) collective-permute-start(f32[64,1024]{1,0:T(8,128)S(1)} %get-tuple-element.34), channel_id=1, source_target_pairs={{0,8},{8,16},{16,24},{24,0},{1,9},{9,17},{17,25},{25,1},{2,10},{10... | collective-permute-start | bytes 786440 | tf_op jit(solution)/shard_map/ppermute | solution.py:284
  12.5 2.1 %collective-permute-start.4 = (f32[32,128]{1,0:T(8,128)S(1)}, f32[32,128]{1,0:T(8,128)S(1)}, u32[]{:S(2)}, u32[]{:S(2)}) collective-permute-start(f32[32,128]{1,0:T(8,128)S(1)} %get-tuple-element.35), channel_id=1, source_target_pairs={{0,1},{1,0},{2,3},{3,2},{4,5},{5,4},{6,7},{7,6},{8,9},{9,8},{10,11... | collective-permute-start | bytes 49160 | tf_op jit(solution)/shard_map/ppermute | solution.py:258
  14.7 0.3 %collective-permute-start.5 = (f32[32,128]{1,0:T(8,128)S(1)}, f32[32,128]{1,0:T(8,128)S(1)}, u32[]{:S(2)}, u32[]{:S(2)}) collective-permute-start(f32[32,128]{1,0:T(8,128)S(1)} %get-tuple-element.36), channel_id=1, source_target_pairs={{0,8},{1,2},{2,1},{3,4},{4,3},{5,6},{6,5},{7,15},{8,0},{9,10},{10,... | collective-permute-start | bytes 49160 | tf_op jit(solution)/shard_map/ppermute | solution.py:258
  15.0 2.7 %local.3 = (f32[128,1024]{1,0:T(8,128)S(1)}, f32[192,1024]{1,0:T(8,128)S(1)}) custom-call(f32[128,1024]{1,0:T(8,128)S(1)} %get-tuple-element.30.v_ref.dir_ref, f32[64,1024]{1,0:T(8,128)S(1)} %get-tuple-element.31.tr_ref, f32[1,1024]{1,0:T(1,128)S(1)} %bitcast.23, f32[192,128]{1,0:T(8,128)S(1)} %copy-done, f32[128,128]{1,0:T(8,128)S(1)} %copy-done.5, ...), custom_call_target="tpu_custom_call" | custom-call | flops 301989888 | bytes 2412544 | tf_op jit(solution)/shard_map/local/pallas_call | solution.py:220
  17.8 0.0 collective-permute-done.4.first_in
  17.8 0.0 collective-permute-done.5.second_in
  17.8 0.0 collective-permute-done.3.prev_ref
  17.8 1.3 %image.1 = (f32[8,1024]{1,0:T(8,128)S(1)}, f32[32,128]{1,0:T(8,128)S(1)}) custom-call(f32[128,1024]{1,0:T(8,128)S(1)} %get-tuple-element.32.part_ref, f32[192,1024]{1,0:T(8,128)S(1)} %get-tuple-element.33.jump_ref, f32[128,1024]{1,0:T(8,128)S(1)} %get-tuple-element.30.v_ref.dir_ref, f32[64,1024]{1,0:T(8,128)S(1)} %collective-permute-done.3.prev_ref, ...), custom_call_target="tpu_custom_call" | custom-call | flops 201326592 | bytes 4718592 | tf_op jit(solution)/shard_map/image/pallas_call | solution.py:220
  19.1 12.8 %all_to_all.11 = f32[32,1,128]{2,1,0:T(1,128)S(1)} all-to-all(f32[32,1,128]{2,1,0:T(1,128)S(1)} %bitcast.24), channel_id=1, replica_groups=mesh['tm'=4,'space'=8] {'tm','space'}, dimensions={0} | all-to-all | bytes 32768 | tf_op jit(solution)/shard_map/all_to_all | solution.py:295
  32.0 1.0 %last.1 = (f32[128,1024]{1,0:T(8,128)}, f32[1,1024]{1,0:T(1,128)}, f32[1,128]{1,0:T(1,128)}) custom-call(f32[32,128]{1,0:T(8,128)S(1)} %bitcast.20, f32[8,1024]{1,0:T(8,128)S(1)} %get-tuple-element.41.coeff_ref, f32[128,1024]{1,0:T(8,128)S(1)} %get-tuple-element.24.v_ref, f32[128,1024]{1,0:T(8,128)S(1)} %get-tuple-element.30.v_ref.dir_ref), custom_call_target="tpu_custom_call" | custom-call | flops 524288 | bytes 1626624 | tf_op jit(solution)/shard_map/last/pallas_call | solution.py:220
Async XLA Ops:
  0.6 6.1 %copy-start = (f32[192,128]{1,0:T(8,128)S(1)}, f32[192,128]{1,0:T(8,128)}, u32[]{:S(2)}) copy-start(f32[192,128]{1,0:T(8,128)} %fp_ref.5) | copy-start | bytes 294916
  0.6 6.1 %copy-start.1 = (f32[128,192]{0,1:T(8,128)S(1)}, f32[128,192]{0,1:T(8,128)}, u32[]{:S(2)}) copy-start(f32[128,192]{0,1:T(8,128)} %param.17) | copy-start | bytes 294916
  0.7 6.1 %copy-start.2 = (s32[6,1024]{1,0:T(8,128)S(1)}, s32[6,1024]{1,0:T(8,128)}, u32[]{:S(2)}) copy-start(s32[6,1024]{1,0:T(8,128)} %nb_ref.7) | copy-start | bytes 73732
  0.7 6.1 %copy-start.3 = (s32[6,1024]{1,0:T(8,128)S(1)}, s32[6,1024]{1,0:T(8,128)}, u32[]{:S(2)}) copy-start(s32[6,1024]{1,0:T(8,128)} %bd_ref.7) | copy-start | bytes 73732
  0.7 6.1 %copy-start.5 = (f32[128,128]{1,0:T(8,128)S(1)}, f32[128,128]{1,0:T(8,128)}, u32[]{:S(2)}) copy-start(f32[128,128]{1,0:T(8,128)} %stiff_ref.3) | copy-start | bytes 196612
  2.4 7.2 %collective-permute-start = (f32[64,1024]{1,0:T(8,128)S(1)}, f32[64,1024]{1,0:T(8,128)S(1)}, u32[]{:S(2)}, u32[]{:S(2)}) collective-permute-start(f32[64,1024]{1,0:T(8,128)S(1)} %get-tuple-element.27), channel_id=1, source_target_pairs={{0,8},{8,16},{16,24},{24,0},{1,9},{9,17},{17,25},{25,1},{2,10},{10... | collective-permute-start | bytes 786440 | tf_op jit(solution)/shard_map/ppermute | solution.py:271
  2.9 6.6 %collective-permute-start.1 = (f32[32,128]{1,0:T(8,128)S(1)}, f32[32,128]{1,0:T(8,128)S(1)}, u32[]{:S(2)}, u32[]{:S(2)}) collective-permute-start(f32[32,128]{1,0:T(8,128)S(1)} %get-tuple-element.28), channel_id=1, source_target_pairs={{0,1},{1,0},{2,3},{3,2},{4,5},{5,4},{6,7},{7,6},{8,9},{9,8},{10,11... | collective-permute-start | bytes 49160 | tf_op jit(solution)/shard_map/ppermute | solution.py:258
  5.5 1.3 %copy-start.8 = (f32[1024]{0:T(1024)S(1)}, f32[1024]{0:T(1024)}, u32[]{:S(2)}) copy-start(f32[1024]{0:T(1024)} %param.13) | copy-start | bytes 12292
  5.5 4.1 %collective-permute-start.2 = (f32[32,128]{1,0:T(8,128)S(1)}, f32[32,128]{1,0:T(8,128)S(1)}, u32[]{:S(2)}, u32[]{:S(2)}) collective-permute-start(f32[32,128]{1,0:T(8,128)S(1)} %get-tuple-element.29), channel_id=1, source_target_pairs={{0,8},{1,2},{2,1},{3,4},{4,3},{5,6},{6,5},{7,15},{8,0},{9,10},{10,... | collective-permute-start | bytes 49160 | tf_op jit(solution)/shard_map/ppermute | solution.py:258
  6.8 2.8 %copy-start.4 = (f32[1,128,1024]{2,1,0:T(8,128)S(1)}, f32[1,128,1024]{2,1,0:T(8,128)}, u32[]{:S(2)}) copy-start(f32[1,128,1024]{2,1,0:T(8,128)} %param.12) | copy-start | bytes 1572868
  6.8 2.8 %copy-start.6 = (f32[128,64]{0,1:T(8,128)S(1)}, f32[128,64]{0,1:T(8,128)}, u32[]{:S(2)}) copy-start(f32[128,64]{0,1:T(8,128)} %param.18) | copy-start | bytes 98308
  6.8 2.8 %copy-start.7 = (f32[128,128]{1,0:T(8,128)S(1)}, f32[128,128]{1,0:T(8,128)}, u32[]{:S(2)}) copy-start(f32[128,128]{1,0:T(8,128)} %inv_ref.1) | copy-start | bytes 196612
  9.6 0.7 %copy-start.9 = (s32[256]{0:T(256)S(1)}, s32[256]{0:T(256)}, u32[]{:S(2)}) copy-start(s32[256]{0:T(256)} %param.21) | copy-start | bytes 3076
  11.9 5.9 %collective-permute-start.3 = (f32[64,1024]{1,0:T(8,128)S(1)}, f32[64,1024]{1,0:T(8,128)S(1)}, u32[]{:S(2)}, u32[]{:S(2)}) collective-permute-start(f32[64,1024]{1,0:T(8,128)S(1)} %get-tuple-element.34), channel_id=1, source_target_pairs={{0,8},{8,16},{16,24},{24,0},{1,9},{9,17},{17,25},{25,1},{2,10},{10... | collective-permute-start | bytes 786440 | tf_op jit(solution)/shard_map/ppermute | solution.py:284
  12.5 5.2 %collective-permute-start.4 = (f32[32,128]{1,0:T(8,128)S(1)}, f32[32,128]{1,0:T(8,128)S(1)}, u32[]{:S(2)}, u32[]{:S(2)}) collective-permute-start(f32[32,128]{1,0:T(8,128)S(1)} %get-tuple-element.35), channel_id=1, source_target_pairs={{0,1},{1,0},{2,3},{3,2},{4,5},{5,4},{6,7},{7,6},{8,9},{9,8},{10,11... | collective-permute-start | bytes 49160 | tf_op jit(solution)/shard_map/ppermute | solution.py:258
  14.7 3.1 %collective-permute-start.5 = (f32[32,128]{1,0:T(8,128)S(1)}, f32[32,128]{1,0:T(8,128)S(1)}, u32[]{:S(2)}, u32[]{:S(2)}) collective-permute-start(f32[32,128]{1,0:T(8,128)S(1)} %get-tuple-element.36), channel_id=1, source_target_pairs={{0,8},{1,2},{2,1},{3,4},{4,3},{5,6},{6,5},{7,15},{8,0},{9,10},{10,... | collective-permute-start | bytes 49160 | tf_op jit(solution)/shard_map/ppermute | solution.py:258

commit v5 on v4

--- a/solution.py
+++ b/solution.py
@@ -11,8 +11,31 @@
 SUBS = 8
 
 
+WIDE = 256
+
+
 def dot(a, b):
     return jnp.dot(a, b, precision=lax.Precision.HIGHEST, preferred_element_type=jnp.float32)
+
+
+def split(x):
+    high = x.astype(jnp.bfloat16)
+    return high, (x - high.astype(jnp.float32)).astype(jnp.bfloat16)
+
+
+def left3(w):
+    high, low = split(w)
+    return jnp.concatenate([high, low, high], axis=1)
+
+
+def dot3(w3, x):
+    high, low = split(x)
+    return jnp.dot(w3, jnp.concatenate([high, high, low], axis=0), preferred_element_type=jnp.float32)
+
+
+def chunks(elements):
+    width = WIDE if elements % WIDE == 0 else LANES
+    return [slice(c, c + width) for c in range(0, elements, width)]
 
 
 def lane_gather(tile_of, tiles, columns, rows):
@@ -97,59 +120,88 @@
                 rim_ref[rows, cols] = 0.0 - found[r] * open_face
 
 
-def first_send(v_hbm, fp_hbm, send_hbm, v_ref, end_ref, tr_ref, first_ref, second_ref, fp_ref, send_ref, sems):
+def first_send(
+    v_hbm, fp_hbm, send_hbm, coef_hbm, nb_hbm, bd_hbm,
+    v_ref, end_ref, fp_ref, send_ref, coef_ref, nb_ref, bd_ref, tr_ref, first_ref, second_ref, sems,
+):
     face_dofs = fp_ref.shape[0] // 6
     elements = v_ref.shape[1]
     half = end_ref.shape[0]
-    pairs = ((v_hbm, v_ref), (fp_hbm, fp_ref), (send_hbm, send_ref), (v_hbm.at[pl.ds(half, half), :], end_ref))
+    parts = chunks(elements)
+    pairs = [(fp_hbm, fp_ref)] + [(v_hbm.at[:, c], v_ref.at[:, c]) for c in parts]
+    pairs += [(send_hbm, send_ref), (v_hbm.at[pl.ds(half, half), :], end_ref), (coef_hbm, coef_ref), (nb_hbm, nb_ref), (bd_hbm, bd_ref)]
     copies = [pltpu.make_async_copy(a, b, sems.at[i]) for i, (a, b) in enumerate(pairs)]
     for copy in copies:
         copy.start()
-    for copy in copies[:3]:
+    copies[0].wait()
+    weights = left3(jnp.concatenate([face_rows(fp_ref, f, face_dofs) for f in range(2)], axis=0))
+    for i, c in enumerate(parts):
+        copies[1 + i].wait()
+        tr_ref[:, c] = dot3(weights, v_ref[:, c])
+    copies[1 + len(parts)].wait()
+    fill_outbound(tr_ref, send_ref, first_ref, second_ref, face_dofs, elements)
+    for copy in copies[2 + len(parts) :]:
         copy.wait()
-    weights = jnp.concatenate([face_rows(fp_ref, f, face_dofs) for f in range(2)], axis=0)
-    tr_ref[...] = dot(weights, v_ref[...])
-    fill_outbound(tr_ref, send_ref, first_ref, second_ref, face_dofs, elements)
-    copies[3].wait()
-
-
-def local_part(v_ref, tr_ref, coef_ref, fp_ref, stiff_ref, liftt_ref, nb_ref, bd_ref, part_ref, jump_ref, traces):
-    face_dofs = fp_ref.shape[0] // 6
-    elements = v_ref.shape[1]
-    traces[: 2 * face_dofs, :] = tr_ref[...]
-    weights = jnp.concatenate([face_rows(fp_ref, f, face_dofs) for f in range(2, 6)], axis=0)
-    traces[2 * face_dofs :, :] = dot(weights, v_ref[...])
-    fill_jump(traces, nb_ref, bd_ref, jump_ref, face_dofs, elements)
-    liftt = jnp.concatenate([face_rows(liftt_ref, f, face_dofs) for f in range(6)], axis=0)
-    part_ref[...] = coef_ref[...] * dot(stiff_ref[...], v_ref[...]) + dot(liftt.T, jump_ref[...])
-
-
-def time_jump_of(v_ref, prev_ref):
-    return v_ref[: prev_ref.shape[0], :] - jnp.where(lax.axis_index("tm") > 0, prev_ref[...], 0.0)
-
-
-def finish_operator(part_ref, v_ref, prev_ref, liftt_ref, tlt_ref, rim, face_dofs):
-    time_jump = time_jump_of(v_ref, prev_ref)
-    liftt = jnp.concatenate([face_rows(liftt_ref, f, face_dofs) for f in range(2)] + [tlt_ref[...]], axis=0)
-    values = jnp.concatenate([rim[...], time_jump], axis=0)
-    return part_ref[...] + dot(liftt.T, values)
-
-
-def residual_step(
-    part_ref, v_ref, rhs_ref, prev_ref, first_in, second_in, coef_ref, inv_ref, fp_ref, liftt_ref, tlt_ref,
-    nb_ref, bd_ref, send_ref, res_ref, rim_ref, dir_ref, end_ref, tr_ref, first_ref, second_ref,
+
+
+def all_traces(v_ref, tr_ref, weights, traces):
+    known = tr_ref.shape[0]
+    for c in chunks(v_ref.shape[1]):
+        traces[:known, c] = tr_ref[:, c]
+        traces[known:, c] = dot3(weights, v_ref[:, c])
+
+
+def local_first(
+    v_ref, tr_ref, coef_ref, fp_ref, nb_ref, bd_ref, rhs_hbm, stiff_hbm, inv_hbm, liftt_hbm, tlt_hbm,
+    jump_ref, part_ref, ahead_ref, fp3_ref, apply3_ref, late3_ref, ahead3_ref,
+    traces, rhs, stiff, inv, liftt, tlt, sems,
 ):
     face_dofs = fp_ref.shape[0] // 6
     elements = v_ref.shape[1]
+    pairs = ((stiff_hbm, stiff), (liftt_hbm, liftt), (tlt_hbm, tlt), (inv_hbm, inv), (rhs_hbm, rhs))
+    copies = [pltpu.make_async_copy(a, b, sems.at[i]) for i, (a, b) in enumerate(pairs)]
+    for copy in copies:
+        copy.start()
+    fp3_ref[...] = left3(jnp.concatenate([face_rows(fp_ref, f, face_dofs) for f in range(2, 6)], axis=0))
+    all_traces(v_ref, tr_ref, fp3_ref[...], traces)
+    for copy in copies:
+        copy.wait()
+    lift_rows = [face_rows(liftt, f, face_dofs) for f in range(6)]
+    apply3_ref[...] = left3(jnp.concatenate([stiff[...], jnp.concatenate(lift_rows, axis=0).T], axis=1))
+    late = jnp.concatenate(lift_rows[:2] + [tlt[...]], axis=0).T
+    late3_ref[...] = left3(late)
+    inverse = inv[...]
+    first_faces = jnp.concatenate([face_rows(fp_ref, f, face_dofs) for f in range(2)], axis=0)
+    both = jnp.concatenate([inverse, dot(first_faces, inverse)], axis=0)
+    ahead3_ref[...] = left3(dot(both, late))
+    both = left3(both)
+    fill_jump(traces, nb_ref, bd_ref, jump_ref, face_dofs, elements)
+    for c in chunks(elements):
+        values = jnp.concatenate([coef_ref[:, c] * v_ref[:, c], jump_ref[:, c]], axis=0)
+        part = rhs[:, c] - dot3(apply3_ref[...], values)
+        part_ref[:, c] = part
+        ahead_ref[:, c] = dot3(both, part)
+
+
+def residual_step(
+    ahead_ref, v_ref, prev_ref, first_in, second_in, ahead3_ref, coef_ref, nb_ref, bd_ref, send_ref,
+    late_ref, dir_ref, end_ref, tr_ref, first_ref, second_ref,
+):
+    face_dofs = first_in.shape[0]
+    dofs, elements = dir_ref.shape
     half = prev_ref.shape[0]
-    rim_terms(first_in, second_in, nb_ref, bd_ref, rim_ref, face_dofs, elements)
-    res_ref[...] = rhs_ref[...] - finish_operator(part_ref, v_ref, prev_ref, liftt_ref, tlt_ref, rim_ref, face_dofs)
-    direction = dot(inv_ref[...], res_ref[...]) / coef_ref[...]
-    dir_ref[...] = direction
-    end_ref[...] = direction[half:, :]
-    weights = jnp.concatenate([face_rows(fp_ref, f, face_dofs) for f in range(2)], axis=0)
-    tr_ref[...] = dot(weights, direction)
+    rim_terms(first_in, second_in, nb_ref, bd_ref, late_ref, face_dofs, elements)
+    late_ref[2 * face_dofs :, :] = time_jump_of(v_ref, prev_ref)
+    for c in chunks(elements):
+        both = (ahead_ref[:, c] - dot3(ahead3_ref[...], late_ref[:, c])) * (1.0 / coef_ref[:, c])
+        dir_ref[:, c] = both[:dofs, :]
+        end_ref[:, c] = both[half:dofs, :]
+        tr_ref[:, c] = both[dofs:, :]
     fill_outbound(tr_ref, send_ref, first_ref, second_ref, face_dofs, elements)
+
+
+def time_jump_of(v_ref, prev_ref):
+    return v_ref[: prev_ref.shape[0], :] - jnp.where(lax.axis_index("tm") > 0, prev_ref[...], 0.0)
 
 
 def column_sum(x):
@@ -160,40 +212,74 @@
     return jnp.sum(row, axis=1, keepdims=True)
 
 
+def lowest(slope, bend):
+    return jnp.where(bend > 0.0, -slope / jnp.where(bend > 0.0, bend, 1.0), 0.0)
+
+
+def local_second(
+    dir_ref, tr_ref, coef_ref, nb_ref, bd_ref, fp3_ref, apply3_ref, late3_ref, part_ref, late_ref, jump0_ref,
+    image_ref, border_ref, res_ref, border0_ref, group_ref, traces, jump,
+):
+    elements = dir_ref.shape[1]
+    face_dofs = jump.shape[0] // 6
+    rim = 2 * face_dofs
+    all_traces(dir_ref, tr_ref, fp3_ref[...], traces)
+    fill_jump(traces, nb_ref, bd_ref, jump, face_dofs, elements)
+    for c in chunks(elements):
+        values = jnp.concatenate([coef_ref[:, c] * dir_ref[:, c], jump[:, c]], axis=0)
+        image_ref[:, c] = dot3(apply3_ref[...], values)
+        res_ref[:, c] = part_ref[:, c] - dot3(late3_ref[...], late_ref[:, c])
+        border_ref[:, c] = jump[:rim, c]
+        border0_ref[:, c] = jump0_ref[:rim, c] + late_ref[:rim, c]
+        j0, j1 = jump0_ref[rim:, c], jump[rim:, c]
+        bend, slope = 0.5 * column_sum(j1 * j1), 0.5 * column_sum(j0 * j1)
+        best = lowest(slope, bend)
+        j = j0 + best * j1
+        base = 0.5 * column_sum(j * j)
+        group_ref[:, c] = jnp.concatenate([base, slope, bend, best, base, base, base, base], axis=0)
+
+
 def image_step(
-    part_ref, jump_ref, dir_ref, prev_ref, first_in, second_in, liftt_ref, tlt_ref, nb_ref, bd_ref,
-    res_ref, jump0_ref, rim0_ref, v_ref, prev0_ref, coeff_ref, sums_ref, rim, image,
+    part_ref, border_ref, dir_ref, prev_ref, first_in, second_in, late3_ref, nb_ref, bd_ref, res_ref, border0_ref, late0_ref, group_ref,
+    coeff_ref, sums_ref, late,
 ):
     face_dofs = first_in.shape[0]
     elements = dir_ref.shape[1]
-    rim_rows = rim.shape[0]
-    rim_terms(first_in, second_in, nb_ref, bd_ref, rim, face_dofs, elements)
-    image[...] = finish_operator(part_ref, dir_ref, prev_ref, liftt_ref, tlt_ref, rim, face_dofs)
-    res, img = res_ref[...], image[...]
-    cross = column_sum(res * img)
-    square = column_sum(img * img)
-    j0 = jnp.concatenate([jump0_ref[:rim_rows, :] + rim0_ref[...], jump0_ref[rim_rows:, :]], axis=0)
-    j1 = jnp.concatenate([jump_ref[:rim_rows, :] + rim[...], jump_ref[rim_rows:, :]], axis=0)
-    t0 = time_jump_of(v_ref, prev0_ref)
-    t1 = time_jump_of(dir_ref, prev_ref)
-    bend = square + 0.5 * column_sum(j1 * j1) + column_sum(t1 * t1)
-    slope = 0.5 * column_sum(j0 * j1) + column_sum(t0 * t1) - cross
-    best = jnp.where(bend > 0.0, -slope / jnp.where(bend > 0.0, bend, 1.0), 0.0)
-    r = res - best * img
-    j = j0 + best * j1
-    t = t0 + best * t1
-    base = column_sum(r * r) + 0.5 * column_sum(j * j) + column_sum(t * t)
-    tilt = slope + best * bend
+    rim = 2 * face_dofs
+    rim_terms(first_in, second_in, nb_ref, bd_ref, late, face_dofs, elements)
+    late[rim:, :] = time_jump_of(dir_ref, prev_ref)
+    crosses, squares = [], []
+    for c in chunks(elements):
+        img = part_ref[:, c] + dot3(late3_ref[...], late[:, c])
+        res = res_ref[:, c]
+        cross, square = column_sum(res * img), column_sum(img * img)
+        j0, j1 = border0_ref[:, c], border_ref[:, c] + late[:rim, c]
+        t0, t1 = late0_ref[rim:, c], late[rim:, c]
+        g_base, g_slope, g_bend, g_best = (group_ref[i : i + 1, c] for i in range(4))
+        bend = square + 0.5 * column_sum(j1 * j1) + column_sum(t1 * t1) + g_bend
+        slope = 0.5 * column_sum(j0 * j1) + column_sum(t0 * t1) + g_slope - cross
+        best = lowest(slope, bend)
+        r = res - best * img
+        j = j0 + best * j1
+        t = t0 + best * t1
+        off = best - g_best
+        group = g_base + off * (2.0 * (g_slope + g_best * g_bend) + off * g_bend)
+        base = column_sum(r * r) + 0.5 * column_sum(j * j) + column_sum(t * t) + group
+        tilt = slope + best * bend
+        coeff_ref[:, c] = jnp.concatenate([base, tilt, bend, best, best, best, best, best], axis=0)
+        crosses.append(cross)
+        squares.append(square)
+    base, tilt, bend, best = (coeff_ref[i : i + 1, :] for i in range(4))
     bend_all = total_sum(bend)
-    weighted = total_sum(best * bend)
-    centre = jnp.where(bend_all > 0.0, weighted / jnp.where(bend_all > 0.0, bend_all, 1.0), 0.0)
+    centre = lowest(-total_sum(best * bend), bend_all)
     off = centre - best
     base_all = total_sum(base + off * (2.0 * tilt + off * bend))
     tilt_all = total_sum(tilt + off * bend)
-    coeff_ref[...] = jnp.concatenate([base, tilt, bend, best, best, best, best, best], axis=0)
+    cross_all = total_sum(jnp.concatenate(crosses, axis=1))
+    square_all = total_sum(jnp.concatenate(squares, axis=1))
     lane = lax.broadcasted_iota(jnp.int32, sums_ref.shape, 1)
     out = jnp.zeros(sums_ref.shape, jnp.float32)
-    for i, value in enumerate((total_sum(cross), total_sum(square), base_all, tilt_all, bend_all, centre)):
+    for i, value in enumerate((cross_all, square_all, base_all, tilt_all, bend_all, centre)):
         out = jnp.where(lane == i, value, out)
     sums_ref[...] = out
 
@@ -212,21 +298,23 @@
 
 VM = pl.BlockSpec(memory_space=pltpu.VMEM)
 HB = pl.BlockSpec(memory_space=pltpu.HBM)
-
-
-def call(body, name, outs, args, flops, scratch=(), spec=VM):
-    shapes = [jax.ShapeDtypeStruct(s, jnp.float32) for s in outs]
-    moved = sum(4 * a.size for a in args) + sum(4 * s.size for s in shapes)
+F32, BF16 = jnp.float32, jnp.bfloat16
+
+
+def call(body, name, outs, args, flops, far=(), scratch=()):
+    shapes = [jax.ShapeDtypeStruct(*s) if isinstance(s[0], tuple) else jax.ShapeDtypeStruct(s, F32) for s in outs]
+    far = tuple(pltpu.with_memory_space_constraint(x, pltpu.HBM) for x in far)
+    moved = sum(4 * a.size for a in args + far) + sum(4 * s.size for s in shapes)
     return pl.pallas_call(
         body,
         name=name,
         out_shape=shapes,
-        in_specs=[spec] * len(args),
+        in_specs=[VM] * len(args) + [HB] * len(far),
         out_specs=[VM] * len(outs),
-        scratch_shapes=[pltpu.VMEM(s, jnp.float32) if isinstance(s, tuple) else s for s in scratch],
+        scratch_shapes=[pltpu.VMEM(s, F32) if isinstance(s, tuple) else s for s in scratch],
         cost_estimate=pl.CostEstimate(flops=flops, bytes_accessed=moved, transcendentals=0),
-        compiler_params=pltpu.CompilerParams(vmem_limit_bytes=20 * 2**20),
-    )(*args)
+        compiler_params=pltpu.CompilerParams(vmem_limit_bytes=24 * 2**20),
+    )(*args, *far)
 
 
 def full_swaps(first, slabs, parts):
@@ -258,39 +346,55 @@
         swap = lambda x, first: lax.ppermute(x, ("tm", "space"), full_swaps(first, slabs, parts))
         return swap(a, 0), swap(b, 1)
 
-    two = 2 * face_dofs
-    v0, end0, tr0, a0, b0 = call(
+    rim = 2 * face_dofs
+    late = rim + half
+    edge = (face_dofs, border)
+    v0, end0, fp, send, coefs, nb, bd, tr0, a0, b0 = call(
         first_send,
         "send0",
-        [(dofs, elements), (half, elements), (two, elements), (face_dofs, border), (face_dofs, border)],
-        tuple(pltpu.with_memory_space_constraint(x, pltpu.HBM) for x in (initial[0], face_proj, send)),
-        2 * two * dofs * elements,
-        scratch=[(traces, dofs), pltpu.VMEM(send.shape, send.dtype), pltpu.SemaphoreType.DMA((4,))],
-        spec=HB,
+        [(dofs, elements), (half, elements), (traces, dofs), (send.shape, send.dtype), coef_row.shape]
+        + [(neighbour.shape, neighbour.dtype), (boundary.shape, boundary.dtype), (rim, elements), edge, edge],
+        (),
+        2 * rim * dofs * elements,
+        far=(initial[0], face_proj, send, coef_row, neighbour, boundary),
+        scratch=[pltpu.SemaphoreType.DMA((6 + len(chunks(elements)),))],
     )
     prev0 = lax.ppermute(end0, "tm", cycle)
     a0, b0 = halo(a0, b0)
-    local = functools.partial(
-        call, local_part, "local", [(dofs, elements), (traces, elements)], flops=12 * traces * dofs * elements, scratch=[(traces, elements)]
-    )
-    part0, jump0 = local(args=(v0, tr0, coef_row, face_proj, stiffness, liftt, neighbour, boundary))
-    res, rim0, direction, end, tr1, a1, b1 = call(
+    jump0, part0, ahead, fp3, apply3, late3, ahead3 = call(
+        local_first,
+        "local0",
+        [(traces, elements), (dofs, elements), (dofs + rim, elements), ((traces - rim, 3 * dofs), BF16)]
+        + [((dofs, 3 * (dofs + traces)), BF16), ((dofs, 3 * late), BF16), ((dofs + rim, 3 * late), BF16)],
+        (v0, tr0, coefs, fp, nb, bd),
+        12 * traces * dofs * elements,
+        far=(source, stiffness, block_inverse, liftt, tlt),
+        scratch=[(traces, elements), (dofs, elements), (dofs, dofs), (dofs, dofs), (traces, dofs), (half, dofs), pltpu.SemaphoreType.DMA((5,))],
+    )
+    late0, direction, end, tr1, a1, b1 = call(
         residual_step,
         "residual",
-        [(dofs, elements), (two, elements), (dofs, elements), (half, elements), (two, elements), (face_dofs, border), (face_dofs, border)],
-        (part0, v0, source, prev0, a0, b0, coef_row, block_inverse, face_proj, liftt, tlt, neighbour, boundary, send),
-        12 * dofs * dofs * elements,
+        [(late, elements), (dofs, elements), (half, elements), (rim, elements), edge, edge],
+        (ahead, v0, prev0, a0, b0, ahead3, coefs, nb, bd, send),
+        6 * dofs * dofs * elements,
     )
     prev1 = lax.ppermute(end, "tm", cycle)
     a1, b1 = halo(a1, b1)
-    part1, jump1 = local(args=(direction, tr1, coef_row, face_proj, stiffness, liftt, neighbour, boundary))
+    part1, border1, res, border0, group = call(
+        local_second,
+        "local1",
+        [(dofs, elements), (rim, elements), (dofs, elements), (rim, elements), (SUBS, elements)],
+        (direction, tr1, coefs, nb, bd, fp3, apply3, late3, part0, late0, jump0),
+        12 * traces * dofs * elements,
+        scratch=[(traces, elements), (traces, elements)],
+    )
     coeffs, sums = call(
         image_step,
         "image",
         [(SUBS, elements), (devices, LANES)],
-        (part1, jump1, direction, prev1, a1, b1, liftt, tlt, neighbour, boundary, res, jump0, rim0, v0, prev0),
-        12 * dofs * dofs * elements,
-        scratch=[(two, elements), (dofs, elements)],
+        (part1, border1, direction, prev1, a1, b1, late3, nb, bd, res, border0, late0, group),
+        6 * dofs * dofs * elements,
+        scratch=[(late, elements)],
     )
     everyone = lax.all_to_all(sums, ("tm", "space"), 0, 0, tiled=True)
     smoothed, indicator, estimate = call(

time: 33.1 us -> 32.6 us (0.985)
  Pallas kernels: 11.1 us -> 12.1 us
  blocking collectives: 12.8 us -> 12.1 us
  local copies, waits for them, and re-layouts: 0.69 us -> 0 us
    pallas_call x6, Pallas kernels: 11.1 us -> 12.1 us  [call(): pl.pallas_call(body, name=name, out_shape=shapes, in_specs=[VM] * len(arg...]
    all_to_all x1, blocking collectives: 12.8 us -> 12.1 us  [on_device(): everyone = lax.all_to_all(sums, ('tm', 'space'), 0, 0, tiled=True)]
    unnamed x20 -> x0, local copies, waits for them, and re-layouts: 0.69 us -> none
    ppermute x4, starting transfers between devices: 6.32 us -> 6.94 us  [halo(): lax.ppermute(x, ('tm', 'space'), full_swaps(first, slabs, parts))]
    ppermute x1, starting transfers between devices: 0.67 us -> 0.06 us  [on_device(): prev1 = lax.ppermute(end, 'tm', cycle)]
  transfers between devices with their start and end apart: 6 -> 6, of which waited for: 0 -> 0; matrix products, arithmetic and copies ran while one was open for 0% -> 0% of each run, Pallas kernels for 17% -> 22%
where the time goes in v5:
time: 32.6 us; the launch traced here: 32.4 us
  Pallas kernels  12.1 us (37%)
  blocking collectives  12.1 us (37%)
  starting transfers between devices  7.55 us (23%)
  between operations  0.71 us (2%)
    all_to_all x1, blocking collectives, on_device(): everyone = lax.all_to_all(sums, ('tm', 'space'), 0, 0, tiled=True)  12.1 us
    pallas_call x6, Pallas kernels, call(): pl.pallas_call(body, name=name, out_shape=shapes, in_specs=[VM] * len(arg...  12.1 us
    ppermute x4, starting transfers between devices, halo(): lax.ppermute(x, ('tm', 'space'), full_swaps(first, slabs, parts))  6.94 us
  transfers between devices with their start and end apart: 6, of which 0 were waited for; matrix products, arithmetic and copies ran while one was open for 0% of the time, Pallas kernels for 22%

profile of v5, /device:TPU:0, one launch (start us, length us, event | category | flops | bytes accessed | tf_op | source)
XLA Modules:
  0.0 32.4 jit_solution(16124907912205002205)
XLA Ops:
  0.6 2.0 %send0.1 = (f32[128,1024]{1,0:T(8,128)S(1)}, f32[64,1024]{1,0:T(8,128)S(1)}, f32[192,128]{1,0:T(8,128)S(1)}, s32[2,128]{1,0:T(2,128)S(1)}, f32[1,1024]{1,0:T(1,1...) custom-call(f32[128,1024]{1,0:T(8,128)} %bitcast.15, ...), custom_call_target="tpu_custom_call" | custom-call | flops 16777216 | bytes 1910784 | tf_op jit(solution)/shard_map/send0/pallas_call | solution.py:308
  2.6 0.5 %collective-permute-start = (f32[64,1024]{1,0:T(8,128)S(1)}, f32[64,1024]{1,0:T(8,128)S(1)}, u32[]{:S(2)}, u32[]{:S(2)}) collective-permute-start(f32[64,1024]{1,0:T(8,128)S(1)} %get-tuple-element.43), channel_id=1, source_target_pairs={{0,8},{8,16},{16,24},{24,0},{1,9},{9,17},{17,25},{25,1},{2,10},{10... | collective-permute-start | bytes 786440 | tf_op jit(solution)/shard_map/ppermute | solution.py:362
  3.2 2.6 %collective-permute-start.1 = (f32[32,128]{1,0:T(8,128)S(1)}, f32[32,128]{1,0:T(8,128)S(1)}, u32[]{:S(2)}, u32[]{:S(2)}) collective-permute-start(f32[32,128]{1,0:T(8,128)S(1)} %get-tuple-element.44), channel_id=1, source_target_pairs={{0,1},{1,0},{2,3},{3,2},{4,5},{5,4},{6,7},{7,6},{8,9},{9,8},{10,11... | collective-permute-start | bytes 49160 | tf_op jit(solution)/shard_map/ppermute | solution.py:346
  5.7 1.3 %collective-permute-start.2 = (f32[32,128]{1,0:T(8,128)S(1)}, f32[32,128]{1,0:T(8,128)S(1)}, u32[]{:S(2)}, u32[]{:S(2)}) collective-permute-start(f32[32,128]{1,0:T(8,128)S(1)} %get-tuple-element.45), channel_id=1, source_target_pairs={{0,8},{1,2},{2,1},{3,4},{4,3},{5,6},{6,5},{7,15},{8,0},{9,10},{10,... | collective-permute-start | bytes 49160 | tf_op jit(solution)/shard_map/ppermute | solution.py:346
  7.0 4.6 %local0.1 = (f32[192,1024]{1,0:T(8,128)S(1)}, f32[128,1024]{1,0:T(8,128)S(1)}, f32[192,1024]{1,0:T(8,128)S(1)}, bf16[128,384]{1,0:T(8,128)(2,1)S(1)}, bf16[128,9...) custom-call(f32[128,1024]{1,0:T(8,128)S(1)} %get-tuple-element.36.v_ref, ...), custom_call_target="tpu_custom_call" | custom-call | flops 301989888 | bytes 5001216 | tf_op jit(solution)/shard_map/local0/pallas_call | solution.py:308
  11.6 0.0 collective-permute-done.1.first_in
  11.6 0.0 collective-permute-done.2.second_in
  11.6 0.0 collective-permute-done.prev_ref
  11.6 0.7 %residual.1 = (f32[128,1024]{1,0:T(8,128)S(1)}, f32[128,1024]{1,0:T(8,128)S(1)}, f32[64,1024]{1,0:T(8,128)S(1)}, f32[64,1024]{1,0:T(8,128)S(1)}, f32[32,128]{1,0:T(8,128)S(1)}, /*index=5*/f32[32,128]{1,0:T(8,128)S(1)}) custom-call(f32[192,1024]{1,0:T(8,128)S(1)} %get-tuple-element.42.ahead_ref, f32[128,1024]{1,0:T(8,128)S(1)} %get-tuple-element.36.v_ref, ...), custom_call_target="tpu_custom_call" | custom-call | flops 100663296 | bytes 3560448 | tf_op jit(solution)/shard_map/residual/pallas_call | solution.py:308
  12.3 0.1 collective-permute-start.3
  12.4 2.8 %collective-permute-start.4 = (f32[32,128]{1,0:T(8,128)S(1)}, f32[32,128]{1,0:T(8,128)S(1)}, u32[]{:S(2)}, u32[]{:S(2)}) collective-permute-start(f32[32,128]{1,0:T(8,128)S(1)} %get-tuple-element.59), channel_id=1, source_target_pairs={{0,1},{1,0},{2,3},{3,2},{4,5},{5,4},{6,7},{7,6},{8,9},{9,8},{10,11... | collective-permute-start | bytes 49160 | tf_op jit(solution)/shard_map/ppermute | solution.py:346
  15.1 0.4 %collective-permute-start.5 = (f32[32,128]{1,0:T(8,128)S(1)}, f32[32,128]{1,0:T(8,128)S(1)}, u32[]{:S(2)}, u32[]{:S(2)}) collective-permute-start(f32[32,128]{1,0:T(8,128)S(1)} %get-tuple-element.60), channel_id=1, source_target_pairs={{0,8},{1,2},{2,1},{3,4},{4,3},{5,6},{6,5},{7,15},{8,0},{9,10},{10,... | collective-permute-start | bytes 49160 | tf_op jit(solution)/shard_map/ppermute | solution.py:346
  15.5 2.6 %local1.1 = (f32[128,1024]{1,0:T(8,128)S(1)}, f32[64,1024]{1,0:T(8,128)S(1)}, f32[128,1024]{1,0:T(8,128)S(1)}, f32[64,1024]{1,0:T(8,128)S(1)}, f32[8,1024]{1,0:T(8,128)S(1)}) custom-call(f32[128,1024]{1,0:T(8,128)S(1)} %get-tuple-element.48.dir_ref, f32[64,1024]{1,0:T(8,128)S(1)} %get-tuple-element.49.tr_ref, f32[1,1024]{1,0:T(1,128)S(1)} %get-tuple-element.38.coef_ref, ...), custom_call_target="tpu_custom_call" | custom-call | flops 301989888 | bytes 5165056 | tf_op jit(solution)/shard_map/local1/pallas_call | solution.py:308
  18.1 0.0 collective-permute-done.4.first_in
  18.1 0.0 collective-permute-done.5.second_in
  18.1 0.0 collective-permute-done.3.prev_ref
  18.2 1.1 %image.1 = (f32[8,1024]{1,0:T(8,128)S(1)}, f32[32,128]{1,0:T(8,128)S(1)}) custom-call(f32[128,1024]{1,0:T(8,128)S(1)} %get-tuple-element.56.part_ref, f32[64,1024]{1,0:T(8,128)S(1)} %get-tuple-element.57.border_ref, f32[128,1024]{1,0:T(8,128)S(1)} %get-tuple-element.48.dir_ref, f32[64,1024]{1,0:T(8,128)S(1)} %collective-permute-done.3.prev_ref, ...), custom_call_target="tpu_custom_call" | custom-call | flops 100663296 | bytes 3244032 | tf_op jit(solution)/shard_map/image/pallas_call | solution.py:308
  19.3 12.1 %all_to_all.11 = f32[32,1,128]{2,1,0:T(1,128)S(1)} all-to-all(f32[32,1,128]{2,1,0:T(1,128)S(1)} %bitcast.14), channel_id=1, replica_groups=mesh['tm'=4,'space'=8] {'tm','space'}, dimensions={0} | all-to-all | bytes 32768 | tf_op jit(solution)/shard_map/all_to_all | solution.py:399
  31.4 1.0 %last.1 = (f32[128,1024]{1,0:T(8,128)}, f32[1,1024]{1,0:T(1,128)}, f32[1,128]{1,0:T(1,128)}) custom-call(f32[32,128]{1,0:T(8,128)S(1)} %bitcast.13, f32[8,1024]{1,0:T(8,128)S(1)} %get-tuple-element.65.coeff_ref, f32[128,1024]{1,0:T(8,128)S(1)} %get-tuple-element.36.v_ref, f32[128,1024]{1,0:T(8,128)S(1)} %get-tuple-element.48.dir_ref), custom_call_target="tpu_custom_call" | custom-call | flops 524288 | bytes 1626624 | tf_op jit(solution)/shard_map/last/pallas_call | solution.py:308
Async XLA Ops:
  2.6 9.0 %collective-permute-start = (f32[64,1024]{1,0:T(8,128)S(1)}, f32[64,1024]{1,0:T(8,128)S(1)}, u32[]{:S(2)}, u32[]{:S(2)}) collective-permute-start(f32[64,1024]{1,0:T(8,128)S(1)} %get-tuple-element.43), channel_id=1, source_target_pairs={{0,8},{8,16},{16,24},{24,0},{1,9},{9,17},{17,25},{25,1},{2,10},{10... | collective-permute-start | bytes 786440 | tf_op jit(solution)/shard_map/ppermute | solution.py:362
  3.2 8.4 %collective-permute-start.1 = (f32[32,128]{1,0:T(8,128)S(1)}, f32[32,128]{1,0:T(8,128)S(1)}, u32[]{:S(2)}, u32[]{:S(2)}) collective-permute-start(f32[32,128]{1,0:T(8,128)S(1)} %get-tuple-element.44), channel_id=1, source_target_pairs={{0,1},{1,0},{2,3},{3,2},{4,5},{5,4},{6,7},{7,6},{8,9},{9,8},{10,11... | collective-permute-start | bytes 49160 | tf_op jit(solution)/shard_map/ppermute | solution.py:346
  5.7 5.9 %collective-permute-start.2 = (f32[32,128]{1,0:T(8,128)S(1)}, f32[32,128]{1,0:T(8,128)S(1)}, u32[]{:S(2)}, u32[]{:S(2)}) collective-permute-start(f32[32,128]{1,0:T(8,128)S(1)} %get-tuple-element.45), channel_id=1, source_target_pairs={{0,8},{1,2},{2,1},{3,4},{4,3},{5,6},{6,5},{7,15},{8,0},{9,10},{10,... | collective-permute-start | bytes 49160 | tf_op jit(solution)/shard_map/ppermute | solution.py:346
  12.3 5.8 %collective-permute-start.3 = (f32[64,1024]{1,0:T(8,128)S(1)}, f32[64,1024]{1,0:T(8,128)S(1)}, u32[]{:S(2)}, u32[]{:S(2)}) collective-permute-start(f32[64,1024]{1,0:T(8,128)S(1)} %get-tuple-element.58), channel_id=1, source_target_pairs={{0,8},{8,16},{16,24},{24,0},{1,9},{9,17},{17,25},{25,1},{2,10},{10... | collective-permute-start | bytes 786440 | tf_op jit(solution)/shard_map/ppermute | solution.py:381
  12.4 5.7 %collective-permute-start.4 = (f32[32,128]{1,0:T(8,128)S(1)}, f32[32,128]{1,0:T(8,128)S(1)}, u32[]{:S(2)}, u32[]{:S(2)}) collective-permute-start(f32[32,128]{1,0:T(8,128)S(1)} %get-tuple-element.59), channel_id=1, source_target_pairs={{0,1},{1,0},{2,3},{3,2},{4,5},{5,4},{6,7},{7,6},{8,9},{9,8},{10,11... | collective-permute-start | bytes 49160 | tf_op jit(solution)/shard_map/ppermute | solution.py:346
  15.1 3.0 %collective-permute-start.5 = (f32[32,128]{1,0:T(8,128)S(1)}, f32[32,128]{1,0:T(8,128)S(1)}, u32[]{:S(2)}, u32[]{:S(2)}) collective-permute-start(f32[32,128]{1,0:T(8,128)S(1)} %get-tuple-element.60), channel_id=1, source_target_pairs={{0,8},{1,2},{2,1},{3,4},{4,3},{5,6},{6,5},{7,15},{8,0},{9,10},{10,... | collective-permute-start | bytes 49160 | tf_op jit(solution)/shard_map/ppermute | solution.py:346

commit v6 on v5

--- a/solution.py
+++ b/solution.py
@@ -78,7 +78,7 @@
             second_ref[rows, cols] = jnp.where(odd, upper[r], lower[r])
 
 
-def fill_jump(traces, nb_ref, bd_ref, jump_ref, face_dofs, elements):
+def fill_jump(traces, nb_ref, bd_ref, jump_ref, face_dofs, elements, chunk):
     per_face = elements // LANES
     for face in range(6):
         other = face ^ 1
@@ -86,8 +86,8 @@
         def tile_of(tile, r, other=other):
             return traces[other * face_dofs + r * SUBS : other * face_dofs + (r + 1) * SUBS, tile * LANES : (tile + 1) * LANES]
 
-        for j in range(per_face):
-            cols = slice(j * LANES, (j + 1) * LANES)
+        for start in range(chunk.start, chunk.stop, LANES):
+            cols = slice(start, start + LANES)
             found = lane_gather(tile_of, per_face, nb_ref[face : face + 1, cols] - other * elements, face_dofs)
             open_face = jnp.broadcast_to(1.0 - bd_ref[face : face + 1, cols].astype(jnp.float32), (SUBS, LANES))
             for r in range(face_dofs // SUBS):
@@ -129,7 +129,7 @@
     half = end_ref.shape[0]
     parts = chunks(elements)
     pairs = [(fp_hbm, fp_ref)] + [(v_hbm.at[:, c], v_ref.at[:, c]) for c in parts]
-    pairs += [(send_hbm, send_ref), (v_hbm.at[pl.ds(half, half), :], end_ref), (coef_hbm, coef_ref), (nb_hbm, nb_ref), (bd_hbm, bd_ref)]
+    pairs += [(send_hbm, send_ref), (coef_hbm, coef_ref), (nb_hbm, nb_ref), (bd_hbm, bd_ref)]
     copies = [pltpu.make_async_copy(a, b, sems.at[i]) for i, (a, b) in enumerate(pairs)]
     for copy in copies:
         copy.start()
@@ -138,6 +138,7 @@
     for i, c in enumerate(parts):
         copies[1 + i].wait()
         tr_ref[:, c] = dot3(weights, v_ref[:, c])
+        end_ref[:, c] = v_ref[half:, c]
     copies[1 + len(parts)].wait()
     fill_outbound(tr_ref, send_ref, first_ref, second_ref, face_dofs, elements)
     for copy in copies[2 + len(parts) :]:
@@ -164,6 +165,10 @@
         copy.start()
     fp3_ref[...] = left3(jnp.concatenate([face_rows(fp_ref, f, face_dofs) for f in range(2, 6)], axis=0))
     all_traces(v_ref, tr_ref, fp3_ref[...], traces)
+    parts = chunks(elements)
+    early = (len(parts) + 1) // 2
+    for c in parts[:early]:
+        fill_jump(traces, nb_ref, bd_ref, jump_ref, face_dofs, elements, c)
     for copy in copies:
         copy.wait()
     lift_rows = [face_rows(liftt, f, face_dofs) for f in range(6)]
@@ -175,8 +180,9 @@
     both = jnp.concatenate([inverse, dot(first_faces, inverse)], axis=0)
     ahead3_ref[...] = left3(dot(both, late))
     both = left3(both)
-    fill_jump(traces, nb_ref, bd_ref, jump_ref, face_dofs, elements)
-    for c in chunks(elements):
+    for i, c in enumerate(parts):
+        if early + i < len(parts):
+            fill_jump(traces, nb_ref, bd_ref, jump_ref, face_dofs, elements, parts[early + i])
         values = jnp.concatenate([coef_ref[:, c] * v_ref[:, c], jump_ref[:, c]], axis=0)
         part = rhs[:, c] - dot3(apply3_ref[...], values)
         part_ref[:, c] = part
@@ -224,8 +230,8 @@
     face_dofs = jump.shape[0] // 6
     rim = 2 * face_dofs
     all_traces(dir_ref, tr_ref, fp3_ref[...], traces)
-    fill_jump(traces, nb_ref, bd_ref, jump, face_dofs, elements)
     for c in chunks(elements):
+        fill_jump(traces, nb_ref, bd_ref, jump, face_dofs, elements, c)
         values = jnp.concatenate([coef_ref[:, c] * dir_ref[:, c], jump[:, c]], axis=0)
         image_ref[:, c] = dot3(apply3_ref[...], values)
         res_ref[:, c] = part_ref[:, c] - dot3(late3_ref[...], late_ref[:, c])
@@ -357,7 +363,7 @@
         (),
         2 * rim * dofs * elements,
         far=(initial[0], face_proj, send, coef_row, neighbour, boundary),
-        scratch=[pltpu.SemaphoreType.DMA((6 + len(chunks(elements)),))],
+        scratch=[pltpu.SemaphoreType.DMA((5 + len(chunks(elements)),))],
     )
     prev0 = lax.ppermute(end0, "tm", cycle)
     a0, b0 = halo(a0, b0)

time: 32.6 us -> 31.8 us (0.975)
  Pallas kernels: 12.1 us -> 11.2 us
    pallas_call x6, Pallas kernels: 12.1 us -> 11.2 us  [call(): pl.pallas_call(body, name=name, out_shape=shapes, in_specs=[VM] * len(arg...]
  transfers between devices with their start and end apart: 6 -> 6, of which waited for: 0 -> 1; matrix products, arithmetic and copies ran while one was open for 0% -> 0% of each run, Pallas kernels for 22% -> 20%
where the time goes in v6:
time: 31.8 us; the launch traced here: 31.6 us
  blocking collectives  12.1 us (38%)
  Pallas kernels  11.2 us (35%)
  starting transfers between devices  7.55 us (24%)
  between operations  0.7 us (2%)
    all_to_all x1, blocking collectives, on_device(): everyone = lax.all_to_all(sums, ('tm', 'space'), 0, 0, tiled=True)  12.1 us
    pallas_call x6, Pallas kernels, call(): pl.pallas_call(body, name=name, out_shape=shapes, in_specs=[VM] * len(arg...  11.2 us
    ppermute x4, starting transfers between devices, halo(): lax.ppermute(x, ('tm', 'space'), full_swaps(first, slabs, parts))  6.94 us
  transfers between devices with their start and end apart: 6, of which 1 were waited for; matrix products, arithmetic and copies ran while one was open for 0% of the time, Pallas kernels for 20%

profile of v6, /device:TPU:0, one launch (start us, length us, event | category | flops | bytes accessed | tf_op | source)
XLA Modules:
  0.0 31.6 jit_solution(8625885311580657855)
XLA Ops:
  0.6 2.0 %send0.1 = (f32[128,1024]{1,0:T(8,128)S(1)}, f32[64,1024]{1,0:T(8,128)S(1)}, f32[192,128]{1,0:T(8,128)S(1)}, s32[2,128]{1,0:T(2,128)S(1)}, f32[1,1024]{1,0:T(1,1...) custom-call(f32[128,1024]{1,0:T(8,128)} %bitcast.15, ...), custom_call_target="tpu_custom_call" | custom-call | flops 16777216 | bytes 1910784 | tf_op jit(solution)/shard_map/send0/pallas_call | solution.py:314
  2.6 0.5 %collective-permute-start = (f32[64,1024]{1,0:T(8,128)S(1)}, f32[64,1024]{1,0:T(8,128)S(1)}, u32[]{:S(2)}, u32[]{:S(2)}) collective-permute-start(f32[64,1024]{1,0:T(8,128)S(1)} %get-tuple-element.43), channel_id=1, source_target_pairs={{0,8},{8,16},{16,24},{24,0},{1,9},{9,17},{17,25},{25,1},{2,10},{10... | collective-permute-start | bytes 786440 | tf_op jit(solution)/shard_map/ppermute | solution.py:368
  3.2 2.6 %collective-permute-start.1 = (f32[32,128]{1,0:T(8,128)S(1)}, f32[32,128]{1,0:T(8,128)S(1)}, u32[]{:S(2)}, u32[]{:S(2)}) collective-permute-start(f32[32,128]{1,0:T(8,128)S(1)} %get-tuple-element.44), channel_id=1, source_target_pairs={{0,1},{1,0},{2,3},{3,2},{4,5},{5,4},{6,7},{7,6},{8,9},{9,8},{10,11... | collective-permute-start | bytes 49160 | tf_op jit(solution)/shard_map/ppermute | solution.py:352
  5.7 1.3 %collective-permute-start.2 = (f32[32,128]{1,0:T(8,128)S(1)}, f32[32,128]{1,0:T(8,128)S(1)}, u32[]{:S(2)}, u32[]{:S(2)}) collective-permute-start(f32[32,128]{1,0:T(8,128)S(1)} %get-tuple-element.45), channel_id=1, source_target_pairs={{0,8},{1,2},{2,1},{3,4},{4,3},{5,6},{6,5},{7,15},{8,0},{9,10},{10,... | collective-permute-start | bytes 49160 | tf_op jit(solution)/shard_map/ppermute | solution.py:352
  7.0 3.8 %local0.1 = (f32[192,1024]{1,0:T(8,128)S(1)}, f32[128,1024]{1,0:T(8,128)S(1)}, f32[192,1024]{1,0:T(8,128)S(1)}, bf16[128,384]{1,0:T(8,128)(2,1)S(1)}, bf16[128,9...) custom-call(f32[128,1024]{1,0:T(8,128)S(1)} %get-tuple-element.36.v_ref, ...), custom_call_target="tpu_custom_call" | custom-call | flops 301989888 | bytes 5001216 | tf_op jit(solution)/shard_map/local0/pallas_call | solution.py:314
  10.8 0.0 collective-permute-done.1.first_in
  10.8 0.0 collective-permute-done.2.second_in
  10.8 0.0 collective-permute-done.prev_ref
  10.9 0.7 %residual.1 = (f32[128,1024]{1,0:T(8,128)S(1)}, f32[128,1024]{1,0:T(8,128)S(1)}, f32[64,1024]{1,0:T(8,128)S(1)}, f32[64,1024]{1,0:T(8,128)S(1)}, f32[32,128]{1,0:T(8,128)S(1)}, /*index=5*/f32[32,128]{1,0:T(8,128)S(1)}) custom-call(f32[192,1024]{1,0:T(8,128)S(1)} %get-tuple-element.42.ahead_ref, f32[128,1024]{1,0:T(8,128)S(1)} %get-tuple-element.36.v_ref, ...), custom_call_target="tpu_custom_call" | custom-call | flops 100663296 | bytes 3560448 | tf_op jit(solution)/shard_map/residual/pallas_call | solution.py:314
  11.5 0.1 collective-permute-start.3
  11.6 2.8 %collective-permute-start.4 = (f32[32,128]{1,0:T(8,128)S(1)}, f32[32,128]{1,0:T(8,128)S(1)}, u32[]{:S(2)}, u32[]{:S(2)}) collective-permute-start(f32[32,128]{1,0:T(8,128)S(1)} %get-tuple-element.59), channel_id=1, source_target_pairs={{0,1},{1,0},{2,3},{3,2},{4,5},{5,4},{6,7},{7,6},{8,9},{9,8},{10,11... | collective-permute-start | bytes 49160 | tf_op jit(solution)/shard_map/ppermute | solution.py:352
  14.4 0.4 %collective-permute-start.5 = (f32[32,128]{1,0:T(8,128)S(1)}, f32[32,128]{1,0:T(8,128)S(1)}, u32[]{:S(2)}, u32[]{:S(2)}) collective-permute-start(f32[32,128]{1,0:T(8,128)S(1)} %get-tuple-element.60), channel_id=1, source_target_pairs={{0,8},{1,2},{2,1},{3,4},{4,3},{5,6},{6,5},{7,15},{8,0},{9,10},{10,... | collective-permute-start | bytes 49160 | tf_op jit(solution)/shard_map/ppermute | solution.py:352
  14.7 2.6 %local1.1 = (f32[128,1024]{1,0:T(8,128)S(1)}, f32[64,1024]{1,0:T(8,128)S(1)}, f32[128,1024]{1,0:T(8,128)S(1)}, f32[64,1024]{1,0:T(8,128)S(1)}, f32[8,1024]{1,0:T(8,128)S(1)}) custom-call(f32[128,1024]{1,0:T(8,128)S(1)} %get-tuple-element.48.dir_ref, f32[64,1024]{1,0:T(8,128)S(1)} %get-tuple-element.49.tr_ref, f32[1,1024]{1,0:T(1,128)S(1)} %get-tuple-element.38.coef_ref, ...), custom_call_target="tpu_custom_call" | custom-call | flops 301989888 | bytes 5165056 | tf_op jit(solution)/shard_map/local1/pallas_call | solution.py:314
  17.3 0.0 collective-permute-done.4.first_in
  17.3 0.0 collective-permute-done.5.second_in
  17.3 0.1 collective-permute-done.3.prev_ref
  17.4 1.1 %image.1 = (f32[8,1024]{1,0:T(8,128)S(1)}, f32[32,128]{1,0:T(8,128)S(1)}) custom-call(f32[128,1024]{1,0:T(8,128)S(1)} %get-tuple-element.56.part_ref, f32[64,1024]{1,0:T(8,128)S(1)} %get-tuple-element.57.border_ref, f32[128,1024]{1,0:T(8,128)S(1)} %get-tuple-element.48.dir_ref, f32[64,1024]{1,0:T(8,128)S(1)} %collective-permute-done.3.prev_ref, ...), custom_call_target="tpu_custom_call" | custom-call | flops 100663296 | bytes 3244032 | tf_op jit(solution)/shard_map/image/pallas_call | solution.py:314
  18.5 12.1 %all_to_all.11 = f32[32,1,128]{2,1,0:T(1,128)S(1)} all-to-all(f32[32,1,128]{2,1,0:T(1,128)S(1)} %bitcast.14), channel_id=1, replica_groups=mesh['tm'=4,'space'=8] {'tm','space'}, dimensions={0} | all-to-all | bytes 32768 | tf_op jit(solution)/shard_map/all_to_all | solution.py:405
  30.6 1.0 %last.1 = (f32[128,1024]{1,0:T(8,128)}, f32[1,1024]{1,0:T(1,128)}, f32[1,128]{1,0:T(1,128)}) custom-call(f32[32,128]{1,0:T(8,128)S(1)} %bitcast.13, f32[8,1024]{1,0:T(8,128)S(1)} %get-tuple-element.65.coeff_ref, f32[128,1024]{1,0:T(8,128)S(1)} %get-tuple-element.36.v_ref, f32[128,1024]{1,0:T(8,128)S(1)} %get-tuple-element.48.dir_ref), custom_call_target="tpu_custom_call" | custom-call | flops 524288 | bytes 1626624 | tf_op jit(solution)/shard_map/last/pallas_call | solution.py:314
Async XLA Ops:
  2.6 8.2 %collective-permute-start = (f32[64,1024]{1,0:T(8,128)S(1)}, f32[64,1024]{1,0:T(8,128)S(1)}, u32[]{:S(2)}, u32[]{:S(2)}) collective-permute-start(f32[64,1024]{1,0:T(8,128)S(1)} %get-tuple-element.43), channel_id=1, source_target_pairs={{0,8},{8,16},{16,24},{24,0},{1,9},{9,17},{17,25},{25,1},{2,10},{10... | collective-permute-start | bytes 786440 | tf_op jit(solution)/shard_map/ppermute | solution.py:368
  3.2 7.6 %collective-permute-start.1 = (f32[32,128]{1,0:T(8,128)S(1)}, f32[32,128]{1,0:T(8,128)S(1)}, u32[]{:S(2)}, u32[]{:S(2)}) collective-permute-start(f32[32,128]{1,0:T(8,128)S(1)} %get-tuple-element.44), channel_id=1, source_target_pairs={{0,1},{1,0},{2,3},{3,2},{4,5},{5,4},{6,7},{7,6},{8,9},{9,8},{10,11... | collective-permute-start | bytes 49160 | tf_op jit(solution)/shard_map/ppermute | solution.py:352
  5.7 5.1 %collective-permute-start.2 = (f32[32,128]{1,0:T(8,128)S(1)}, f32[32,128]{1,0:T(8,128)S(1)}, u32[]{:S(2)}, u32[]{:S(2)}) collective-permute-start(f32[32,128]{1,0:T(8,128)S(1)} %get-tuple-element.45), channel_id=1, source_target_pairs={{0,8},{1,2},{2,1},{3,4},{4,3},{5,6},{6,5},{7,15},{8,0},{9,10},{10,... | collective-permute-start | bytes 49160 | tf_op jit(solution)/shard_map/ppermute | solution.py:352
  11.5 5.8 %collective-permute-start.3 = (f32[64,1024]{1,0:T(8,128)S(1)}, f32[64,1024]{1,0:T(8,128)S(1)}, u32[]{:S(2)}, u32[]{:S(2)}) collective-permute-start(f32[64,1024]{1,0:T(8,128)S(1)} %get-tuple-element.58), channel_id=1, source_target_pairs={{0,8},{8,16},{16,24},{24,0},{1,9},{9,17},{17,25},{25,1},{2,10},{10... | collective-permute-start | bytes 786440 | tf_op jit(solution)/shard_map/ppermute | solution.py:387
  11.6 5.7 %collective-permute-start.4 = (f32[32,128]{1,0:T(8,128)S(1)}, f32[32,128]{1,0:T(8,128)S(1)}, u32[]{:S(2)}, u32[]{:S(2)}) collective-permute-start(f32[32,128]{1,0:T(8,128)S(1)} %get-tuple-element.59), channel_id=1, source_target_pairs={{0,1},{1,0},{2,3},{3,2},{4,5},{5,4},{6,7},{7,6},{8,9},{9,8},{10,11... | collective-permute-start | bytes 49160 | tf_op jit(solution)/shard_map/ppermute | solution.py:352
  14.4 2.9 %collective-permute-start.5 = (f32[32,128]{1,0:T(8,128)S(1)}, f32[32,128]{1,0:T(8,128)S(1)}, u32[]{:S(2)}, u32[]{:S(2)}) collective-permute-start(f32[32,128]{1,0:T(8,128)S(1)} %get-tuple-element.60), channel_id=1, source_target_pairs={{0,8},{1,2},{2,1},{3,4},{4,3},{5,6},{6,5},{7,15},{8,0},{9,10},{10,... | collective-permute-start | bytes 49160 | tf_op jit(solution)/shard_map/ppermute | solution.py:352

commit v7 on v6

--- a/solution.py
+++ b/solution.py
@@ -120,29 +120,27 @@
                 rim_ref[rows, cols] = 0.0 - found[r] * open_face
 
 
-def first_send(
-    v_hbm, fp_hbm, send_hbm, coef_hbm, nb_hbm, bd_hbm,
-    v_ref, end_ref, fp_ref, send_ref, coef_ref, nb_ref, bd_ref, tr_ref, first_ref, second_ref, sems,
+def load_first(
+    v_hbm, fp_hbm, send_hbm, coef_hbm, nb_hbm, bd_hbm, v_ref, end_ref, fp_ref, send_ref, coef_ref, nb_ref, bd_ref, sems
 ):
-    face_dofs = fp_ref.shape[0] // 6
-    elements = v_ref.shape[1]
     half = end_ref.shape[0]
-    parts = chunks(elements)
-    pairs = [(fp_hbm, fp_ref)] + [(v_hbm.at[:, c], v_ref.at[:, c]) for c in parts]
-    pairs += [(send_hbm, send_ref), (coef_hbm, coef_ref), (nb_hbm, nb_ref), (bd_hbm, bd_ref)]
+    pairs = ((v_hbm, v_ref), (fp_hbm, fp_ref), (send_hbm, send_ref), (coef_hbm, coef_ref), (nb_hbm, nb_ref), (bd_hbm, bd_ref))
     copies = [pltpu.make_async_copy(a, b, sems.at[i]) for i, (a, b) in enumerate(pairs)]
     for copy in copies:
         copy.start()
     copies[0].wait()
+    end_ref[...] = v_ref[half:, :]
+    for copy in copies[1:]:
+        copy.wait()
+
+
+def first_send(v_ref, fp_ref, send_ref, tr_ref, first_ref, second_ref):
+    face_dofs = fp_ref.shape[0] // 6
+    elements = v_ref.shape[1]
     weights = left3(jnp.concatenate([face_rows(fp_ref, f, face_dofs) for f in range(2)], axis=0))
-    for i, c in enumerate(parts):
-        copies[1 + i].wait()
+    for c in chunks(elements):
         tr_ref[:, c] = dot3(weights, v_ref[:, c])
-        end_ref[:, c] = v_ref[half:, c]
-    copies[1 + len(parts)].wait()
     fill_outbound(tr_ref, send_ref, first_ref, second_ref, face_dofs, elements)
-    for copy in copies[2 + len(parts) :]:
-        copy.wait()
 
 
 def all_traces(v_ref, tr_ref, weights, traces):
@@ -169,7 +167,7 @@
     early = (len(parts) + 1) // 2
     for c in parts[:early]:
         fill_jump(traces, nb_ref, bd_ref, jump_ref, face_dofs, elements, c)
-    for copy in copies:
+    for copy in copies[:4]:
         copy.wait()
     lift_rows = [face_rows(liftt, f, face_dofs) for f in range(6)]
     apply3_ref[...] = left3(jnp.concatenate([stiff[...], jnp.concatenate(lift_rows, axis=0).T], axis=1))
@@ -180,29 +178,49 @@
     both = jnp.concatenate([inverse, dot(first_faces, inverse)], axis=0)
     ahead3_ref[...] = left3(dot(both, late))
     both = left3(both)
-    for i, c in enumerate(parts):
-        if early + i < len(parts):
-            fill_jump(traces, nb_ref, bd_ref, jump_ref, face_dofs, elements, parts[early + i])
+    def apply(c):
         values = jnp.concatenate([coef_ref[:, c] * v_ref[:, c], jump_ref[:, c]], axis=0)
-        part = rhs[:, c] - dot3(apply3_ref[...], values)
+        part_ref[:, c] = dot3(apply3_ref[...], values)
+
+    def subtract(c):
+        part = rhs[:, c] - part_ref[:, c]
         part_ref[:, c] = part
         ahead_ref[:, c] = dot3(both, part)
 
-
-def residual_step(
-    ahead_ref, v_ref, prev_ref, first_in, second_in, ahead3_ref, coef_ref, nb_ref, bd_ref, send_ref,
-    late_ref, dir_ref, end_ref, tr_ref, first_ref, second_ref,
-):
+    for i, c in enumerate(parts[early:]):
+        apply(parts[i])
+        if i == len(parts) - early - 1:
+            copies[4].wait()
+        fill_jump(traces, nb_ref, bd_ref, jump_ref, face_dofs, elements, c)
+    for i in range(len(parts)):
+        if len(parts) - early + i < len(parts):
+            apply(parts[len(parts) - early + i])
+        subtract(parts[i])
+
+
+def end_step(ahead_ref, v_ref, prev_ref, first_in, second_in, ahead3_ref, coef_ref, nb_ref, bd_ref, late_ref, end_ref):
     face_dofs = first_in.shape[0]
-    dofs, elements = dir_ref.shape
+    elements = v_ref.shape[1]
     half = prev_ref.shape[0]
+    dofs = v_ref.shape[0]
     rim_terms(first_in, second_in, nb_ref, bd_ref, late_ref, face_dofs, elements)
     late_ref[2 * face_dofs :, :] = time_jump_of(v_ref, prev_ref)
     for c in chunks(elements):
-        both = (ahead_ref[:, c] - dot3(ahead3_ref[...], late_ref[:, c])) * (1.0 / coef_ref[:, c])
-        dir_ref[:, c] = both[:dofs, :]
-        end_ref[:, c] = both[half:dofs, :]
-        tr_ref[:, c] = both[dofs:, :]
+        end_ref[:, c] = (ahead_ref[half:dofs, c] - dot3(ahead3_ref[half:dofs, :], late_ref[:, c])) * (1.0 / coef_ref[:, c])
+
+
+def rest_step(ahead_ref, late_ref, end_ref, ahead3_ref, coef_ref, send_ref, dir_ref, tr_ref, first_ref, second_ref):
+    face_dofs = first_ref.shape[0]
+    dofs, elements = dir_ref.shape
+    half = end_ref.shape[0]
+    weights = jnp.concatenate([ahead3_ref[dofs:, :], ahead3_ref[:half, :]], axis=0)
+    rim = 2 * face_dofs
+    for c in chunks(elements):
+        scale = 1.0 / coef_ref[:, c]
+        both = dot3(weights, late_ref[:, c])
+        tr_ref[:, c] = (ahead_ref[dofs:, c] - both[:rim, :]) * scale
+        dir_ref[:half, c] = (ahead_ref[:half, c] - both[rim:, :]) * scale
+        dir_ref[half:, c] = end_ref[:, c]
     fill_outbound(tr_ref, send_ref, first_ref, second_ref, face_dofs, elements)
 
 
@@ -355,17 +373,18 @@
     rim = 2 * face_dofs
     late = rim + half
     edge = (face_dofs, border)
-    v0, end0, fp, send, coefs, nb, bd, tr0, a0, b0 = call(
-        first_send,
-        "send0",
+    v0, end0, fp, send, coefs, nb, bd = call(
+        load_first,
+        "load",
         [(dofs, elements), (half, elements), (traces, dofs), (send.shape, send.dtype), coef_row.shape]
-        + [(neighbour.shape, neighbour.dtype), (boundary.shape, boundary.dtype), (rim, elements), edge, edge],
+        + [(neighbour.shape, neighbour.dtype), (boundary.shape, boundary.dtype)],
         (),
-        2 * rim * dofs * elements,
+        0,
         far=(initial[0], face_proj, send, coef_row, neighbour, boundary),
-        scratch=[pltpu.SemaphoreType.DMA((5 + len(chunks(elements)),))],
+        scratch=[pltpu.SemaphoreType.DMA((6,))],
     )
     prev0 = lax.ppermute(end0, "tm", cycle)
+    tr0, a0, b0 = call(first_send, "send0", [(rim, elements), edge, edge], (v0, fp, send), 2 * rim * dofs * elements)
     a0, b0 = halo(a0, b0)
     jump0, part0, ahead, fp3, apply3, late3, ahead3 = call(
         local_first,
@@ -377,14 +396,21 @@
         far=(source, stiffness, block_inverse, liftt, tlt),
         scratch=[(traces, elements), (dofs, elements), (dofs, dofs), (dofs, dofs), (traces, dofs), (half, dofs), pltpu.SemaphoreType.DMA((5,))],
     )
-    late0, direction, end, tr1, a1, b1 = call(
-        residual_step,
-        "residual",
-        [(late, elements), (dofs, elements), (half, elements), (rim, elements), edge, edge],
-        (ahead, v0, prev0, a0, b0, ahead3, coefs, nb, bd, send),
+    late0, end = call(
+        end_step,
+        "end",
+        [(late, elements), (half, elements)],
+        (ahead, v0, prev0, a0, b0, ahead3, coefs, nb, bd),
+        6 * half * dofs * elements,
+    )
+    prev1 = lax.ppermute(end, "tm", cycle)
+    direction, tr1, a1, b1 = call(
+        rest_step,
+        "rest",
+        [(dofs, elements), (rim, elements), edge, edge],
+        (ahead, late0, end, ahead3, coefs, send),
         6 * dofs * dofs * elements,
     )
-    prev1 = lax.ppermute(end, "tm", cycle)
     a1, b1 = halo(a1, b1)
     part1, border1, res, border0, group = call(
         local_second,

time: 31.8 us -> 30.7 us (0.965)
  Pallas kernels: 11.2 us -> 10.4 us
  blocking collectives: 12.1 us -> 11.7 us
    pallas_call x6 -> x8, Pallas kernels: 11.2 us -> 10.4 us  [call(): pl.pallas_call(body, name=name, out_shape=shapes, in_specs=[VM] * len(arg...]
    all_to_all x1, blocking collectives: 12.1 us -> 11.7 us  [on_device(): everyone = lax.all_to_all(sums, ('tm', 'space'), 0, 0, tiled=True)]
  transfers between devices with their start and end apart: 6 -> 6, of which waited for: 1 -> 0; matrix products, arithmetic and copies ran while one was open for 0% -> 0% of each run, Pallas kernels for 20% -> 22%
where the time goes in v7:
time: 30.7 us; the launch traced here: 30.5 us
  blocking collectives  11.7 us (38%)
  Pallas kernels  10.4 us (34%)
  starting transfers between devices  7.6 us (25%)
  between operations  0.73 us (2%)
    all_to_all x1, blocking collectives, on_device(): everyone = lax.all_to_all(sums, ('tm', 'space'), 0, 0, tiled=True)  11.7 us
    pallas_call x8, Pallas kernels, call(): pl.pallas_call(body, name=name, out_shape=shapes, in_specs=[VM] * len(arg...  10.4 us
    ppermute x4, starting transfers between devices, halo(): lax.ppermute(x, ('tm', 'space'), full_swaps(first, slabs, parts))  6.99 us
  transfers between devices with their start and end apart: 6, of which 0 were waited for; matrix products, arithmetic and copies ran while one was open for 0% of the time, Pallas kernels for 22%

profile of v7, /device:TPU:0, one launch (start us, length us, event | category | flops | bytes accessed | tf_op | source)
XLA Modules:
  0.0 30.5 jit_solution(13534325410373551415)
XLA Ops:
  0.6 1.1 %load.1 = (f32[128,1024]{1,0:T(8,128)S(1)}, f32[64,1024]{1,0:T(8,128)S(1)}, f32[192,128]{1,0:T(8,128)S(1)}, s32[2,128]{1,0:T(2,128)S(1)}, f32[1,1024]{1,0:T(1,12...) custom-call(f32[128,1024]{1,0:T(8,128)} %bitcast.15, f32[192,128]{1,0:T(8,128)} %fp_hbm.1, s32[2,128]{1,0:T(2,128)} %bitcast.20, ...), custom_call_target="tpu_custom_call" | custom-call | bytes 1615872 | tf_op jit(solution)/shard_map/load/pallas_call | solution.py:332
  1.8 0.5 %collective-permute-start = (f32[64,1024]{1,0:T(8,128)S(1)}, f32[64,1024]{1,0:T(8,128)S(1)}, u32[]{:S(2)}, u32[]{:S(2)}) collective-permute-start(f32[64,1024]{1,0:T(8,128)S(1)} %get-tuple-element.44), channel_id=1, source_target_pairs={{0,8},{8,16},{16,24},{24,0},{1,9},{9,17},{17,25},{25,1},{2,10},{10... | collective-permute-start | bytes 786440 | tf_op jit(solution)/shard_map/ppermute | solution.py:386
  2.3 0.4 %send0.1 = (f32[64,1024]{1,0:T(8,128)S(1)}, f32[32,128]{1,0:T(8,128)S(1)}, f32[32,128]{1,0:T(8,128)S(1)}) custom-call(f32[128,1024]{1,0:T(8,128)S(1)} %get-tuple-element.36.v_ref, f32[192,128]{1,0:T(8,128)S(1)} %get-tuple-element.37.fp_ref, s32[2,128]{1,0:T(2,128)S(1)} %get-tuple-element.38.send_ref), custom_call_target="tpu_custom_call" | custom-call | flops 16777216 | bytes 918528 | tf_op jit(solution)/shard_map/send0/pallas_call | solution.py:332
  2.7 2.6 %collective-permute-start.1 = (f32[32,128]{1,0:T(8,128)S(1)}, f32[32,128]{1,0:T(8,128)S(1)}, u32[]{:S(2)}, u32[]{:S(2)}) collective-permute-start(f32[32,128]{1,0:T(8,128)S(1)} %get-tuple-element.45), channel_id=1, source_target_pairs={{0,1},{1,0},{2,3},{3,2},{4,5},{5,4},{6,7},{7,6},{8,9},{9,8},{10,11... | collective-permute-start | bytes 49160 | tf_op jit(solution)/shard_map/ppermute | solution.py:370
  5.3 1.3 %collective-permute-start.2 = (f32[32,128]{1,0:T(8,128)S(1)}, f32[32,128]{1,0:T(8,128)S(1)}, u32[]{:S(2)}, u32[]{:S(2)}) collective-permute-start(f32[32,128]{1,0:T(8,128)S(1)} %get-tuple-element.46), channel_id=1, source_target_pairs={{0,8},{1,2},{2,1},{3,4},{4,3},{5,6},{6,5},{7,15},{8,0},{9,10},{10,... | collective-permute-start | bytes 49160 | tf_op jit(solution)/shard_map/ppermute | solution.py:370
  6.6 3.1 %local0.1 = (f32[192,1024]{1,0:T(8,128)S(1)}, f32[128,1024]{1,0:T(8,128)S(1)}, f32[192,1024]{1,0:T(8,128)S(1)}, bf16[128,384]{1,0:T(8,128)(2,1)S(1)}, bf16[128,9...) custom-call(f32[128,1024]{1,0:T(8,128)S(1)} %get-tuple-element.36.v_ref, ...), custom_call_target="tpu_custom_call" | custom-call | flops 301989888 | bytes 5001216 | tf_op jit(solution)/shard_map/local0/pallas_call | solution.py:332
  9.7 0.0 collective-permute-done.1.first_in
  9.8 0.0 collective-permute-done.2.second_in
  9.8 0.0 collective-permute-done.prev_ref
  9.8 0.6 %end.1 = (f32[128,1024]{1,0:T(8,128)S(1)}, f32[64,1024]{1,0:T(8,128)S(1)}) custom-call(f32[192,1024]{1,0:T(8,128)S(1)} %get-tuple-element.43.ahead_ref, f32[128,1024]{1,0:T(8,128)S(1)} %get-tuple-element.36.v_ref, f32[64,1024]{1,0:T(8,128)S(1)} %collective-permute-done.prev_ref, f32[32,128]{1,0:T(8,128)S(1)} %collective-permute-done.1.first_in, ...), custom_call_target="tpu_custom_call" | custom-call | flops 50331648 | bytes 2740224 | tf_op jit(solution)/shard_map/end/pallas_call | solution.py:332
  10.4 0.1 collective-permute-start.3
  10.4 0.5 %rest.1 = (f32[128,1024]{1,0:T(8,128)S(1)}, f32[64,1024]{1,0:T(8,128)S(1)}, f32[32,128]{1,0:T(8,128)S(1)}, f32[32,128]{1,0:T(8,128)S(1)}) custom-call(f32[192,1024]{1,0:T(8,128)S(1)} %get-tuple-element.43.ahead_ref, f32[128,1024]{1,0:T(8,128)S(1)} %get-tuple-element.48.late_ref.late0_ref, f32[64,1024]{1,0:T(8,128)S(1)} %get-tuple-element.49.end_ref, ...), custom_call_target="tpu_custom_call" | custom-call | flops 100663296 | bytes 2692096 | tf_op jit(solution)/shard_map/rest/pallas_call | solution.py:332
  10.9 2.8 %collective-permute-start.4 = (f32[32,128]{1,0:T(8,128)S(1)}, f32[32,128]{1,0:T(8,128)S(1)}, u32[]{:S(2)}, u32[]{:S(2)}) collective-permute-start(f32[32,128]{1,0:T(8,128)S(1)} %get-tuple-element.59), channel_id=1, source_target_pairs={{0,1},{1,0},{2,3},{3,2},{4,5},{5,4},{6,7},{7,6},{8,9},{9,8},{10,11... | collective-permute-start | bytes 49160 | tf_op jit(solution)/shard_map/ppermute | solution.py:370
  13.7 0.3 collective-permute-start.5
  14.0 2.6 %local1.1 = (f32[128,1024]{1,0:T(8,128)S(1)}, f32[64,1024]{1,0:T(8,128)S(1)}, f32[128,1024]{1,0:T(8,128)S(1)}, f32[64,1024]{1,0:T(8,128)S(1)}, f32[8,1024]{1,0:T(8,128)S(1)}) custom-call(f32[128,1024]{1,0:T(8,128)S(1)} %get-tuple-element.50.dir_ref, f32[64,1024]{1,0:T(8,128)S(1)} %get-tuple-element.51.tr_ref, f32[1,1024]{1,0:T(1,128)S(1)} %get-tuple-element.40.coef_ref, ...), custom_call_target="tpu_custom_call" | custom-call | flops 301989888 | bytes 5165056 | tf_op jit(solution)/shard_map/local1/pallas_call | solution.py:332
  16.6 0.0 collective-permute-done.4.first_in
  16.6 0.0 collective-permute-done.5.second_in
  16.6 0.0 collective-permute-done.3.prev_ref
  16.6 1.1 %image.1 = (f32[8,1024]{1,0:T(8,128)S(1)}, f32[32,128]{1,0:T(8,128)S(1)}) custom-call(f32[128,1024]{1,0:T(8,128)S(1)} %get-tuple-element.57.part_ref, f32[64,1024]{1,0:T(8,128)S(1)} %get-tuple-element.58.border_ref, f32[128,1024]{1,0:T(8,128)S(1)} %get-tuple-element.50.dir_ref, f32[64,1024]{1,0:T(8,128)S(1)} %collective-permute-done.3.prev_ref, ...), custom_call_target="tpu_custom_call" | custom-call | flops 100663296 | bytes 3244032 | tf_op jit(solution)/shard_map/image/pallas_call | solution.py:332
  17.8 11.7 %all_to_all.11 = f32[32,1,128]{2,1,0:T(1,128)S(1)} all-to-all(f32[32,1,128]{2,1,0:T(1,128)S(1)} %bitcast.14), channel_id=1, replica_groups=mesh['tm'=4,'space'=8] {'tm','space'}, dimensions={0} | all-to-all | bytes 32768 | tf_op jit(solution)/shard_map/all_to_all | solution.py:431
  29.5 1.0 %last.1 = (f32[128,1024]{1,0:T(8,128)}, f32[1,1024]{1,0:T(1,128)}, f32[1,128]{1,0:T(1,128)}) custom-call(f32[32,128]{1,0:T(8,128)S(1)} %bitcast.13, f32[8,1024]{1,0:T(8,128)S(1)} %get-tuple-element.65.coeff_ref, f32[128,1024]{1,0:T(8,128)S(1)} %get-tuple-element.36.v_ref, f32[128,1024]{1,0:T(8,128)S(1)} %get-tuple-element.50.dir_ref), custom_call_target="tpu_custom_call" | custom-call | flops 524288 | bytes 1626624 | tf_op jit(solution)/shard_map/last/pallas_call | solution.py:332
Async XLA Ops:
  1.8 8.0 %collective-permute-start = (f32[64,1024]{1,0:T(8,128)S(1)}, f32[64,1024]{1,0:T(8,128)S(1)}, u32[]{:S(2)}, u32[]{:S(2)}) collective-permute-start(f32[64,1024]{1,0:T(8,128)S(1)} %get-tuple-element.44), channel_id=1, source_target_pairs={{0,8},{8,16},{16,24},{24,0},{1,9},{9,17},{17,25},{25,1},{2,10},{10... | collective-permute-start | bytes 786440 | tf_op jit(solution)/shard_map/ppermute | solution.py:386
  2.7 7.0 %collective-permute-start.1 = (f32[32,128]{1,0:T(8,128)S(1)}, f32[32,128]{1,0:T(8,128)S(1)}, u32[]{:S(2)}, u32[]{:S(2)}) collective-permute-start(f32[32,128]{1,0:T(8,128)S(1)} %get-tuple-element.45), channel_id=1, source_target_pairs={{0,1},{1,0},{2,3},{3,2},{4,5},{5,4},{6,7},{7,6},{8,9},{9,8},{10,11... | collective-permute-start | bytes 49160 | tf_op jit(solution)/shard_map/ppermute | solution.py:370
  5.3 4.5 %collective-permute-start.2 = (f32[32,128]{1,0:T(8,128)S(1)}, f32[32,128]{1,0:T(8,128)S(1)}, u32[]{:S(2)}, u32[]{:S(2)}) collective-permute-start(f32[32,128]{1,0:T(8,128)S(1)} %get-tuple-element.46), channel_id=1, source_target_pairs={{0,8},{1,2},{2,1},{3,4},{4,3},{5,6},{6,5},{7,15},{8,0},{9,10},{10,... | collective-permute-start | bytes 49160 | tf_op jit(solution)/shard_map/ppermute | solution.py:370
  10.4 6.2 %collective-permute-start.3 = (f32[64,1024]{1,0:T(8,128)S(1)}, f32[64,1024]{1,0:T(8,128)S(1)}, u32[]{:S(2)}, u32[]{:S(2)}) collective-permute-start(f32[64,1024]{1,0:T(8,128)S(1)} %get-tuple-element.49.end_ref), channel_id=1, source_target_pairs={{0,8},{8,16},{16,24},{24,0},{1,9},{9,17},{17,25},{25,1},{2,10},{10... | collective-permute-start | bytes 786440 | tf_op jit(solution)/shard_map/ppermute | solution.py:406
  10.9 5.7 %collective-permute-start.4 = (f32[32,128]{1,0:T(8,128)S(1)}, f32[32,128]{1,0:T(8,128)S(1)}, u32[]{:S(2)}, u32[]{:S(2)}) collective-permute-start(f32[32,128]{1,0:T(8,128)S(1)} %get-tuple-element.59), channel_id=1, source_target_pairs={{0,1},{1,0},{2,3},{3,2},{4,5},{5,4},{6,7},{7,6},{8,9},{9,8},{10,11... | collective-permute-start | bytes 49160 | tf_op jit(solution)/shard_map/ppermute | solution.py:370
  13.7 2.9 %collective-permute-start.5 = (f32[32,128]{1,0:T(8,128)S(1)}, f32[32,128]{1,0:T(8,128)S(1)}, u32[]{:S(2)}, u32[]{:S(2)}) collective-permute-start(f32[32,128]{1,0:T(8,128)S(1)} %get-tuple-element.60), channel_id=1, source_target_pairs={{0,8},{1,2},{2,1},{3,4},{4,3},{5,6},{6,5},{7,15},{8,0},{9,10},{10,... | collective-permute-start | bytes 49160 | tf_op jit(solution)/shard_map/ppermute | solution.py:370

commit v8 on v7

--- a/solution.py
+++ b/solution.py
@@ -11,7 +11,8 @@
 SUBS = 8
 
 
-WIDE = 256
+WIDE = 512
+SELECTED = (2, 3)
 
 
 def dot(a, b):
@@ -78,10 +79,32 @@
             second_ref[rows, cols] = jnp.where(odd, upper[r], lower[r])
 
 
-def fill_jump(traces, nb_ref, bd_ref, jump_ref, face_dofs, elements, chunk):
+def thirds(x):
+    high = x.astype(jnp.bfloat16)
+    rest = x - high.astype(jnp.float32)
+    middle = rest.astype(jnp.bfloat16)
+    return jnp.concatenate([high, middle, (rest - middle.astype(jnp.float32)).astype(jnp.bfloat16)], axis=0)
+
+
+def fill_jump(traces, terms, nb_ref, bd_ref, jump_ref, face_dofs, elements, chunk):
     per_face = elements // LANES
+    width = chunk.stop - chunk.start
     for face in range(6):
         other = face ^ 1
+        if face in SELECTED:
+            columns = nb_ref[face : face + 1, chunk] - other * elements
+            block = 2 * LANES if elements % (2 * LANES) == 0 else LANES
+            number = lax.broadcasted_iota(jnp.int32, (block, width), 0).astype(jnp.float32).astype(jnp.bfloat16)
+            picks = []
+            for start in range(0, elements, block):
+                place = jnp.clip(columns - start, -1, block).astype(jnp.float32).astype(jnp.bfloat16)
+                picks.append(jnp.where(number == jnp.broadcast_to(place, (block, width)), jnp.bfloat16(1), jnp.bfloat16(0)))
+            at = SELECTED.index(other) * 3 * face_dofs
+            found = jnp.dot(terms[at : at + 3 * face_dofs, :], jnp.concatenate(picks, axis=0), preferred_element_type=jnp.float32)
+            found = (found[:face_dofs] + found[face_dofs : 2 * face_dofs]) + found[2 * face_dofs :]
+            rows = slice(face * face_dofs, (face + 1) * face_dofs)
+            jump_ref[rows, chunk] = traces[rows, chunk] - found * (1.0 - bd_ref[face : face + 1, chunk].astype(jnp.float32))
+            continue
 
         def tile_of(tile, r, other=other):
             return traces[other * face_dofs + r * SUBS : other * face_dofs + (r + 1) * SUBS, tile * LANES : (tile + 1) * LANES]
@@ -143,83 +166,69 @@
     fill_outbound(tr_ref, send_ref, first_ref, second_ref, face_dofs, elements)
 
 
-def all_traces(v_ref, tr_ref, weights, traces):
+def all_traces(v_ref, tr_ref, weights, traces, terms):
     known = tr_ref.shape[0]
+    face_dofs = traces.shape[0] // 6
     for c in chunks(v_ref.shape[1]):
         traces[:known, c] = tr_ref[:, c]
         traces[known:, c] = dot3(weights, v_ref[:, c])
+        for i, face in enumerate(SELECTED):
+            terms[3 * i * face_dofs : 3 * (i + 1) * face_dofs, c] = thirds(traces[face * face_dofs : (face + 1) * face_dofs, c])
 
 
 def local_first(
-    v_ref, tr_ref, coef_ref, fp_ref, nb_ref, bd_ref, rhs_hbm, stiff_hbm, inv_hbm, liftt_hbm, tlt_hbm,
-    jump_ref, part_ref, ahead_ref, fp3_ref, apply3_ref, late3_ref, ahead3_ref,
-    traces, rhs, stiff, inv, liftt, tlt, sems,
+    v_ref, tr_ref, coef_ref, fp_ref, nb_ref, bd_ref, stiff, inv, liftt, tlt, rhs,
+    jump_ref, part_ref, ahead_ref, fp3_ref, apply3_ref, rim3_ref, time3_ref, ahead_rim3_ref, ahead_time3_ref,
+    traces, terms,
 ):
     face_dofs = fp_ref.shape[0] // 6
     elements = v_ref.shape[1]
-    pairs = ((stiff_hbm, stiff), (liftt_hbm, liftt), (tlt_hbm, tlt), (inv_hbm, inv), (rhs_hbm, rhs))
-    copies = [pltpu.make_async_copy(a, b, sems.at[i]) for i, (a, b) in enumerate(pairs)]
-    for copy in copies:
-        copy.start()
     fp3_ref[...] = left3(jnp.concatenate([face_rows(fp_ref, f, face_dofs) for f in range(2, 6)], axis=0))
-    all_traces(v_ref, tr_ref, fp3_ref[...], traces)
-    parts = chunks(elements)
-    early = (len(parts) + 1) // 2
-    for c in parts[:early]:
-        fill_jump(traces, nb_ref, bd_ref, jump_ref, face_dofs, elements, c)
-    for copy in copies[:4]:
-        copy.wait()
+    all_traces(v_ref, tr_ref, fp3_ref[...], traces, terms)
     lift_rows = [face_rows(liftt, f, face_dofs) for f in range(6)]
     apply3_ref[...] = left3(jnp.concatenate([stiff[...], jnp.concatenate(lift_rows, axis=0).T], axis=1))
-    late = jnp.concatenate(lift_rows[:2] + [tlt[...]], axis=0).T
-    late3_ref[...] = left3(late)
+    rim, time = jnp.concatenate(lift_rows[:2], axis=0).T, tlt[...].T
+    rim3_ref[...] = left3(rim)
+    time3_ref[...] = left3(time)
     inverse = inv[...]
     first_faces = jnp.concatenate([face_rows(fp_ref, f, face_dofs) for f in range(2)], axis=0)
     both = jnp.concatenate([inverse, dot(first_faces, inverse)], axis=0)
-    ahead3_ref[...] = left3(dot(both, late))
+    ahead_rim3_ref[...] = left3(dot(both, rim))
+    ahead_time3_ref[...] = left3(dot(both, time))
     both = left3(both)
-    def apply(c):
+    for c in chunks(elements):
+        fill_jump(traces, terms, nb_ref, bd_ref, jump_ref, face_dofs, elements, c)
         values = jnp.concatenate([coef_ref[:, c] * v_ref[:, c], jump_ref[:, c]], axis=0)
-        part_ref[:, c] = dot3(apply3_ref[...], values)
-
-    def subtract(c):
-        part = rhs[:, c] - part_ref[:, c]
+        part = rhs[:, c] - dot3(apply3_ref[...], values)
         part_ref[:, c] = part
         ahead_ref[:, c] = dot3(both, part)
 
-    for i, c in enumerate(parts[early:]):
-        apply(parts[i])
-        if i == len(parts) - early - 1:
-            copies[4].wait()
-        fill_jump(traces, nb_ref, bd_ref, jump_ref, face_dofs, elements, c)
-    for i in range(len(parts)):
-        if len(parts) - early + i < len(parts):
-            apply(parts[len(parts) - early + i])
-        subtract(parts[i])
-
-
-def end_step(ahead_ref, v_ref, prev_ref, first_in, second_in, ahead3_ref, coef_ref, nb_ref, bd_ref, late_ref, end_ref):
-    face_dofs = first_in.shape[0]
-    elements = v_ref.shape[1]
+
+def edge_first(ahead_ref, first_in, second_in, ahead_rim3_ref, nb_ref, bd_ref, near_ref, rim_ref):
+    rim_terms(first_in, second_in, nb_ref, bd_ref, rim_ref, first_in.shape[0], near_ref.shape[1])
+    for c in chunks(near_ref.shape[1]):
+        near_ref[:, c] = ahead_ref[:, c] - dot3(ahead_rim3_ref[...], rim_ref[:, c])
+
+
+def end_step(near_ref, v_ref, prev_ref, ahead_time3_ref, coef_ref, time_ref, end_ref):
+    dofs, elements = v_ref.shape
     half = prev_ref.shape[0]
-    dofs = v_ref.shape[0]
-    rim_terms(first_in, second_in, nb_ref, bd_ref, late_ref, face_dofs, elements)
-    late_ref[2 * face_dofs :, :] = time_jump_of(v_ref, prev_ref)
-    for c in chunks(elements):
-        end_ref[:, c] = (ahead_ref[half:dofs, c] - dot3(ahead3_ref[half:dofs, :], late_ref[:, c])) * (1.0 / coef_ref[:, c])
-
-
-def rest_step(ahead_ref, late_ref, end_ref, ahead3_ref, coef_ref, send_ref, dir_ref, tr_ref, first_ref, second_ref):
+    time_ref[...] = time_jump_of(v_ref, prev_ref)
+    for c in chunks(elements):
+        end_ref[:, c] = (near_ref[half:dofs, c] - dot3(ahead_time3_ref[half:dofs, :], time_ref[:, c])) * (1.0 / coef_ref[:, c])
+
+
+def rest_step(near_ref, time_ref, end_ref, ahead_time3_ref, coef_ref, send_ref, dir_ref, tr_ref, first_ref, second_ref):
     face_dofs = first_ref.shape[0]
     dofs, elements = dir_ref.shape
     half = end_ref.shape[0]
-    weights = jnp.concatenate([ahead3_ref[dofs:, :], ahead3_ref[:half, :]], axis=0)
+    weights = jnp.concatenate([ahead_time3_ref[dofs:, :], ahead_time3_ref[:half, :]], axis=0)
     rim = 2 * face_dofs
     for c in chunks(elements):
         scale = 1.0 / coef_ref[:, c]
-        both = dot3(weights, late_ref[:, c])
-        tr_ref[:, c] = (ahead_ref[dofs:, c] - both[:rim, :]) * scale
-        dir_ref[:half, c] = (ahead_ref[:half, c] - both[rim:, :]) * scale
+        both = dot3(weights, time_ref[:, c])
+        tr_ref[:, c] = (near_ref[dofs:, c] - both[:rim, :]) * scale
+        dir_ref[:half, c] = (near_ref[:half, c] - both[rim:, :]) * scale
         dir_ref[half:, c] = end_ref[:, c]
     fill_outbound(tr_ref, send_ref, first_ref, second_ref, face_dofs, elements)
 
@@ -240,55 +249,62 @@
     return jnp.where(bend > 0.0, -slope / jnp.where(bend > 0.0, bend, 1.0), 0.0)
 
 
+def group_sums(j0, j1):
+    bend, slope = 0.5 * column_sum(j1 * j1), 0.5 * column_sum(j0 * j1)
+    best = lowest(slope, bend)
+    j = j0 + best * j1
+    return [0.5 * column_sum(j * j), slope, bend, best]
+
+
+def group_at(group, s):
+    base, slope, bend, best = group
+    off = s - best
+    return base + off * (2.0 * (slope + best * bend) + off * bend)
+
+
 def local_second(
-    dir_ref, tr_ref, coef_ref, nb_ref, bd_ref, fp3_ref, apply3_ref, late3_ref, part_ref, late_ref, jump0_ref,
-    image_ref, border_ref, res_ref, border0_ref, group_ref, traces, jump,
+    dir_ref, tr_ref, coef_ref, nb_ref, bd_ref, fp3_ref, apply3_ref, rim3_ref, time3_ref, part_ref, rim_ref, time_ref, jump0_ref,
+    image_ref, border_ref, res_ref, border0_ref, group_ref, traces, terms, jump,
 ):
     elements = dir_ref.shape[1]
     face_dofs = jump.shape[0] // 6
     rim = 2 * face_dofs
-    all_traces(dir_ref, tr_ref, fp3_ref[...], traces)
-    for c in chunks(elements):
-        fill_jump(traces, nb_ref, bd_ref, jump, face_dofs, elements, c)
+    all_traces(dir_ref, tr_ref, fp3_ref[...], traces, terms)
+    for c in chunks(elements):
+        fill_jump(traces, terms, nb_ref, bd_ref, jump, face_dofs, elements, c)
         values = jnp.concatenate([coef_ref[:, c] * dir_ref[:, c], jump[:, c]], axis=0)
         image_ref[:, c] = dot3(apply3_ref[...], values)
-        res_ref[:, c] = part_ref[:, c] - dot3(late3_ref[...], late_ref[:, c])
+        res_ref[:, c] = part_ref[:, c] - dot3(rim3_ref[...], rim_ref[:, c]) - dot3(time3_ref[...], time_ref[:, c])
         border_ref[:, c] = jump[:rim, c]
-        border0_ref[:, c] = jump0_ref[:rim, c] + late_ref[:rim, c]
-        j0, j1 = jump0_ref[rim:, c], jump[rim:, c]
-        bend, slope = 0.5 * column_sum(j1 * j1), 0.5 * column_sum(j0 * j1)
-        best = lowest(slope, bend)
-        j = j0 + best * j1
-        base = 0.5 * column_sum(j * j)
-        group_ref[:, c] = jnp.concatenate([base, slope, bend, best, base, base, base, base], axis=0)
-
-
-def image_step(
-    part_ref, border_ref, dir_ref, prev_ref, first_in, second_in, late3_ref, nb_ref, bd_ref, res_ref, border0_ref, late0_ref, group_ref,
-    coeff_ref, sums_ref, late,
-):
-    face_dofs = first_in.shape[0]
+        border0_ref[:, c] = jump0_ref[:rim, c] + rim_ref[:, c]
+        group_ref[:, c] = jnp.concatenate(group_sums(jump0_ref[rim:, c], jump[rim:, c]) * 2, axis=0)
+
+
+def edge_second(part_ref, border_ref, first_in, second_in, rim3_ref, nb_ref, bd_ref, border0_ref, group_ref, near_ref, groups_ref, rim):
+    elements = part_ref.shape[1]
+    rim_terms(first_in, second_in, nb_ref, bd_ref, rim, first_in.shape[0], elements)
+    for c in chunks(elements):
+        near_ref[:, c] = part_ref[:, c] + dot3(rim3_ref[...], rim[:, c])
+        sums = group_sums(border0_ref[:, c], border_ref[:, c] + rim[:, c])
+        groups_ref[:, c] = jnp.concatenate([group_ref[:4, c]] + sums, axis=0)
+
+
+def image_step(near_ref, dir_ref, prev_ref, time3_ref, res_ref, time0_ref, group_ref, coeff_ref, sums_ref, time):
     elements = dir_ref.shape[1]
-    rim = 2 * face_dofs
-    rim_terms(first_in, second_in, nb_ref, bd_ref, late, face_dofs, elements)
-    late[rim:, :] = time_jump_of(dir_ref, prev_ref)
     crosses, squares = [], []
-    for c in chunks(elements):
-        img = part_ref[:, c] + dot3(late3_ref[...], late[:, c])
+    time[...] = time_jump_of(dir_ref, prev_ref)
+    for c in chunks(elements):
+        t0, t1 = time0_ref[:, c], time[:, c]
+        img = near_ref[:, c] + dot3(time3_ref[...], t1)
         res = res_ref[:, c]
         cross, square = column_sum(res * img), column_sum(img * img)
-        j0, j1 = border0_ref[:, c], border_ref[:, c] + late[:rim, c]
-        t0, t1 = late0_ref[rim:, c], late[rim:, c]
-        g_base, g_slope, g_bend, g_best = (group_ref[i : i + 1, c] for i in range(4))
-        bend = square + 0.5 * column_sum(j1 * j1) + column_sum(t1 * t1) + g_bend
-        slope = 0.5 * column_sum(j0 * j1) + column_sum(t0 * t1) + g_slope - cross
+        groups = [[group_ref[i : i + 1, c] for i in range(k, k + 4)] for k in (0, 4)]
+        bend = square + column_sum(t1 * t1) + groups[0][2] + groups[1][2]
+        slope = column_sum(t0 * t1) + groups[0][1] + groups[1][1] - cross
         best = lowest(slope, bend)
         r = res - best * img
-        j = j0 + best * j1
         t = t0 + best * t1
-        off = best - g_best
-        group = g_base + off * (2.0 * (g_slope + g_best * g_bend) + off * g_bend)
-        base = column_sum(r * r) + 0.5 * column_sum(j * j) + column_sum(t * t) + group
+        base = column_sum(r * r) + column_sum(t * t) + group_at(groups[0], best) + group_at(groups[1], best)
         tilt = slope + best * bend
         coeff_ref[:, c] = jnp.concatenate([base, tilt, bend, best, best, best, best, best], axis=0)
         crosses.append(cross)
@@ -325,13 +341,12 @@
 F32, BF16 = jnp.float32, jnp.bfloat16
 
 
-def call(body, name, outs, args, flops, far=(), scratch=()):
+def call(body, outs, args, flops, far=(), scratch=()):
     shapes = [jax.ShapeDtypeStruct(*s) if isinstance(s[0], tuple) else jax.ShapeDtypeStruct(s, F32) for s in outs]
     far = tuple(pltpu.with_memory_space_constraint(x, pltpu.HBM) for x in far)
     moved = sum(4 * a.size for a in args + far) + sum(4 * s.size for s in shapes)
     return pl.pallas_call(
         body,
-        name=name,
         out_shape=shapes,
         in_specs=[VM] * len(args) + [HB] * len(far),
         out_specs=[VM] * len(outs),
@@ -368,70 +383,75 @@
 
     def halo(a, b):
         swap = lambda x, first: lax.ppermute(x, ("tm", "space"), full_swaps(first, slabs, parts))
-        return swap(a, 0), swap(b, 1)
+        even = swap(a, 0)
+        odd = swap(b, 1)
+        return even, odd
 
     rim = 2 * face_dofs
-    late = rim + half
     edge = (face_dofs, border)
+    terms = pltpu.VMEM((3 * face_dofs * len(SELECTED), elements), BF16)
     v0, end0, fp, send, coefs, nb, bd = call(
         load_first,
-        "load",
         [(dofs, elements), (half, elements), (traces, dofs), (send.shape, send.dtype), coef_row.shape]
         + [(neighbour.shape, neighbour.dtype), (boundary.shape, boundary.dtype)],
         (),
-        0,
+        2 * 10**9,
         far=(initial[0], face_proj, send, coef_row, neighbour, boundary),
         scratch=[pltpu.SemaphoreType.DMA((6,))],
     )
     prev0 = lax.ppermute(end0, "tm", cycle)
-    tr0, a0, b0 = call(first_send, "send0", [(rim, elements), edge, edge], (v0, fp, send), 2 * rim * dofs * elements)
+    tr0, a0, b0 = call(first_send, [(rim, elements), edge, edge], (v0, fp, send), 2 * 10**9)
     a0, b0 = halo(a0, b0)
-    jump0, part0, ahead, fp3, apply3, late3, ahead3 = call(
+    jump0, part0, ahead, fp3, apply3, rim3, time3, ahead_rim3, ahead_time3 = call(
         local_first,
-        "local0",
         [(traces, elements), (dofs, elements), (dofs + rim, elements), ((traces - rim, 3 * dofs), BF16)]
-        + [((dofs, 3 * (dofs + traces)), BF16), ((dofs, 3 * late), BF16), ((dofs + rim, 3 * late), BF16)],
-        (v0, tr0, coefs, fp, nb, bd),
+        + [((dofs, 3 * (dofs + traces)), BF16), ((dofs, 3 * rim), BF16), ((dofs, 3 * half), BF16)]
+        + [((dofs + rim, 3 * rim), BF16), ((dofs + rim, 3 * half), BF16)],
+        (v0, tr0, coefs, fp, nb, bd, stiffness, block_inverse, liftt, tlt, source),
         12 * traces * dofs * elements,
-        far=(source, stiffness, block_inverse, liftt, tlt),
-        scratch=[(traces, elements), (dofs, elements), (dofs, dofs), (dofs, dofs), (traces, dofs), (half, dofs), pltpu.SemaphoreType.DMA((5,))],
-    )
-    late0, end = call(
-        end_step,
-        "end",
-        [(late, elements), (half, elements)],
-        (ahead, v0, prev0, a0, b0, ahead3, coefs, nb, bd),
-        6 * half * dofs * elements,
+        scratch=[(traces, elements), terms],
+    )
+    near0, rim0 = call(
+        edge_first,
+        [(dofs + rim, elements), (rim, elements)],
+        (ahead, a0, b0, ahead_rim3, nb, bd),
+        6 * dofs * dofs * elements,
+    )
+    time0, end = call(
+        end_step, [(half, elements), (half, elements)], (near0, v0, prev0, ahead_time3, coefs), 6 * half * half * elements
     )
     prev1 = lax.ppermute(end, "tm", cycle)
     direction, tr1, a1, b1 = call(
         rest_step,
-        "rest",
         [(dofs, elements), (rim, elements), edge, edge],
-        (ahead, late0, end, ahead3, coefs, send),
-        6 * dofs * dofs * elements,
+        (near0, time0, end, ahead_time3, coefs, send),
+        6 * dofs * half * elements,
     )
     a1, b1 = halo(a1, b1)
     part1, border1, res, border0, group = call(
         local_second,
-        "local1",
         [(dofs, elements), (rim, elements), (dofs, elements), (rim, elements), (SUBS, elements)],
-        (direction, tr1, coefs, nb, bd, fp3, apply3, late3, part0, late0, jump0),
+        (direction, tr1, coefs, nb, bd, fp3, apply3, rim3, time3, part0, rim0, time0, jump0),
         12 * traces * dofs * elements,
-        scratch=[(traces, elements), (traces, elements)],
+        scratch=[(traces, elements), terms, (traces, elements)],
+    )
+    near1, groups = call(
+        edge_second,
+        [(dofs, elements), (SUBS, elements)],
+        (part1, border1, a1, b1, rim3, nb, bd, border0, group),
+        6 * dofs * rim * elements,
+        scratch=[(rim, elements)],
     )
     coeffs, sums = call(
         image_step,
-        "image",
         [(SUBS, elements), (devices, LANES)],
-        (part1, border1, direction, prev1, a1, b1, late3, nb, bd, res, border0, late0, group),
-        6 * dofs * dofs * elements,
-        scratch=[(late, elements)],
+        (near1, direction, prev1, time3, res, time0, groups),
+        6 * dofs * half * elements,
+        scratch=[(half, elements)],
     )
     everyone = lax.all_to_all(sums, ("tm", "space"), 0, 0, tiled=True)
     smoothed, indicator, estimate = call(
         functools.partial(last_step, float(elements * devices)),
-        "last",
         [(dofs, elements), (1, elements), (1, LANES)],
         (everyone, coeffs, v0, direction),
         4 * dofs * elements,

time: 30.7 us -> 30.8 us (level)
  blocking collectives: 11.7 us -> 12.4 us
  Pallas kernels: 10.4 us -> 9.81 us
    all_to_all x1, blocking collectives: 11.7 us -> 12.4 us  [on_device(): everyone = lax.all_to_all(sums, ('tm', 'space'), 0, 0, tiled=True)]
    pallas_call x8 -> x10, Pallas kernels: 10.4 us -> 9.81 us  [call(): pl.pallas_call(body, out_shape=shapes, in_specs=[VM] * len(args) + [HB] *...]
where the time goes in v8:
time: 30.8 us; the launch traced here: 30.7 us
  blocking collectives  12.4 us (40%)
  Pallas kernels  9.81 us (32%)
  starting transfers between devices  7.64 us (25%)
  between operations  0.77 us (2%)
    all_to_all x1, blocking collectives, on_device(): everyone = lax.all_to_all(sums, ('tm', 'space'), 0, 0, tiled=True)  12.4 us
    pallas_call x10, Pallas kernels, call(): pl.pallas_call(body, out_shape=shapes, in_specs=[VM] * len(args) + [HB] *...  9.81 us
    ppermute x4, starting transfers between devices, halo(): lax.ppermute(x, ('tm', 'space'), full_swaps(first, slabs, parts))  7.03 us
  transfers between devices with their start and end apart: 6, of which 0 were waited for; matrix products, arithmetic and copies ran while one was open for 0% of the time, Pallas kernels for 22%

profile of v8, /device:TPU:0, one launch (start us, length us, event | category | flops | bytes accessed | tf_op | source)
XLA Modules:
  0.0 30.7 jit_solution(9175242210398481474)
XLA Ops:
  0.6 1.1 %shard_map.130 = (f32[128,1024]{1,0:T(8,128)S(1)}, f32[64,1024]{1,0:T(8,128)S(1)}, f32[192,128]{1,0:T(8,128)S(1)}, s32[2,128]{1,0:T(2,128)S(1)}, f32[1,1024]{1,0...) custom-call(f32[128,1024]{1,0:T(8,128)} %bitcast.18, f32[192,128]{1,0:T(8,128)} %fp_hbm.1, ...), custom_call_target="tpu_custom_call" | custom-call | flops 2000000000 | bytes 1615872 | tf_op jit(solution)/shard_map/pallas_call | solution.py:348
  1.8 0.5 %collective-permute-start.2 = (f32[64,1024]{1,0:T(8,128)S(1)}, f32[64,1024]{1,0:T(8,128)S(1)}, u32[]{:S(2)}, u32[]{:S(2)}) collective-permute-start(f32[64,1024]{1,0:T(8,128)S(1)} %get-tuple-element.54), channel_id=1, source_target_pairs={{0,8},{8,16},{16,24},{24,0},{1,9},{9,17},{17,25},{25,1},{2,10},{10... | collective-permute-start | bytes 786440 | tf_op jit(solution)/shard_map/ppermute | solution.py:402
  2.3 0.0 copy-start
  2.3 0.0 copy-start.1
  2.3 0.0 copy-start.2
  2.3 0.0 copy-start.3
  2.3 0.0 copy-start.4
  2.3 0.4 %shard_map.131 = (f32[64,1024]{1,0:T(8,128)S(1)}, f32[32,128]{1,0:T(8,128)S(1)}, f32[32,128]{1,0:T(8,128)S(1)}) custom-call(f32[128,1024]{1,0:T(8,128)S(1)} %get-tuple-element.42.v_ref, f32[192,128]{1,0:T(8,128)S(1)} %get-tuple-element.43.fp_ref, s32[2,128]{1,0:T(2,128)S(1)} %get-tuple-element.44.send_ref), custom_call_target="tpu_custom_call" | custom-call | flops 2000000000 | bytes 918528 | tf_op jit(solution)/shard_map/pallas_call | solution.py:348
  2.8 2.6 %collective-permute-start = (f32[32,128]{1,0:T(8,128)S(1)}, f32[32,128]{1,0:T(8,128)S(1)}, u32[]{:S(2)}, u32[]{:S(2)}) collective-permute-start(f32[32,128]{1,0:T(8,128)S(1)} %get-tuple-element.50), channel_id=1, source_target_pairs={{0,1},{1,0},{2,3},{3,2},{4,5},{5,4},{6,7},{7,6},{8,9},{9,8},{10,11... | collective-permute-start | bytes 49160 | tf_op jit(solution)/shard_map/ppermute | solution.py:385
  5.4 1.3 %collective-permute-start.1 = (f32[32,128]{1,0:T(8,128)S(1)}, f32[32,128]{1,0:T(8,128)S(1)}, u32[]{:S(2)}, u32[]{:S(2)}) collective-permute-start(f32[32,128]{1,0:T(8,128)S(1)} %get-tuple-element.51), channel_id=1, source_target_pairs={{0,8},{1,2},{2,1},{3,4},{4,3},{5,6},{6,5},{7,15},{8,0},{9,10},{10,... | collective-permute-start | bytes 49160 | tf_op jit(solution)/shard_map/ppermute | solution.py:385
  6.7 0.0 copy-done
  6.7 0.0 copy-done.1
  6.7 0.0 copy-done.2
  6.7 0.0 copy-done.3
  6.7 0.0 copy-done.4
  6.7 2.6 %shard_map.132 = (f32[192,1024]{1,0:T(8,128)S(1)}, f32[128,1024]{1,0:T(8,128)S(1)}, f32[192,1024]{1,0:T(8,128)S(1)}, bf16[128,384]{1,0:T(8,128)(2,1)S(1)}, bf16[...) custom-call(f32[128,1024]{1,0:T(8,128)S(1)} %get-tuple-element.42.v_, ...), custom_call_target="tpu_custom_call" | custom-call | flops 301989888 | bytes 5001216 | tf_op jit(solution)/shard_map/pallas_call | solution.py:348
  9.3 0.0 collective-permute-done.first_in
  9.3 0.0 collective-permute-done.1.second_in
  9.3 0.6 %shard_map.133 = (f32[192,1024]{1,0:T(8,128)S(1)}, f32[64,1024]{1,0:T(8,128)S(1)}) custom-call(f32[192,1024]{1,0:T(8,128)S(1)} %get-tuple-element.49.ahead_ref, f32[32,128]{1,0:T(8,128)S(1)} %collective-permute-done.first_in, f32[32,128]{1,0:T(8,128)S(1)} %collective-permute-done.1.second_in, bf16[192,192]{1,0:T(8,128)(2,1)S(1)} %get-tuple-element.52.ahead_rim3_ref, ...), custom_call_target="tpu_custom_call" | custom-call | flops 100663296 | bytes 2064384 | tf_op jit(solution)/shard_map/pallas_call | solution.py:348
  9.9 0.0 collective-permute-done.2.prev_ref
  9.9 0.2 shard_map.134
  10.1 0.1 collective-permute-start.5
  10.2 0.4 %shard_map.135 = (f32[128,1024]{1,0:T(8,128)S(1)}, f32[64,1024]{1,0:T(8,128)S(1)}, f32[32,128]{1,0:T(8,128)S(1)}, f32[32,128]{1,0:T(8,128)S(1)}) custom-call(f32[192,1024]{1,0:T(8,128)S(1)} %get-tuple-element.53.near_ref, f32[64,1024]{1,0:T(8,128)S(1)} %get-tuple-element.56.time_ref.time0_ref, f32[64,1024]{1,0:T(8,128)S(1)} %get-tuple-element.57.end_ref, ...), custom_call_target="tpu_custom_call" | custom-call | flops 50331648 | bytes 2282496 | tf_op jit(solution)/shard_map/pallas_call | solution.py:348
  10.6 2.8 %collective-permute-start.3 = (f32[32,128]{1,0:T(8,128)S(1)}, f32[32,128]{1,0:T(8,128)S(1)}, u32[]{:S(2)}, u32[]{:S(2)}) collective-permute-start(f32[32,128]{1,0:T(8,128)S(1)} %get-tuple-element.69), channel_id=1, source_target_pairs={{0,1},{1,0},{2,3},{3,2},{4,5},{5,4},{6,7},{7,6},{8,9},{9,8},{10,11... | collective-permute-start | bytes 49160 | tf_op jit(solution)/shard_map/ppermute | solution.py:385
  13.4 0.3 %collective-permute-start.4 = (f32[32,128]{1,0:T(8,128)S(1)}, f32[32,128]{1,0:T(8,128)S(1)}, u32[]{:S(2)}, u32[]{:S(2)}) collective-permute-start(f32[32,128]{1,0:T(8,128)S(1)} %get-tuple-element.70), channel_id=1, source_target_pairs={{0,8},{1,2},{2,1},{3,4},{4,3},{5,6},{6,5},{7,15},{8,0},{9,10},{10,... | collective-permute-start | bytes 49160 | tf_op jit(solution)/shard_map/ppermute | solution.py:385
  13.8 2.1 %shard_map.136 = (f32[128,1024]{1,0:T(8,128)S(1)}, f32[64,1024]{1,0:T(8,128)S(1)}, f32[128,1024]{1,0:T(8,128)S(1)}, f32[64,1024]{1,0:T(8,128)S(1)}, f32[8,1024]{1,0:T(8,128)S(1)}) custom-call(f32[128,1024]{1,0:T(8,128)S(1)} %get-tuple-element.58.dir_ref, f32[64,1024]{1,0:T(8,128)S(1)} %get-tuple-element.59.tr_ref, f32[1,1024]{1,0:T(1,128)S(1)} %get-tuple-element.46.coef_ref, ...), custom_call_target="tpu_custom_call" | custom-call | flops 301989888 | bytes 5165056 | tf_op jit(solution)/shard_map/pallas_call | solution.py:348
  15.9 0.0 collective-permute-done.3.first_in
  15.9 0.0 collective-permute-done.4.second_in
  15.9 0.6 %shard_map.137 = (f32[128,1024]{1,0:T(8,128)S(1)}, f32[8,1024]{1,0:T(8,128)S(1)}) custom-call(f32[128,1024]{1,0:T(8,128)S(1)} %get-tuple-element.67.part_ref, f32[64,1024]{1,0:T(8,128)S(1)} %get-tuple-element.68.border_ref, f32[32,128]{1,0:T(8,128)S(1)} %collective-permute-done.3.first_in, f32[32,128]{1,0:T(8,128)S(1)} %collective-permute-done.4.second_in, ...), custom_call_target="tpu_custom_call" | custom-call | flops 50331648 | bytes 1818624 | tf_op jit(solution)/shard_map/pallas_call | solution.py:348
  16.5 0.0 collective-permute-done.5.prev_ref
  16.5 0.7 %shard_map.138 = (f32[8,1024]{1,0:T(8,128)S(1)}, f32[32,128]{1,0:T(8,128)S(1)}) custom-call(f32[128,1024]{1,0:T(8,128)S(1)} %get-tuple-element.73.near_ref, f32[128,1024]{1,0:T(8,128)S(1)} %get-tuple-element.58.dir_ref, f32[64,1024]{1,0:T(8,128)S(1)} %collective-permute-done.5.prev_ref, bf16[128,192]{1,0:T(8,128)(2,1)S(1)} %get-tuple-element.63.time3_ref, ...), custom_call_target="tpu_custom_call" | custom-call | flops 50331648 | bytes 2277376 | tf_op jit(solution)/shard_map/pallas_call | solution.py:348
  17.2 12.4 %all_to_all.11 = f32[32,1,128]{2,1,0:T(1,128)S(1)} all-to-all(f32[32,1,128]{2,1,0:T(1,128)S(1)} %bitcast.17), channel_id=1, replica_groups=mesh['tm'=4,'space'=8] {'tm','space'}, dimensions={0} | all-to-all | bytes 32768 | tf_op jit(solution)/shard_map/all_to_all | solution.py:452
  29.6 1.0 %shard_map.139 = (f32[128,1024]{1,0:T(8,128)}, f32[1,1024]{1,0:T(1,128)}, f32[1,128]{1,0:T(1,128)}) custom-call(f32[32,128]{1,0:T(8,128)S(1)} %bitcast.15, f32[8,1024]{1,0:T(8,128)S(1)} %get-tuple-element.77.coeff_ref, f32[128,1024]{1,0:T(8,128)S(1)} %get-tuple-element.42.v_ref, f32[128,1024]{1,0:T(8,128)S(1)} %get-tuple-element.58.dir_ref), custom_call_target="tpu_custom_call" | custom-call | flops 524288 | bytes 1626624 | tf_op jit(solution)/shard_map/pallas_call | solution.py:348
Async XLA Ops:
  1.8 8.2 %collective-permute-start.2 = (f32[64,1024]{1,0:T(8,128)S(1)}, f32[64,1024]{1,0:T(8,128)S(1)}, u32[]{:S(2)}, u32[]{:S(2)}) collective-permute-start(f32[64,1024]{1,0:T(8,128)S(1)} %get-tuple-element.54), channel_id=1, source_target_pairs={{0,8},{8,16},{16,24},{24,0},{1,9},{9,17},{17,25},{25,1},{2,10},{10... | collective-permute-start | bytes 786440 | tf_op jit(solution)/shard_map/ppermute | solution.py:402
  2.3 4.4 %copy-start = (f32[1,128,1024]{2,1,0:T(8,128)S(1)}, f32[1,128,1024]{2,1,0:T(8,128)}, u32[]{:S(2)}) copy-start(f32[1,128,1024]{2,1,0:T(8,128)} %param.12) | copy-start | bytes 1572868
  2.3 4.4 %copy-start.1 = (f32[128,192]{0,1:T(8,128)S(1)}, f32[128,192]{0,1:T(8,128)}, u32[]{:S(2)}) copy-start(f32[128,192]{0,1:T(8,128)} %param.17) | copy-start | bytes 294916
  2.3 4.4 %copy-start.2 = (f32[128,128]{1,0:T(8,128)S(1)}, f32[128,128]{1,0:T(8,128)}, u32[]{:S(2)}) copy-start(f32[128,128]{1,0:T(8,128)} %stiff.1) | copy-start | bytes 196612
  2.3 4.4 %copy-start.3 = (f32[128,128]{1,0:T(8,128)S(1)}, f32[128,128]{1,0:T(8,128)}, u32[]{:S(2)}) copy-start(f32[128,128]{1,0:T(8,128)} %inv.1) | copy-start | bytes 196612
  2.3 4.4 %copy-start.4 = (f32[128,64]{0,1:T(8,128)S(1)}, f32[128,64]{0,1:T(8,128)}, u32[]{:S(2)}) copy-start(f32[128,64]{0,1:T(8,128)} %param.18) | copy-start | bytes 98308
  2.8 6.5 %collective-permute-start = (f32[32,128]{1,0:T(8,128)S(1)}, f32[32,128]{1,0:T(8,128)S(1)}, u32[]{:S(2)}, u32[]{:S(2)}) collective-permute-start(f32[32,128]{1,0:T(8,128)S(1)} %get-tuple-element.50), channel_id=1, source_target_pairs={{0,1},{1,0},{2,3},{3,2},{4,5},{5,4},{6,7},{7,6},{8,9},{9,8},{10,11... | collective-permute-start | bytes 49160 | tf_op jit(solution)/shard_map/ppermute | solution.py:385
  5.4 3.9 %collective-permute-start.1 = (f32[32,128]{1,0:T(8,128)S(1)}, f32[32,128]{1,0:T(8,128)S(1)}, u32[]{:S(2)}, u32[]{:S(2)}) collective-permute-start(f32[32,128]{1,0:T(8,128)S(1)} %get-tuple-element.51), channel_id=1, source_target_pairs={{0,8},{1,2},{2,1},{3,4},{4,3},{5,6},{6,5},{7,15},{8,0},{9,10},{10,... | collective-permute-start | bytes 49160 | tf_op jit(solution)/shard_map/ppermute | solution.py:385
  10.1 6.4 %collective-permute-start.5 = (f32[64,1024]{1,0:T(8,128)S(1)}, f32[64,1024]{1,0:T(8,128)S(1)}, u32[]{:S(2)}, u32[]{:S(2)}) collective-permute-start(f32[64,1024]{1,0:T(8,128)S(1)} %get-tuple-element.57.end_ref), channel_id=1, source_target_pairs={{0,8},{8,16},{16,24},{24,0},{1,9},{9,17},{17,25},{25,1},{2,10},{10... | collective-permute-start | bytes 786440 | tf_op jit(solution)/shard_map/ppermute | solution.py:423
  10.6 5.3 %collective-permute-start.3 = (f32[32,128]{1,0:T(8,128)S(1)}, f32[32,128]{1,0:T(8,128)S(1)}, u32[]{:S(2)}, u32[]{:S(2)}) collective-permute-start(f32[32,128]{1,0:T(8,128)S(1)} %get-tuple-element.69), channel_id=1, source_target_pairs={{0,1},{1,0},{2,3},{3,2},{4,5},{5,4},{6,7},{7,6},{8,9},{9,8},{10,11... | collective-permute-start | bytes 49160 | tf_op jit(solution)/shard_map/ppermute | solution.py:385
  13.4 2.5 %collective-permute-start.4 = (f32[32,128]{1,0:T(8,128)S(1)}, f32[32,128]{1,0:T(8,128)S(1)}, u32[]{:S(2)}, u32[]{:S(2)}) collective-permute-start(f32[32,128]{1,0:T(8,128)S(1)} %get-tuple-element.70), channel_id=1, source_target_pairs={{0,8},{1,2},{2,1},{3,4},{4,3},{5,6},{6,5},{7,15},{8,0},{9,10},{10,... | collective-permute-start | bytes 49160 | tf_op jit(solution)/shard_map/ppermute | solution.py:385

commit v9 on v8

--- a/solution.py
+++ b/solution.py
@@ -13,10 +13,6 @@
 
 WIDE = 512
 SELECTED = (2, 3)
-
-
-def dot(a, b):
-    return jnp.dot(a, b, precision=lax.Precision.HIGHEST, preferred_element_type=jnp.float32)
 
 
 def split(x):
@@ -192,12 +188,14 @@
     time3_ref[...] = left3(time)
     inverse = inv[...]
     first_faces = jnp.concatenate([face_rows(fp_ref, f, face_dofs) for f in range(2)], axis=0)
-    both = jnp.concatenate([inverse, dot(first_faces, inverse)], axis=0)
-    ahead_rim3_ref[...] = left3(dot(both, rim))
-    ahead_time3_ref[...] = left3(dot(both, time))
-    both = left3(both)
-    for c in chunks(elements):
-        fill_jump(traces, terms, nb_ref, bd_ref, jump_ref, face_dofs, elements, c)
+    both = left3(jnp.concatenate([inverse, dot3(left3(first_faces), inverse)], axis=0))
+    ahead_rim3_ref[...] = left3(dot3(both, rim))
+    ahead_time3_ref[...] = left3(dot3(both, time))
+    parts = chunks(elements)
+    fill_jump(traces, terms, nb_ref, bd_ref, jump_ref, face_dofs, elements, parts[0])
+    for i, c in enumerate(parts):
+        if i + 1 < len(parts):
+            fill_jump(traces, terms, nb_ref, bd_ref, jump_ref, face_dofs, elements, parts[i + 1])
         values = jnp.concatenate([coef_ref[:, c] * v_ref[:, c], jump_ref[:, c]], axis=0)
         part = rhs[:, c] - dot3(apply3_ref[...], values)
         part_ref[:, c] = part

time: 30.8 us -> 30.8 us (level)
  transfers between devices with their start and end apart: 6 -> 6, of which waited for: 0 -> 0; matrix products, arithmetic and copies ran while one was open for 0% -> 0% of each run, Pallas kernels for 22% -> 21%
where the time goes in v9:
time: 30.8 us; the launch traced here: 30.7 us
  blocking collectives  12.6 us (41%)
  Pallas kernels  9.61 us (31%)
  starting transfers between devices  7.65 us (25%)
  between operations  0.77 us (2%)
    all_to_all x1, blocking collectives, on_device(): everyone = lax.all_to_all(sums, ('tm', 'space'), 0, 0, tiled=True)  12.6 us
    pallas_call x10, Pallas kernels, call(): pl.pallas_call(body, out_shape=shapes, in_specs=[VM] * len(args) + [HB] *...  9.61 us
    ppermute x4, starting transfers between devices, halo(): lax.ppermute(x, ('tm', 'space'), full_swaps(first, slabs, parts))  7.03 us
  transfers between devices with their start and end apart: 6, of which 0 were waited for; matrix products, arithmetic and copies ran while one was open for 0% of the time, Pallas kernels for 21%

profile of v9, /device:TPU:0, one launch (start us, length us, event | category | flops | bytes accessed | tf_op | source)
XLA Modules:
  0.0 30.7 jit_solution(1870816025987337683)
XLA Ops:
  0.6 1.1 %shard_map.130 = (f32[128,1024]{1,0:T(8,128)S(1)}, f32[64,1024]{1,0:T(8,128)S(1)}, f32[192,128]{1,0:T(8,128)S(1)}, s32[2,128]{1,0:T(2,128)S(1)}, f32[1,1024]{1,0...) custom-call(f32[128,1024]{1,0:T(8,128)} %bitcast.18, f32[192,128]{1,0:T(8,128)} %fp_hbm.1, ...), custom_call_target="tpu_custom_call" | custom-call | flops 2000000000 | bytes 1615872 | tf_op jit(solution)/shard_map/pallas_call | solution.py:346
  1.8 0.5 %collective-permute-start.2 = (f32[64,1024]{1,0:T(8,128)S(1)}, f32[64,1024]{1,0:T(8,128)S(1)}, u32[]{:S(2)}, u32[]{:S(2)}) collective-permute-start(f32[64,1024]{1,0:T(8,128)S(1)} %get-tuple-element.54), channel_id=1, source_target_pairs={{0,8},{8,16},{16,24},{24,0},{1,9},{9,17},{17,25},{25,1},{2,10},{10... | collective-permute-start | bytes 786440 | tf_op jit(solution)/shard_map/ppermute | solution.py:400
  2.3 0.0 copy-start
  2.3 0.0 copy-start.1
  2.3 0.0 copy-start.2
  2.3 0.0 copy-start.3
  2.3 0.0 copy-start.4
  2.3 0.4 %shard_map.131 = (f32[64,1024]{1,0:T(8,128)S(1)}, f32[32,128]{1,0:T(8,128)S(1)}, f32[32,128]{1,0:T(8,128)S(1)}) custom-call(f32[128,1024]{1,0:T(8,128)S(1)} %get-tuple-element.42.v_ref, f32[192,128]{1,0:T(8,128)S(1)} %get-tuple-element.43.fp_ref, s32[2,128]{1,0:T(2,128)S(1)} %get-tuple-element.44.send_ref), custom_call_target="tpu_custom_call" | custom-call | flops 2000000000 | bytes 918528 | tf_op jit(solution)/shard_map/pallas_call | solution.py:346
  2.8 2.6 %collective-permute-start = (f32[32,128]{1,0:T(8,128)S(1)}, f32[32,128]{1,0:T(8,128)S(1)}, u32[]{:S(2)}, u32[]{:S(2)}) collective-permute-start(f32[32,128]{1,0:T(8,128)S(1)} %get-tuple-element.50), channel_id=1, source_target_pairs={{0,1},{1,0},{2,3},{3,2},{4,5},{5,4},{6,7},{7,6},{8,9},{9,8},{10,11... | collective-permute-start | bytes 49160 | tf_op jit(solution)/shard_map/ppermute | solution.py:383
  5.4 1.3 %collective-permute-start.1 = (f32[32,128]{1,0:T(8,128)S(1)}, f32[32,128]{1,0:T(8,128)S(1)}, u32[]{:S(2)}, u32[]{:S(2)}) collective-permute-start(f32[32,128]{1,0:T(8,128)S(1)} %get-tuple-element.51), channel_id=1, source_target_pairs={{0,8},{1,2},{2,1},{3,4},{4,3},{5,6},{6,5},{7,15},{8,0},{9,10},{10,... | collective-permute-start | bytes 49160 | tf_op jit(solution)/shard_map/ppermute | solution.py:383
  6.7 0.0 copy-done
  6.7 0.0 copy-done.1
  6.7 0.0 copy-done.2
  6.7 0.0 copy-done.3
  6.7 0.0 copy-done.4
  6.7 2.4 %shard_map.132 = (f32[192,1024]{1,0:T(8,128)S(1)}, f32[128,1024]{1,0:T(8,128)S(1)}, f32[192,1024]{1,0:T(8,128)S(1)}, bf16[128,384]{1,0:T(8,128)(2,1)S(1)}, bf16[...) custom-call(f32[128,1024]{1,0:T(8,128)S(1)} %get-tuple-element.42.v_, ...), custom_call_target="tpu_custom_call" | custom-call | flops 301989888 | bytes 5001216 | tf_op jit(solution)/shard_map/pallas_call | solution.py:346
  9.1 0.0 collective-permute-done.first_in
  9.1 0.0 collective-permute-done.1.second_in
  9.1 0.6 %shard_map.133 = (f32[192,1024]{1,0:T(8,128)S(1)}, f32[64,1024]{1,0:T(8,128)S(1)}) custom-call(f32[192,1024]{1,0:T(8,128)S(1)} %get-tuple-element.49.ahead_ref, f32[32,128]{1,0:T(8,128)S(1)} %collective-permute-done.first_in, f32[32,128]{1,0:T(8,128)S(1)} %collective-permute-done.1.second_in, bf16[192,192]{1,0:T(8,128)(2,1)S(1)} %get-tuple-element.52.ahead_rim3_ref, ...), custom_call_target="tpu_custom_call" | custom-call | flops 100663296 | bytes 2064384 | tf_op jit(solution)/shard_map/pallas_call | solution.py:346
  9.7 0.0 collective-permute-done.2.prev_ref
  9.7 0.2 shard_map.134
  10.0 0.1 collective-permute-start.5
  10.0 0.4 %shard_map.135 = (f32[128,1024]{1,0:T(8,128)S(1)}, f32[64,1024]{1,0:T(8,128)S(1)}, f32[32,128]{1,0:T(8,128)S(1)}, f32[32,128]{1,0:T(8,128)S(1)}) custom-call(f32[192,1024]{1,0:T(8,128)S(1)} %get-tuple-element.53.near_ref, f32[64,1024]{1,0:T(8,128)S(1)} %get-tuple-element.56.time_ref.time0_ref, f32[64,1024]{1,0:T(8,128)S(1)} %get-tuple-element.57.end_ref, ...), custom_call_target="tpu_custom_call" | custom-call | flops 50331648 | bytes 2282496 | tf_op jit(solution)/shard_map/pallas_call | solution.py:346
  10.4 2.8 %collective-permute-start.3 = (f32[32,128]{1,0:T(8,128)S(1)}, f32[32,128]{1,0:T(8,128)S(1)}, u32[]{:S(2)}, u32[]{:S(2)}) collective-permute-start(f32[32,128]{1,0:T(8,128)S(1)} %get-tuple-element.69), channel_id=1, source_target_pairs={{0,1},{1,0},{2,3},{3,2},{4,5},{5,4},{6,7},{7,6},{8,9},{9,8},{10,11... | collective-permute-start | bytes 49160 | tf_op jit(solution)/shard_map/ppermute | solution.py:383
  13.2 0.3 %collective-permute-start.4 = (f32[32,128]{1,0:T(8,128)S(1)}, f32[32,128]{1,0:T(8,128)S(1)}, u32[]{:S(2)}, u32[]{:S(2)}) collective-permute-start(f32[32,128]{1,0:T(8,128)S(1)} %get-tuple-element.70), channel_id=1, source_target_pairs={{0,8},{1,2},{2,1},{3,4},{4,3},{5,6},{6,5},{7,15},{8,0},{9,10},{10,... | collective-permute-start | bytes 49160 | tf_op jit(solution)/shard_map/ppermute | solution.py:383
  13.6 2.1 %shard_map.136 = (f32[128,1024]{1,0:T(8,128)S(1)}, f32[64,1024]{1,0:T(8,128)S(1)}, f32[128,1024]{1,0:T(8,128)S(1)}, f32[64,1024]{1,0:T(8,128)S(1)}, f32[8,1024]{1,0:T(8,128)S(1)}) custom-call(f32[128,1024]{1,0:T(8,128)S(1)} %get-tuple-element.58.dir_ref, f32[64,1024]{1,0:T(8,128)S(1)} %get-tuple-element.59.tr_ref, f32[1,1024]{1,0:T(1,128)S(1)} %get-tuple-element.46.coef_ref, ...), custom_call_target="tpu_custom_call" | custom-call | flops 301989888 | bytes 5165056 | tf_op jit(solution)/shard_map/pallas_call | solution.py:346
  15.7 0.0 collective-permute-done.3.first_in
  15.7 0.0 collective-permute-done.4.second_in
  15.7 0.6 %shard_map.137 = (f32[128,1024]{1,0:T(8,128)S(1)}, f32[8,1024]{1,0:T(8,128)S(1)}) custom-call(f32[128,1024]{1,0:T(8,128)S(1)} %get-tuple-element.67.part_ref, f32[64,1024]{1,0:T(8,128)S(1)} %get-tuple-element.68.border_ref, f32[32,128]{1,0:T(8,128)S(1)} %collective-permute-done.3.first_in, f32[32,128]{1,0:T(8,128)S(1)} %collective-permute-done.4.second_in, ...), custom_call_target="tpu_custom_call" | custom-call | flops 50331648 | bytes 1818624 | tf_op jit(solution)/shard_map/pallas_call | solution.py:346
  16.3 0.0 collective-permute-done.5.prev_ref
  16.3 0.7 %shard_map.138 = (f32[8,1024]{1,0:T(8,128)S(1)}, f32[32,128]{1,0:T(8,128)S(1)}) custom-call(f32[128,1024]{1,0:T(8,128)S(1)} %get-tuple-element.73.near_ref, f32[128,1024]{1,0:T(8,128)S(1)} %get-tuple-element.58.dir_ref, f32[64,1024]{1,0:T(8,128)S(1)} %collective-permute-done.5.prev_ref, bf16[128,192]{1,0:T(8,128)(2,1)S(1)} %get-tuple-element.63.time3_ref, ...), custom_call_target="tpu_custom_call" | custom-call | flops 50331648 | bytes 2277376 | tf_op jit(solution)/shard_map/pallas_call | solution.py:346
  17.0 12.6 %all_to_all.11 = f32[32,1,128]{2,1,0:T(1,128)S(1)} all-to-all(f32[32,1,128]{2,1,0:T(1,128)S(1)} %bitcast.17), channel_id=1, replica_groups=mesh['tm'=4,'space'=8] {'tm','space'}, dimensions={0} | all-to-all | bytes 32768 | tf_op jit(solution)/shard_map/all_to_all | solution.py:450
  29.6 1.0 %shard_map.139 = (f32[128,1024]{1,0:T(8,128)}, f32[1,1024]{1,0:T(1,128)}, f32[1,128]{1,0:T(1,128)}) custom-call(f32[32,128]{1,0:T(8,128)S(1)} %bitcast.15, f32[8,1024]{1,0:T(8,128)S(1)} %get-tuple-element.77.coeff_ref, f32[128,1024]{1,0:T(8,128)S(1)} %get-tuple-element.42.v_ref, f32[128,1024]{1,0:T(8,128)S(1)} %get-tuple-element.58.dir_ref), custom_call_target="tpu_custom_call" | custom-call | flops 524288 | bytes 1626624 | tf_op jit(solution)/shard_map/pallas_call | solution.py:346
Async XLA Ops:
  1.8 8.0 %collective-permute-start.2 = (f32[64,1024]{1,0:T(8,128)S(1)}, f32[64,1024]{1,0:T(8,128)S(1)}, u32[]{:S(2)}, u32[]{:S(2)}) collective-permute-start(f32[64,1024]{1,0:T(8,128)S(1)} %get-tuple-element.54), channel_id=1, source_target_pairs={{0,8},{8,16},{16,24},{24,0},{1,9},{9,17},{17,25},{25,1},{2,10},{10... | collective-permute-start | bytes 786440 | tf_op jit(solution)/shard_map/ppermute | solution.py:400
  2.3 4.4 %copy-start = (f32[1,128,1024]{2,1,0:T(8,128)S(1)}, f32[1,128,1024]{2,1,0:T(8,128)}, u32[]{:S(2)}) copy-start(f32[1,128,1024]{2,1,0:T(8,128)} %param.12) | copy-start | bytes 1572868
  2.3 4.4 %copy-start.1 = (f32[128,192]{0,1:T(8,128)S(1)}, f32[128,192]{0,1:T(8,128)}, u32[]{:S(2)}) copy-start(f32[128,192]{0,1:T(8,128)} %param.17) | copy-start | bytes 294916
  2.3 4.4 %copy-start.2 = (f32[128,128]{1,0:T(8,128)S(1)}, f32[128,128]{1,0:T(8,128)}, u32[]{:S(2)}) copy-start(f32[128,128]{1,0:T(8,128)} %stiff.1) | copy-start | bytes 196612
  2.3 4.4 %copy-start.3 = (f32[128,128]{1,0:T(8,128)S(1)}, f32[128,128]{1,0:T(8,128)}, u32[]{:S(2)}) copy-start(f32[128,128]{1,0:T(8,128)} %inv.1) | copy-start | bytes 196612
  2.3 4.4 %copy-start.4 = (f32[128,64]{0,1:T(8,128)S(1)}, f32[128,64]{0,1:T(8,128)}, u32[]{:S(2)}) copy-start(f32[128,64]{0,1:T(8,128)} %param.18) | copy-start | bytes 98308
  2.8 6.3 %collective-permute-start = (f32[32,128]{1,0:T(8,128)S(1)}, f32[32,128]{1,0:T(8,128)S(1)}, u32[]{:S(2)}, u32[]{:S(2)}) collective-permute-start(f32[32,128]{1,0:T(8,128)S(1)} %get-tuple-element.50), channel_id=1, source_target_pairs={{0,1},{1,0},{2,3},{3,2},{4,5},{5,4},{6,7},{7,6},{8,9},{9,8},{10,11... | collective-permute-start | bytes 49160 | tf_op jit(solution)/shard_map/ppermute | solution.py:383
  5.4 3.7 %collective-permute-start.1 = (f32[32,128]{1,0:T(8,128)S(1)}, f32[32,128]{1,0:T(8,128)S(1)}, u32[]{:S(2)}, u32[]{:S(2)}) collective-permute-start(f32[32,128]{1,0:T(8,128)S(1)} %get-tuple-element.51), channel_id=1, source_target_pairs={{0,8},{1,2},{2,1},{3,4},{4,3},{5,6},{6,5},{7,15},{8,0},{9,10},{10,... | collective-permute-start | bytes 49160 | tf_op jit(solution)/shard_map/ppermute | solution.py:383
  10.0 6.4 %collective-permute-start.5 = (f32[64,1024]{1,0:T(8,128)S(1)}, f32[64,1024]{1,0:T(8,128)S(1)}, u32[]{:S(2)}, u32[]{:S(2)}) collective-permute-start(f32[64,1024]{1,0:T(8,128)S(1)} %get-tuple-element.57.end_ref), channel_id=1, source_target_pairs={{0,8},{8,16},{16,24},{24,0},{1,9},{9,17},{17,25},{25,1},{2,10},{10... | collective-permute-start | bytes 786440 | tf_op jit(solution)/shard_map/ppermute | solution.py:421
  10.4 5.3 %collective-permute-start.3 = (f32[32,128]{1,0:T(8,128)S(1)}, f32[32,128]{1,0:T(8,128)S(1)}, u32[]{:S(2)}, u32[]{:S(2)}) collective-permute-start(f32[32,128]{1,0:T(8,128)S(1)} %get-tuple-element.69), channel_id=1, source_target_pairs={{0,1},{1,0},{2,3},{3,2},{4,5},{5,4},{6,7},{7,6},{8,9},{9,8},{10,11... | collective-permute-start | bytes 49160 | tf_op jit(solution)/shard_map/ppermute | solution.py:383
  13.2 2.5 %collective-permute-start.4 = (f32[32,128]{1,0:T(8,128)S(1)}, f32[32,128]{1,0:T(8,128)S(1)}, u32[]{:S(2)}, u32[]{:S(2)}) collective-permute-start(f32[32,128]{1,0:T(8,128)S(1)} %get-tuple-element.70), channel_id=1, source_target_pairs={{0,8},{1,2},{2,1},{3,4},{4,3},{5,6},{6,5},{7,15},{8,0},{9,10},{10,... | collective-permute-start | bytes 49160 | tf_op jit(solution)/shard_map/ppermute | solution.py:383
